TPU v7x, 32 devices: a whole 2x2x4 slice. The times are simulated.
32 devices in a mesh: win: 2 (over y), wide: 8 (over z, core), narrow: 2 (over x).
Axes of the slice: x: 2, y: 2, z: 4, core: 2. Of those that a mesh axis runs over, the one named last changes fastest.
Arguments:
- traces: float32 [4, 8, 256, 1024], P(('win', 'narrow'), 'wide'), parts along dimension 0, may hold values from -40 to 40
- mask: int32 [4, 8, 256], P(('win', 'narrow'), 'wide'), parts along dimension 0, may hold values 0 or 1
- omega: float32 [32, 810], P('narrow'), may hold values from -6 to 6
Outputs:
- filtered: float32 [4, 8, 256, 1024], P(('win', 'narrow'), 'wide'), parts along dimension 0
There are 2 independent parts, one for each index of `win`. A program takes and returns all parts, laid end to end along the dimension named above; an argument that names none is the same for every part. Nothing has to cross between parts.
Inputs may be any that keep to these rules, and one draw needn't show every extreme that they name: `mask`: 1 keeps a trace, 0 marks it as not recorded.
All inputs are finite; a program needn't handle non-finite values. No bound on the sum of `mask` on one device may be relied on, other than what follows from the above.
Results may differ from a plain program's by a relative error of at most 0.00027.
Values sent between devices are 32-bit elements; how exact they have to be, the bound alone decides.
No kernel may reach another device: no remote copies, remote signals or barrier semaphores. Data moves between devices by JAX's collectives and lax.ppermute only.
A program may use at most 64 MiB of HBM per device.

v0:
```python
import functools
import math

import jax
import jax.numpy as jnp
import ml_dtypes
import numpy as np
from jax import lax
from jax.experimental import pallas as pl
from jax.experimental.pallas import tpu as pltpu
from jax.sharding import PartitionSpec as P

G3 = 16
G4 = 16
S = 1024
FREQ_DEV = 1
FIRST_BIN = 16
LANES = 128
CELLS = G3 * G4
KEEP3, KEEP4 = G3 // 2, G4 // 2
SPAN3, SPAN4 = G3 - KEEP3 + 1, G4 - KEEP4 + 1
SHIFT3, SHIFT4 = (SPAN3 - 1) // 2, (SPAN4 - 1) // 2
ROWS = KEEP3 * KEEP4
COLS = SPAN3 * SPAN4
PIECES = CELLS // LANES

VMEM = pl.BlockSpec(memory_space=pltpu.VMEM)
highest = lax.Precision.HIGHEST


def halves(table):
    table = np.asarray(table, np.float32)
    high = table.astype(ml_dtypes.bfloat16)
    low = (table - high.astype(np.float32)).astype(ml_dtypes.bfloat16)
    return high, low


def phases(freq_total):
    bins = FIRST_BIN + np.arange(freq_total)
    return 2.0 * np.pi * ((bins[:, None] * np.arange(S)[None, :]) % S) / S


def cell_angles(positions3, positions4):
    wave = np.arange(CELLS)
    turns = (
        np.outer(positions3, wave // G4) % G3 / G3 + np.outer(positions4, wave % G4) % G4 / G4
    )
    return 2.0 * np.pi * turns


def correlation(length, keep_size):
    position = np.arange(length)
    span_size = length - keep_size + 1
    return (
        np.minimum(position, keep_size - 1) - np.maximum(position - span_size + 1, 0) + 1
    ).astype(np.float64)


def spectrum_table(freq_total, copies):
    angles = np.repeat(phases(freq_total), copies, 0)
    return np.concatenate([np.cos(angles), -np.sin(angles)], 0) / math.sqrt(S)


def synthesis_table(freq_total):
    angles = phases(freq_total)
    return np.concatenate([np.cos(angles), -np.sin(angles)], 0) * math.sqrt(2.0 / freq_total)


def centred_angles():
    cell = np.arange(CELLS)
    return cell_angles(cell // G4 - SHIFT3, cell % G4 - SHIFT4)


def omega_table():
    column = np.arange(COLS)
    angles = cell_angles(column // SPAN4, column % SPAN4)
    table = np.zeros((LANES, 2 * CELLS))
    table[:COLS] = np.concatenate([np.cos(angles), -np.sin(angles)], 1)
    return table


def sketch_table():
    row = np.arange(ROWS)
    angles = cell_angles(row // KEEP4 - SHIFT3, row % KEEP4 - SHIFT4).T
    real, imag = np.cos(angles) / CELLS, np.sin(angles) / CELLS
    from_real = np.concatenate([real, imag, imag, -real], 1)
    from_imag = np.concatenate([-imag, real, real, imag], 1)
    return np.concatenate([from_real, from_imag], 0)


def basis_table():
    row = np.arange(ROWS)
    angles = cell_angles(row // KEEP4, row % KEEP4)
    real, imag = np.cos(angles), np.sin(angles)
    return np.concatenate(
        [np.concatenate([real, -imag], 1), np.concatenate([imag, real], 1)], 0
    )


def window_table():
    parts = []
    for length, shift in ((G3, SHIFT3), (G4, SHIFT4)):
        wave = np.arange(length)
        turns = (wave[:, None] - wave[None, :])[:, :, None] * np.arange(-shift, shift + 1) / length
        parts.append(np.cos(2.0 * np.pi * turns).sum(-1) / length)
    return np.kron(parts[0], parts[1])


def split(value):
    high = value.astype(jnp.bfloat16)
    low = (value - high.astype(jnp.float32)).astype(jnp.bfloat16)
    return high, low


def dot(left, right):
    return jnp.dot(left, right, preferred_element_type=jnp.float32)


def wide_dot(value, high, low):
    rows = value.shape[0]
    value_high, value_low = split(value)
    main = dot(jnp.concatenate([value_high, value_low], 0), high)
    return main[:rows] + (main[rows:] + dot(value_high, low))


def spectrum_kernel(traces_ref, mask_ref, table_ref, out_ref):
    rows = table_ref.shape[0] // 2
    dests = rows // 2
    high, low = split(traces_ref[...])
    contract = (((1,), (1,)), ((), ()))
    main = lax.dot_general(table_ref[...], high, contract, preferred_element_type=jnp.float32)
    rest = lax.dot_general(table_ref[:rows], low, contract, preferred_element_type=jnp.float32)
    result = (main[:rows] + (main[rows:] + rest)) * mask_ref[...].astype(jnp.float32)
    for part in range(2):
        for piece in range(PIECES):
            out_ref[:, part * PIECES + piece, :] = result[
                part * dests : (part + 1) * dests, piece * LANES : (piece + 1) * LANES
            ]


def omega_kernel(columns, *refs):
    omega_refs = refs[:-3]
    high_ref, low_ref, out_ref = refs[-3:]
    omega = jnp.concatenate([ref[...] for ref in omega_refs], 0)
    pad = jnp.zeros((omega.shape[0], LANES - COLS), jnp.float32)
    blocks = [
        jnp.concatenate([omega[:, k * COLS : (k + 1) * COLS], pad], 1) for k in range(columns)
    ]
    out_ref[...] = wide_dot(jnp.concatenate(blocks, 0), high_ref[...], low_ref[...])


def invert(gram_real, gram_imag):
    size = gram_real.shape[0]
    row_index = lax.broadcasted_iota(jnp.int32, (size, size), 0)
    column_index = lax.broadcasted_iota(jnp.int32, (size, size), 1)
    identity = (row_index == column_index).astype(jnp.float32)
    real = jnp.concatenate([gram_real, identity], 1)
    imag = jnp.concatenate([gram_imag, jnp.zeros_like(identity)], 1)
    wide_index = lax.broadcasted_iota(jnp.int32, (size, 2 * size), 0)
    for j in range(size):
        scale = 1.0 / real[j : j + 1, j : j + 1]
        pivot_real = real[j : j + 1, :] * scale
        pivot_imag = imag[j : j + 1, :] * scale
        factor_real = real[:, j : j + 1]
        factor_imag = imag[:, j : j + 1]
        here = wide_index == j
        next_real = real - (factor_real * pivot_real - factor_imag * pivot_imag)
        next_imag = imag - (factor_real * pivot_imag + factor_imag * pivot_real)
        real = jnp.where(here, pivot_real, next_real)
        imag = jnp.where(here, pivot_imag, next_imag)
    return real[:, size:], imag[:, size:]


def core_kernel(
    dims,
    x_ref,
    omega_ref,
    analysis_high,
    analysis_low,
    sketch_high,
    sketch_low,
    basis_high,
    basis_low,
    window_high,
    window_low,
    back_high,
    back_low,
    weight_ref,
    out_ref,
    xhat,
    shat,
    bhat,
    uhat,
    dhat,
    ghat,
):
    first, second, rank = dims
    keep1, keep2 = first // 2, second // 2
    span1, span2 = first - keep1 + 1, second - keep2 + 1
    own = lax.axis_index("narrow")
    half = CELLS
    tiles = rank // 8
    pieces = CELLS // LANES
    small = keep1 * keep2 * span1 * span2 <= 64

    def sweep(count, body, carry):
        if small:
            for i in range(count):
                carry = body(i, carry)
            return carry
        return lax.fori_loop(0, count, body, carry)

    def rows(start, count=8):
        if isinstance(start, int):
            return pl.ds(start, count)
        return pl.ds(pl.multiple_of(start, 8), count)

    def lanes(part, piece):
        start = part * half + piece * LANES
        return pl.ds(start, LANES)

    planes = first * second
    spectrum = jnp.concatenate(
        [
            jnp.concatenate([x_ref[:, part * pieces + piece, :] for piece in range(pieces)], 1)
            for part in range(2)
        ],
        0,
    )
    both = wide_dot(spectrum, analysis_high[...], analysis_low[...])
    hats = (
        both[:planes, :half] + both[planes:, half:],
        both[planes:, :half] - both[:planes, half:],
    )
    for part in range(2):
        for piece in range(pieces):
            values = hats[part][:, piece * LANES : (piece + 1) * LANES]
            xhat[:, part * pieces + piece] = jnp.broadcast_to(
                values[:, None, :], (planes, 8, LANES)
            )

    def load_x(g1, g2, piece):
        row = g2 * first + g1
        return xhat[row, piece], xhat[row, pieces + piece]

    for piece in range(pieces):
        cache = {}

        def cached_x(g1, g2):
            if not small:
                return load_x(g1, g2, piece)
            if (g1, g2) not in cache:
                cache[g1, g2] = load_x(g1, g2, piece)
            return cache[g1, g2]

        def sketch_tile(tile, carry):
            def first_keep(l1, carry):
                zero = jnp.zeros((8, LANES), jnp.float32)

                def columns(k1, sums):
                    def column(k2, sums):
                        start = (k1 * span2 + k2) * rank + tile * 8
                        w_real = omega_ref[rows(start), lanes(0, piece)]
                        w_imag = omega_ref[rows(start), lanes(1, piece)]
                        sums = list(sums)
                        for l2 in range(keep2):
                            x_real, x_imag = cached_x(l1 + k1, l2 + k2)
                            real, imag = sums[l2]
                            sums[l2] = (
                                real + (x_real * w_real + x_imag * w_imag),
                                imag + (x_imag * w_real - x_real * w_imag),
                            )
                        return tuple(sums)

                    return sweep(span2, column, sums)

                sums = sweep(span1, columns, ((zero, zero),) * keep2)
                for l2 in range(keep2):
                    start = (l1 * keep2 + l2) * rank + tile * 8
                    shat[rows(start), lanes(0, piece)] = sums[l2][0]
                    shat[rows(start), lanes(1, piece)] = sums[l2][1]
                return carry

            return sweep(keep1, first_keep, carry)

        sweep(tiles, sketch_tile, 0)

    blocks = keep1 * keep2
    sketch = wide_dot(shat[...], sketch_high[...], sketch_low[...])
    straight = jnp.concatenate(
        [sketch[b * rank : (b + 1) * rank, : 2 * ROWS] for b in range(blocks)], 1
    )
    turned = jnp.concatenate(
        [sketch[b * rank : (b + 1) * rank, 2 * ROWS :] for b in range(blocks)], 1
    )
    contract = (((1,), (1,)), ((), ()))
    gram_real = lax.dot_general(
        straight, straight, contract, precision=highest, preferred_element_type=jnp.float32
    )
    gram_imag = lax.dot_general(
        straight, turned, contract, precision=highest, preferred_element_type=jnp.float32
    )
    inverse_real, inverse_imag = invert(gram_real, gram_imag)

    bhat[...] = wide_dot(sketch[:, : 2 * ROWS], basis_high[...], basis_low[...])
    mixer = jnp.concatenate([inverse_real, inverse_imag], 1)

    def mix(b, carry):
        real = bhat[rows(b * rank, rank), :half]
        imag = bhat[rows(b * rank, rank), half:]
        uhat[rows(b * rank, rank), :half] = jnp.dot(
            mixer,
            jnp.concatenate([real, imag], 0),
            precision=highest,
            preferred_element_type=jnp.float32,
        )
        uhat[rows(b * rank, rank), half:] = jnp.dot(
            mixer,
            jnp.concatenate([imag, -real], 0),
            precision=highest,
            preferred_element_type=jnp.float32,
        )
        return carry

    sweep(blocks, mix, 0)

    ghat[...] = jnp.zeros_like(ghat)

    def own_pair(a, carry):
        k1 = own - a
        valid = jnp.logical_and(k1 >= 0, k1 < span1).astype(jnp.float32)
        k1 = jnp.clip(k1, 0, span1 - 1)
        for piece in range(pieces):
            cache = {}

            def cached_x(l1, g2):
                if not small:
                    return load_x(l1 + k1, g2, piece)
                if (l1, g2) not in cache:
                    cache[l1, g2] = load_x(l1 + k1, g2, piece)
                return cache[l1, g2]

            def column_tile(tile, carry):
                zero = jnp.zeros((8, LANES), jnp.float32)

                def first_keep(l1, sums):
                    sums = list(sums)
                    for l2 in range(keep2):
                        start = (l1 * keep2 + l2) * rank + tile * 8
                        s_real = bhat[rows(start), lanes(0, piece)]
                        s_imag = bhat[rows(start), lanes(1, piece)]
                        for k2 in range(span2):
                            x_real, x_imag = cached_x(l1, l2 + k2)
                            real, imag = sums[k2]
                            sums[k2] = (
                                real + (s_real * x_real + s_imag * x_imag),
                                imag + (s_real * x_imag - s_imag * x_real),
                            )
                    return tuple(sums)

                sums = sweep(keep1, first_keep, ((zero, zero),) * span2)
                for k2 in range(span2):
                    for part in range(2):
                        start = (part * span2 + k2) * rank + tile * 8
                        dhat[rows(start), pl.ds(piece * LANES, LANES)] = sums[k2][part]
                return carry

            sweep(tiles, column_tile, 0)
        dhat[...] = wide_dot(dhat[...], window_high[...], window_low[...])
        for piece in range(pieces):

            def rebuild_tile(tile, sums):
                sums = list(sums)
                us = []
                for l2 in range(keep2):
                    start = (a * keep2 + l2) * rank + tile * 8
                    us.append(
                        (
                            uhat[rows(start), lanes(0, piece)],
                            uhat[rows(start), lanes(1, piece)],
                        )
                    )
                for k2 in range(span2):
                    d_real = dhat[rows(k2 * rank + tile * 8), pl.ds(piece * LANES, LANES)]
                    d_imag = dhat[
                        rows((span2 + k2) * rank + tile * 8), pl.ds(piece * LANES, LANES)
                    ]
                    for l2 in range(keep2):
                        u_real, u_imag = us[l2]
                        real, imag = sums[l2 + k2]
                        sums[l2 + k2] = (
                            real + (u_real * d_real - u_imag * d_imag),
                            imag + (u_real * d_imag + u_imag * d_real),
                        )
                return tuple(sums)

            zero = jnp.zeros((8, LANES), jnp.float32)
            sums = sweep(tiles, rebuild_tile, ((zero, zero),) * second)
            for part in range(2):
                summed = jnp.concatenate(
                    [jnp.sum(sums[g2][part], 0, keepdims=True) for g2 in range(second)], 0
                )
                place = pl.ds(piece * LANES, LANES)
                where = pl.ds(part * second, second)
                ghat[where, place] = ghat[where, place] + summed * valid
        return carry

    sweep(keep1, own_pair, 0)

    both = wide_dot(ghat[...], back_high[...], back_low[...])
    real = both[:second, :half] - both[second:, half:]
    imag = both[:second, half:] + both[second:, :half]
    weight = weight_ref[pl.ds(pl.multiple_of(own * second, 8), second), :]
    real = real * weight
    imag = imag * weight
    for piece in range(pieces):
        out_ref[:, piece, :] = real[:, piece * LANES : (piece + 1) * LANES]
        out_ref[:, pieces + piece, :] = imag[:, piece * LANES : (piece + 1) * LANES]


def synthesis_kernel(cells_ref, table_ref, out_ref):
    parts = [
        jnp.concatenate([cells_ref[:, part * PIECES + piece, :] for piece in range(PIECES)], 1)
        for part in range(2)
    ]
    high, low = split(jnp.concatenate(parts, 0))
    stacked = jnp.concatenate([high, low, high], 0)
    out_ref[...] = lax.dot_general(
        stacked, table_ref[...], (((0,), (0,)), ((), ())), preferred_element_type=jnp.float32
    )


def per_device(traces, mask, omega):
    narrow_count = lax.axis_size("narrow")
    wide_count = lax.axis_size("wide")
    assert traces.shape[:2] == (1, 1)
    first, second = narrow_count, wide_count
    freq_total = FREQ_DEV * wide_count
    keep1, keep2 = first // 2, second // 2
    span1, span2 = first - keep1 + 1, second - keep2 + 1
    rank = omega.shape[0] * narrow_count
    dests = wide_count * narrow_count
    lines = 2 * PIECES

    omegas = [omega]
    for step in range(1, narrow_count):
        ring = [(i, (i + step) % narrow_count) for i in range(narrow_count)]
        omegas.append(lax.ppermute(omega, "narrow", ring))

    high, low = halves(spectrum_table(freq_total, narrow_count))
    blocks = pl.pallas_call(
        spectrum_kernel,
        out_shape=jax.ShapeDtypeStruct((dests, lines, LANES), jnp.float32),
        in_specs=[VMEM] * 3,
        out_specs=VMEM,
        name="spectrum",
    )(traces.reshape(CELLS, S), mask.reshape(1, CELLS), np.concatenate([high, low], 0))
    grid = lax.all_to_all(blocks, ("wide", "narrow"), split_axis=0, concat_axis=0, tiled=True)

    if omega.shape[0] % 8:
        omegas = [jnp.concatenate(omegas, 0)]
    columns = span1 * span2
    omega_hat = pl.pallas_call(
        functools.partial(omega_kernel, columns),
        out_shape=jax.ShapeDtypeStruct((columns * rank, 2 * CELLS), jnp.float32),
        in_specs=[VMEM] * (len(omegas) + 2),
        out_specs=VMEM,
        cost_estimate=pl.CostEstimate(
            flops=6 * columns * rank * LANES * 2 * CELLS,
            bytes_accessed=4 * columns * rank * 2 * CELLS,
            transcendentals=0,
        ),
        name="omega",
    )(*omegas, *halves(omega_table()))

    angles = centred_angles()
    counts = (
        correlation(first, keep1)[:, None, None]
        * correlation(second, keep2)[None, :, None]
        * np.outer(correlation(G3, KEEP3), correlation(G4, KEEP4)).reshape(1, 1, CELLS)
    ).reshape(first * second, CELLS)
    forward = np.concatenate([np.cos(angles), np.sin(angles)], 1)
    backward = np.concatenate([np.cos(angles.T), np.sin(angles.T)], 1) / CELLS
    tables = (
        *halves(forward),
        *halves(sketch_table()),
        *halves(basis_table()),
        *halves(window_table()),
        *halves(backward),
        (1.0 / counts).astype(np.float32),
    )
    area = keep1 * keep2 * rank
    scratch = [
        (first * second, lines, 8, LANES),
        (area, 2 * CELLS),
        (area, 2 * CELLS),
        (area, 2 * CELLS),
        (2 * span2 * rank, CELLS),
        (2 * second, CELLS),
    ]
    rebuilt = pl.pallas_call(
        functools.partial(core_kernel, (first, second, rank)),
        out_shape=jax.ShapeDtypeStruct((second, lines, LANES), jnp.float32),
        in_specs=[VMEM] * (2 + len(tables)),
        out_specs=VMEM,
        scratch_shapes=[pltpu.VMEM(shape, jnp.float32) for shape in scratch],
        name="core",
    )(grid, omega_hat, *tables)
    returned = lax.all_to_all(rebuilt, "wide", split_axis=0, concat_axis=0, tiled=True)

    high, low = halves(synthesis_table(freq_total))
    filtered = pl.pallas_call(
        synthesis_kernel,
        out_shape=jax.ShapeDtypeStruct((CELLS, S), jnp.float32),
        in_specs=[VMEM] * 2,
        out_specs=VMEM,
        name="synthesis",
    )(returned, np.concatenate([high, high, low], 0))
    return filtered.reshape(traces.shape)


def solution(mesh):
    return jax.shard_map(
        per_device,
        mesh=mesh,
        in_specs=(
            P(("win", "narrow"), "wide", None, None),
            P(("win", "narrow"), "wide", None),
            P("narrow", None),
        ),
        out_specs=P(("win", "narrow"), "wide", None, None),
        check_vma=False,
    )
```

profile of v0, /device:TPU:0, one launch (start us, length us, event | category | flops | bytes accessed | tf_op | source)
XLA Modules:
  0.0 36.5 jit_solution(9272733737507217428)
XLA Ops:
  0.0 3.0 %collective-permute-start = (f32[16,810]{1,0:T(8,128)}, f32[16,810]{1,0:T(8,128)S(1)}, u32[]{:S(2)}, u32[]{:S(2)}) collective-permute-start(f32[16,810]{1,0:T(8,128)} %refs_0_.1), channel_id=1, source_target_pairs={{0,1},{1,0},{2,3},{3,2},{4,5},{5,4},{6,7},{7,6},{8,9},{9,8},{10,11... | collective-permute-start | bytes 155528 | tf_op jit(solution)/shard_map/ppermute | solution.py:448
  3.0 2.3 %spectrum.1 = f32[16,4,128]{2,1,0:T(4,128)} custom-call(f32[256,1024]{1,0:T(8,128)} %bitcast.3, s32[1,256]{1,0:T(1,128)} %bitcast.4, bf16[64,1024]{1,0:T(8,128)(2,1)} %constant.30.clone.table_ref), custom_call_target="tpu_custom_call" | custom-call | tf_op jit(solution)/shard_map/spectrum/pallas_call | solution.py:451
  5.3 5.0 %all-to-all-start = ((f32[16,4,128]{2,1,0:T(4,128)}), f32[16,4,128]{2,1,0:T(4,128)S(1)}, u32[]{:S(2)}, u32[]{:S(2)}) async-start(f32[16,4,128]{2,1,0:T(4,128)} %spectrum.1), calls=%async_computation | async-start | bytes 65536 | tf_op jit(solution)/shard_map/all_to_all | solution.py:458
  10.2 0.0 collective-permute-done.refs_1_
  10.3 0.0 copy-start.1
  10.3 0.6 %copy-done.1 = f32[16,810]{1,0:T(8,128)} copy-done((f32[16,810]{1,0:T(8,128)}, f32[16,810]{1,0:T(8,128)S(1)}, u32[]{:S(2)}) %copy-start.1) | copy-done | bytes 51864
  10.9 2.3 %omega.1.omega_ref = f32[320,512]{1,0:T(8,128)} custom-call(f32[16,810]{1,0:T(8,128)} %refs_0_.1, f32[16,810]{1,0:T(8,128)} %copy-done.1, bf16[128,512]{1,0:T(8,128)(2,1)} %constant.31.clone.refs_2_, bf16[128,512]{1,0:T(8,128)(2,1)} %constant.32.clone.refs_3_), custom_call_target="tpu_custom_call" | custom-call | flops 125829120 | bytes 655360 | tf_op jit(solution)/shard_map/omega/pallas_call | solution.py:463
  13.2 3.6 %all-to-all-done.x_ref = f32[16,4,128]{2,1,0:T(4,128)S(1)} async-done(((f32[16,4,128]{2,1,0:T(4,128)}), f32[16,4,128]{2,1,0:T(4,128)S(1)}, u32[]{:S(2)}, u32[]{:S(2)}) %all-to-all-start) | async-done | bytes 32800 | tf_op jit(solution)/shard_map/all_to_all | solution.py:458
  16.8 0.0 copy-start
  16.8 0.6 %copy-done = f32[16,4,128]{2,1,0:T(4,128)} copy-done((f32[16,4,128]{2,1,0:T(4,128)}, f32[16,4,128]{2,1,0:T(4,128)S(1)}, u32[]{:S(2)}) %copy-start) | copy-done | bytes 32792
  17.4 7.3 %core.1 = f32[8,4,128]{2,1,0:T(4,128)} custom-call(f32[16,4,128]{2,1,0:T(4,128)} %copy-done, f32[320,512]{1,0:T(8,128)} %omega.1.omega_ref, bf16[256,512]{1,0:T(8,128)(2,1)} %constant.33.clone.analysis_high, bf16[256,512]{1,0:T(8,128)(2,1)} %constant.34.clone.analysis_low, bf16[512,256]{1,0:T(8,128)(2,1)} %constant.35.clone.sketch_high, ...), custom_call_target="tpu_custom_call" | custom-call | tf_op jit(solution)/shard_map/core/pallas_call | solution.py:501
  24.7 9.6 %all_to_all.10.cells_ref = f32[8,4,128]{2,1,0:T(4,128)} all-to-all(f32[8,4,128]{2,1,0:T(4,128)} %core.1), channel_id=1, replica_groups=mesh['win'=2,'wide'=8,'narrow'=2] {'wide'}, dimensions={0} | all-to-all | bytes 32768 | tf_op jit(solution)/shard_map/all_to_all | solution.py:509
  34.3 2.2 %synthesis.1 = f32[256,1024]{1,0:T(8,128)} custom-call(f32[8,4,128]{2,1,0:T(4,128)} %all_to_all.10.cells_ref, bf16[48,1024]{1,0:T(8,128)(2,1)} %constant.44.clone.table_ref), custom_call_target="tpu_custom_call" | custom-call | tf_op jit(solution)/shard_map/synthesis/pallas_call | solution.py:512
Async XLA Ops:
  0.0 10.3 %collective-permute-start = (f32[16,810]{1,0:T(8,128)}, f32[16,810]{1,0:T(8,128)S(1)}, u32[]{:S(2)}, u32[]{:S(2)}) collective-permute-start(f32[16,810]{1,0:T(8,128)} %refs_0_.1), channel_id=1, source_target_pairs={{0,1},{1,0},{2,3},{3,2},{4,5},{5,4},{6,7},{7,6},{8,9},{9,8},{10,11... | collective-permute-start | bytes 155528 | tf_op jit(solution)/shard_map/ppermute | solution.py:448
  5.3 11.5 %all-to-all-start = ((f32[16,4,128]{2,1,0:T(4,128)}), f32[16,4,128]{2,1,0:T(4,128)S(1)}, u32[]{:S(2)}, u32[]{:S(2)}) async-start(f32[16,4,128]{2,1,0:T(4,128)} %spectrum.1), calls=%async_computation | async-start | bytes 65536 | tf_op jit(solution)/shard_map/all_to_all | solution.py:458
  10.3 0.6 %copy-start.1 = (f32[16,810]{1,0:T(8,128)}, f32[16,810]{1,0:T(8,128)S(1)}, u32[]{:S(2)}) copy-start(f32[16,810]{1,0:T(8,128)S(1)} %collective-permute-done.refs_1_) | copy-start | bytes 155524
  16.8 0.6 %copy-start = (f32[16,4,128]{2,1,0:T(4,128)}, f32[16,4,128]{2,1,0:T(4,128)S(1)}, u32[]{:S(2)}) copy-start(f32[16,4,128]{2,1,0:T(4,128)S(1)} %all-to-all-done.x_ref) | copy-start | bytes 98308
where the time goes:
time: 36.8 us; the launch traced here: 36.5 us
  Pallas kernels  14.2 us (39%)
  blocking collectives  9.58 us (26%)
  starting transfers between devices  7.95 us (22%)
  waiting for transfers between devices  3.55 us (10%)
  local copies, waits for them, and re-layouts  1.22 us (3%)
    all_to_all x1, blocking collectives, per_device(): lax.all_to_all(rebuilt, 'wide', split_axis=0, concat_axis=0, tiled=True)  9.58 us
    pallas_call x1, Pallas kernels, per_device(): pl.pallas_call(functools.partial(core_kernel, (first, second, rank)), out...  7.34 us
    all_to_all x1, starting transfers between devices, per_device(): lax.all_to_all(blocks, ('wide', 'narrow'), split_axis=0, concat_axis=0, t...  4.98 us
    all_to_all x1, waiting for transfers between devices, per_device(): lax.all_to_all(blocks, ('wide', 'narrow'), split_axis=0, concat_axis=0, t...  3.55 us
    ppermute x1, starting transfers between devices, per_device(): omegas.append(lax.ppermute(omega, 'narrow', ring))  2.97 us
    pallas_call x1, Pallas kernels, per_device(): pl.pallas_call(functools.partial(omega_kernel, columns), out_shape=jax.Sh...  2.33 us
    pallas_call x1, Pallas kernels, per_device(): pl.pallas_call(spectrum_kernel, out_shape=jax.ShapeDtypeStruct((dests, li...  2.29 us
    pallas_call x1, Pallas kernels, per_device(): pl.pallas_call(synthesis_kernel, out_shape=jax.ShapeDtypeStruct((CELLS, S...  2.21 us
  transfers between devices with their start and end apart: 2, of which 1 were waited for; matrix products, arithmetic and copies ran while one was open for 0% of the time, Pallas kernels for 13%

commit v1 on v0

--- a/solution.py
+++ b/solution.py
@@ -16,6 +16,8 @@
 FREQ_DEV = 1
 FIRST_BIN = 16
 LANES = 128
+MIB = 1 << 20
+CHUNKS = 4
 CELLS = G3 * G4
 KEEP3, KEEP4 = G3 // 2, G4 // 2
 SPAN3, SPAN4 = G3 - KEEP3 + 1, G4 - KEEP4 + 1
@@ -24,6 +26,7 @@
 COLS = SPAN3 * SPAN4
 PIECES = CELLS // LANES
 
+HBM = pl.BlockSpec(memory_space=pltpu.HBM)
 VMEM = pl.BlockSpec(memory_space=pltpu.VMEM)
 highest = lax.Precision.HIGHEST
 
@@ -123,14 +126,37 @@
     return main[:rows] + (main[rows:] + dot(value_high, low))
 
 
-def spectrum_kernel(traces_ref, mask_ref, table_ref, out_ref):
-    rows = table_ref.shape[0] // 2
+def spectrum_kernel(traces_ref, mask_ref, table_ref, out_ref, traces, mask, table, sems):
+    rows = table.shape[0] // 2
     dests = rows // 2
-    high, low = split(traces_ref[...])
+    chunks, _, width = traces.shape
+    copies = [
+        pltpu.make_async_copy(table_ref, table, sems.at[0]),
+        pltpu.make_async_copy(mask_ref, mask, sems.at[1]),
+    ] + [
+        pltpu.make_async_copy(
+            traces_ref.at[:, pl.ds(i * width, width)], traces.at[i], sems.at[2 + i]
+        )
+        for i in range(chunks)
+    ]
+    for copy in copies:
+        copy.start()
+    copies[0].wait()
     contract = (((1,), (1,)), ((), ()))
-    main = lax.dot_general(table_ref[...], high, contract, preferred_element_type=jnp.float32)
-    rest = lax.dot_general(table_ref[:rows], low, contract, preferred_element_type=jnp.float32)
-    result = (main[:rows] + (main[rows:] + rest)) * mask_ref[...].astype(jnp.float32)
+    total = jnp.zeros((2 * rows, CELLS), jnp.float32)
+    rest = jnp.zeros((rows, CELLS), jnp.float32)
+    for i in range(chunks):
+        copies[2 + i].wait()
+        high, low = split(traces[i])
+        place = pl.ds(i * width, width)
+        total += lax.dot_general(
+            table[:, place], high, contract, preferred_element_type=jnp.float32
+        )
+        rest += lax.dot_general(
+            table[:rows, place], low, contract, preferred_element_type=jnp.float32
+        )
+    copies[1].wait()
+    result = (total[:rows] + (total[rows:] + rest)) * mask[...].astype(jnp.float32)
     for part in range(2):
         for piece in range(PIECES):
             out_ref[:, part * PIECES + piece, :] = result[
@@ -418,16 +444,29 @@
         out_ref[:, pieces + piece, :] = imag[:, piece * LANES : (piece + 1) * LANES]
 
 
-def synthesis_kernel(cells_ref, table_ref, out_ref):
+def synthesis_kernel(cells_ref, table_ref, out_ref, out, sems):
     parts = [
         jnp.concatenate([cells_ref[:, part * PIECES + piece, :] for piece in range(PIECES)], 1)
         for part in range(2)
     ]
     high, low = split(jnp.concatenate(parts, 0))
     stacked = jnp.concatenate([high, low, high], 0)
-    out_ref[...] = lax.dot_general(
-        stacked, table_ref[...], (((0,), (0,)), ((), ())), preferred_element_type=jnp.float32
-    )
+    contract = (((0,), (0,)), ((), ()))
+    chunks, width, _ = out.shape
+    copies = []
+    for i in range(chunks):
+        out[i] = lax.dot_general(
+            stacked[:, i * width : (i + 1) * width],
+            table_ref[...],
+            contract,
+            preferred_element_type=jnp.float32,
+        )
+        copies.append(
+            pltpu.make_async_copy(out.at[i], out_ref.at[pl.ds(i * width, width)], sems.at[i])
+        )
+        copies[-1].start()
+    for copy in copies:
+        copy.wait()
 
 
 def per_device(traces, mask, omega):
@@ -451,8 +490,14 @@
     blocks = pl.pallas_call(
         spectrum_kernel,
         out_shape=jax.ShapeDtypeStruct((dests, lines, LANES), jnp.float32),
-        in_specs=[VMEM] * 3,
+        in_specs=[HBM] * 3,
         out_specs=VMEM,
+        scratch_shapes=[
+            pltpu.VMEM((CHUNKS, CELLS, S // CHUNKS), jnp.float32),
+            pltpu.VMEM((1, CELLS), jnp.int32),
+            pltpu.VMEM((4 * dests, S), jnp.bfloat16),
+            pltpu.SemaphoreType.DMA((2 + CHUNKS,)),
+        ],
         name="spectrum",
     )(traces.reshape(CELLS, S), mask.reshape(1, CELLS), np.concatenate([high, low], 0))
     grid = lax.all_to_all(blocks, ("wide", "narrow"), split_axis=0, concat_axis=0, tiled=True)
@@ -470,6 +515,7 @@
             bytes_accessed=4 * columns * rank * 2 * CELLS,
             transcendentals=0,
         ),
+        compiler_params=pltpu.CompilerParams(vmem_limit_bytes=16 * MIB),
         name="omega",
     )(*omegas, *halves(omega_table()))
 
@@ -504,6 +550,7 @@
         in_specs=[VMEM] * (2 + len(tables)),
         out_specs=VMEM,
         scratch_shapes=[pltpu.VMEM(shape, jnp.float32) for shape in scratch],
+        compiler_params=pltpu.CompilerParams(vmem_limit_bytes=24 * MIB),
         name="core",
     )(grid, omega_hat, *tables)
     returned = lax.all_to_all(rebuilt, "wide", split_axis=0, concat_axis=0, tiled=True)
@@ -513,7 +560,12 @@
         synthesis_kernel,
         out_shape=jax.ShapeDtypeStruct((CELLS, S), jnp.float32),
         in_specs=[VMEM] * 2,
-        out_specs=VMEM,
+        out_specs=HBM,
+        scratch_shapes=[
+            pltpu.VMEM((PIECES, LANES, S), jnp.float32),
+            pltpu.SemaphoreType.DMA((PIECES,)),
+        ],
+        compiler_params=pltpu.CompilerParams(vmem_limit_bytes=8 * MIB),
         name="synthesis",
     )(returned, np.concatenate([high, high, low], 0))
     return filtered.reshape(traces.shape)

time: 36.8 us -> 32.2 us (0.88)
  Pallas kernels: 14.2 us -> 9.56 us
  blocking collectives: 9.58 us -> 8.02 us
  waiting for transfers between devices: 3.55 us -> 4.21 us
  local copies, waits for them, and re-layouts: 1.22 us -> 1.85 us
    pallas_call x1, Pallas kernels: 7.34 us -> 5.18 us  [per_device(): pl.pallas_call(functools.partial(core_kernel, (first, second, rank)), out...]
    pallas_call x1, Pallas kernels: 2.33 us -> 0.45 us  [per_device(): pl.pallas_call(functools.partial(omega_kernel, columns), out_shape=jax.Sh...]
    all_to_all x1, blocking collectives: 9.58 us -> 8.02 us  [per_device(): lax.all_to_all(rebuilt, 'wide', split_axis=0, concat_axis=0, tiled=True)]
    pallas_call x1, Pallas kernels: 2.21 us -> 1.25 us  [per_device(): pl.pallas_call(synthesis_kernel, out_shape=jax.ShapeDtypeStruct((CELLS, S...]
    all_to_all x1, waiting for transfers between devices: 3.55 us -> 4.21 us  [per_device(): lax.all_to_all(blocks, ('wide', 'narrow'), split_axis=0, concat_axis=0, t...]
    unnamed x4 -> x30, local copies, waits for them, and re-layouts: 1.22 us -> 1.85 us
    pallas_call x1, Pallas kernels: 2.29 us -> 2.68 us  [per_device(): pl.pallas_call(spectrum_kernel, out_shape=jax.ShapeDtypeStruct((dests, li...]
  transfers between devices with their start and end apart: 2 -> 2, of which waited for: 1 -> 1; matrix products, arithmetic and copies ran while one was open for 0% -> 0% of each run, Pallas kernels for 13% -> 10%
where the time goes in v1:
time: 32.2 us; the launch traced here: 31.9 us
  Pallas kernels  9.56 us (30%)
  starting transfers between devices  8.09 us (25%)
  blocking collectives  8.02 us (25%)
  waiting for transfers between devices  4.21 us (13%)
  local copies, waits for them, and re-layouts  1.85 us (6%)
    all_to_all x1, blocking collectives, per_device(): lax.all_to_all(rebuilt, 'wide', split_axis=0, concat_axis=0, tiled=True)  8.02 us
    pallas_call x1, Pallas kernels, per_device(): pl.pallas_call(functools.partial(core_kernel, (first, second, rank)), out...  5.18 us
    all_to_all x1, starting transfers between devices, per_device(): lax.all_to_all(blocks, ('wide', 'narrow'), split_axis=0, concat_axis=0, t...  5.13 us
    all_to_all x1, waiting for transfers between devices, per_device(): lax.all_to_all(blocks, ('wide', 'narrow'), split_axis=0, concat_axis=0, t...  4.21 us
    ppermute x1, starting transfers between devices, per_device(): omegas.append(lax.ppermute(omega, 'narrow', ring))  2.97 us
    pallas_call x1, Pallas kernels, per_device(): pl.pallas_call(spectrum_kernel, out_shape=jax.ShapeDtypeStruct((dests, li...  2.68 us
    unnamed x30, local copies, waits for them, and re-layouts  1.85 us
    pallas_call x1, Pallas kernels, per_device(): pl.pallas_call(synthesis_kernel, out_shape=jax.ShapeDtypeStruct((CELLS, S...  1.25 us
  transfers between devices with their start and end apart: 2, of which 1 were waited for; matrix products, arithmetic and copies ran while one was open for 0% of the time, Pallas kernels for 10%

profile of v1, /device:TPU:0, one launch (start us, length us, event | category | flops | bytes accessed | tf_op | source)
XLA Modules:
  0.0 31.9 jit_solution(11406412274375359966)
XLA Ops:
  0.0 3.0 %collective-permute-start = (f32[16,810]{1,0:T(8,128)}, f32[16,810]{1,0:T(8,128)S(1)}, u32[]{:S(2)}, u32[]{:S(2)}) collective-permute-start(f32[16,810]{1,0:T(8,128)} %refs_0_.1), channel_id=1, source_target_pairs={{0,1},{1,0},{2,3},{3,2},{4,5},{5,4},{6,7},{7,6},{8,9},{9,8},{10,11... | collective-permute-start | bytes 155528 | tf_op jit(solution)/shard_map/ppermute | solution.py:487
  3.0 0.0 copy-start.7
  3.0 0.0 copy-start.8
  3.0 0.0 copy-start.9
  3.0 2.7 %spectrum.1 = f32[16,4,128]{2,1,0:T(4,128)} custom-call(f32[256,1024]{1,0:T(8,128)} %bitcast.3, s32[1,256]{1,0:T(1,128)} %bitcast.4, bf16[64,1024]{1,0:T(8,128)(2,1)} %constant.30.clone.table_ref), custom_call_target="tpu_custom_call" | custom-call | tf_op jit(solution)/shard_map/spectrum/pallas_call | solution.py:490
  5.7 0.0 copy-start.3
  5.7 5.1 %all-to-all-start = ((f32[16,4,128]{2,1,0:T(4,128)}), f32[16,4,128]{2,1,0:T(4,128)S(1)}, u32[]{:S(2)}, u32[]{:S(2)}) async-start(f32[16,4,128]{2,1,0:T(4,128)} %spectrum.1), calls=%async_computation | async-start | bytes 65536 | tf_op jit(solution)/shard_map/all_to_all | solution.py:503
  10.9 0.0 copy-start
  10.9 0.0 copy-start.1
  10.9 0.0 copy-start.2
  10.9 0.0 collective-permute-done.refs_1_
  10.9 0.0 copy-done.10
  10.9 0.0 copy-start.11
  10.9 1.0 %copy-done.11 = bf16[128,512]{1,0:T(8,128)(2,1)S(1)} copy-done((bf16[128,512]{1,0:T(8,128)(2,1)S(1)}, bf16[128,512]{1,0:T(8,128)(2,1)}, u32[]{:S(2)}) %copy-start.11) | copy-done | bytes 131096
  11.9 0.8 %copy-done.13 = f32[16,810]{1,0:T(8,128)S(1)} copy-done((f32[16,810]{1,0:T(8,128)S(1)}, f32[16,810]{1,0:T(8,128)}, u32[]{:S(2)}) %copy-start.13) | copy-done | bytes 51864
  12.7 0.5 %omega.1.omega_ref = f32[320,512]{1,0:T(8,128)S(1)} custom-call(f32[16,810]{1,0:T(8,128)S(1)} %copy-done.13, f32[16,810]{1,0:T(8,128)S(1)} %collective-permute-done.refs_1_, bf16[128,512]{1,0:T(8,128)(2,1)S(1)} %copy-done.11, bf16[128,512]{1,0:T(8,128)(2,1)S(1)} %copy-done.10), custom_call_target="tpu_custom_call" | custom-call | flops 125829120 | bytes 655360 | tf_op jit(solution)/shard_map/omega/pallas_call | solution.py:508
  13.2 4.2 %all-to-all-done.x_ref = f32[16,4,128]{2,1,0:T(4,128)S(1)} async-done(((f32[16,4,128]{2,1,0:T(4,128)}), f32[16,4,128]{2,1,0:T(4,128)S(1)}, u32[]{:S(2)}, u32[]{:S(2)}) %all-to-all-start) | async-done | bytes 32800 | tf_op jit(solution)/shard_map/all_to_all | solution.py:503
  17.4 0.0 copy-done.4
  17.4 0.0 copy-done.5
  17.4 0.0 copy-done.6
  17.4 0.0 copy-done.7
  17.4 0.0 copy-done.8
  17.4 0.0 copy-done.9
  17.4 0.0 copy-done.3
  17.4 0.0 copy-done
  17.4 0.0 copy-done.1
  17.4 0.0 copy-done.2
  17.5 0.0 copy-done.14
  17.5 0.0 copy-start.12
  17.5 5.2 %core.1 = f32[8,4,128]{2,1,0:T(4,128)S(1)} custom-call(f32[16,4,128]{2,1,0:T(4,128)S(1)} %all-to-all-done.x_ref, f32[320,512]{1,0:T(8,128)S(1)} %omega.1.omega_ref, bf16[256,512]{1,0:T(8,128)(2,1)S(1)} %copy-done.5, bf16[256,512]{1,0:T(8,128)(2,1)S(1)} %copy-done.4, bf16[512,256]{1,0:T(8,128)(2,1)S(1)} %copy-done.3, bf16[512,256]{1,0:T(8,128)(2,1)S(1)} %copy-done.2, ...), custom_call_target="tpu_custom_call" | custom-call | tf_op jit(solution)/shard_map/core/pallas_call | solution.py:547
  22.7 8.0 %all_to_all.10.cells_ref = f32[8,4,128]{2,1,0:T(4,128)S(1)} all-to-all(f32[8,4,128]{2,1,0:T(4,128)S(1)} %core.1), channel_id=1, replica_groups=mesh['win'=2,'wide'=8,'narrow'=2] {'wide'}, dimensions={0} | all-to-all | bytes 32768 | tf_op jit(solution)/shard_map/all_to_all | solution.py:556
  30.7 1.2 %synthesis.1 = f32[256,1024]{1,0:T(8,128)} custom-call(f32[8,4,128]{2,1,0:T(4,128)S(1)} %all_to_all.10.cells_ref, bf16[48,1024]{1,0:T(8,128)(2,1)S(1)} %copy-done.12), custom_call_target="tpu_custom_call" | custom-call | tf_op jit(solution)/shard_map/synthesis/pallas_call | solution.py:559
  (7 shorter events, 0.0 us)
Async XLA Ops:
  0.0 10.9 %collective-permute-start = (f32[16,810]{1,0:T(8,128)}, f32[16,810]{1,0:T(8,128)S(1)}, u32[]{:S(2)}, u32[]{:S(2)}) collective-permute-start(f32[16,810]{1,0:T(8,128)} %refs_0_.1), channel_id=1, source_target_pairs={{0,1},{1,0},{2,3},{3,2},{4,5},{5,4},{6,7},{7,6},{8,9},{9,8},{10,11... | collective-permute-start | bytes 155528 | tf_op jit(solution)/shard_map/ppermute | solution.py:487
  3.0 7.9 %copy-start.10 = (bf16[128,512]{1,0:T(8,128)(2,1)S(1)}, bf16[128,512]{1,0:T(8,128)(2,1)}, u32[]{:S(2)}) copy-start(bf16[128,512]{1,0:T(8,128)(2,1)} %constant.32.clone.refs_3_) | copy-start | bytes 393220
  3.0 14.4 %copy-start.4 = (bf16[256,512]{1,0:T(8,128)(2,1)S(1)}, bf16[256,512]{1,0:T(8,128)(2,1)}, u32[]{:S(2)}) copy-start(bf16[256,512]{1,0:T(8,128)(2,1)} %constant.34.clone.analysis_low) | copy-start | bytes 786436
  3.0 14.4 %copy-start.5 = (bf16[256,512]{1,0:T(8,128)(2,1)S(1)}, bf16[256,512]{1,0:T(8,128)(2,1)}, u32[]{:S(2)}) copy-start(bf16[256,512]{1,0:T(8,128)(2,1)} %constant.33.clone.analysis_high) | copy-start | bytes 786436
  3.0 14.4 %copy-start.6 = (bf16[256,256]{1,0:T(8,128)(2,1)S(1)}, bf16[256,256]{1,0:T(8,128)(2,1)}, u32[]{:S(2)}) copy-start(bf16[256,256]{1,0:T(8,128)(2,1)} %constant.40.clone.window_low) | copy-start | bytes 393220
  3.0 14.4 %copy-start.7 = (bf16[256,256]{1,0:T(8,128)(2,1)S(1)}, bf16[256,256]{1,0:T(8,128)(2,1)}, u32[]{:S(2)}) copy-start(bf16[256,256]{1,0:T(8,128)(2,1)} %constant.39.clone.window_high) | copy-start | bytes 393220
  3.0 14.4 %copy-start.8 = (bf16[128,512]{1,0:T(8,128)(2,1)S(1)}, bf16[128,512]{1,0:T(8,128)(2,1)}, u32[]{:S(2)}) copy-start(bf16[128,512]{1,0:T(8,128)(2,1)} %constant.38.clone.basis_low) | copy-start | bytes 393220
  3.0 14.4 %copy-start.9 = (bf16[128,512]{1,0:T(8,128)(2,1)S(1)}, bf16[128,512]{1,0:T(8,128)(2,1)}, u32[]{:S(2)}) copy-start(bf16[128,512]{1,0:T(8,128)(2,1)} %constant.37.clone.basis_high) | copy-start | bytes 393220
  5.7 11.7 %copy-start.3 = (bf16[512,256]{1,0:T(8,128)(2,1)S(1)}, bf16[512,256]{1,0:T(8,128)(2,1)}, u32[]{:S(2)}) copy-start(bf16[512,256]{1,0:T(8,128)(2,1)} %constant.35.clone.sketch_high) | copy-start | bytes 786436
  5.7 11.7 %all-to-all-start = ((f32[16,4,128]{2,1,0:T(4,128)}), f32[16,4,128]{2,1,0:T(4,128)S(1)}, u32[]{:S(2)}, u32[]{:S(2)}) async-start(f32[16,4,128]{2,1,0:T(4,128)} %spectrum.1), calls=%async_computation | async-start | bytes 65536 | tf_op jit(solution)/shard_map/all_to_all | solution.py:503
  10.9 6.6 %copy-start = (bf16[256,512]{1,0:T(8,128)(2,1)S(1)}, bf16[256,512]{1,0:T(8,128)(2,1)}, u32[]{:S(2)}) copy-start(bf16[256,512]{1,0:T(8,128)(2,1)} %constant.42.clone.back_low) | copy-start | bytes 786436
  10.9 6.6 %copy-start.1 = (bf16[256,512]{1,0:T(8,128)(2,1)S(1)}, bf16[256,512]{1,0:T(8,128)(2,1)}, u32[]{:S(2)}) copy-start(bf16[256,512]{1,0:T(8,128)(2,1)} %constant.41.clone.back_high) | copy-start | bytes 786436
  10.9 6.6 %copy-start.2 = (bf16[512,256]{1,0:T(8,128)(2,1)S(1)}, bf16[512,256]{1,0:T(8,128)(2,1)}, u32[]{:S(2)}) copy-start(bf16[512,256]{1,0:T(8,128)(2,1)} %constant.36.clone.sketch_low) | copy-start | bytes 786436
  10.9 1.0 %copy-start.11 = (bf16[128,512]{1,0:T(8,128)(2,1)S(1)}, bf16[128,512]{1,0:T(8,128)(2,1)}, u32[]{:S(2)}) copy-start(bf16[128,512]{1,0:T(8,128)(2,1)} %constant.31.clone.refs_2_) | copy-start | bytes 393220
  11.9 0.8 %copy-start.13 = (f32[16,810]{1,0:T(8,128)S(1)}, f32[16,810]{1,0:T(8,128)}, u32[]{:S(2)}) copy-start(f32[16,810]{1,0:T(8,128)} %refs_0_.1) | copy-start | bytes 155524
  12.7 4.8 %copy-start.14 = (f32[16,256]{1,0:T(8,128)S(1)}, f32[16,256]{1,0:T(8,128)}, u32[]{:S(2)}) copy-start(f32[16,256]{1,0:T(8,128)} %constant.43.clone.weight_ref) | copy-start | bytes 49156
  17.5 13.2 %copy-start.12 = (bf16[48,1024]{1,0:T(8,128)(2,1)S(1)}, bf16[48,1024]{1,0:T(8,128)(2,1)}, u32[]{:S(2)}) copy-start(bf16[48,1024]{1,0:T(8,128)(2,1)} %constant.44.clone.table_ref) | copy-start | bytes 294916

commit v2 on v1

--- a/solution.py
+++ b/solution.py
@@ -18,6 +18,7 @@
 LANES = 128
 MIB = 1 << 20
 CHUNKS = 4
+PIVOTS = 4
 CELLS = G3 * G4
 KEEP3, KEEP4 = G3 // 2, G4 // 2
 SPAN3, SPAN4 = G3 - KEEP3 + 1, G4 - KEEP4 + 1
@@ -175,26 +176,69 @@
     out_ref[...] = wide_dot(jnp.concatenate(blocks, 0), high_ref[...], low_ref[...])
 
 
-def invert(gram_real, gram_imag):
+def minus_product(value, left, right):
+    return (
+        value[0] - (left[0] * right[0] - left[1] * right[1]),
+        value[1] - (left[0] * right[1] + left[1] * right[0]),
+    )
+
+
+def invert(gram_real, gram_imag, result):
     size = gram_real.shape[0]
+    width = 2 * size
     row_index = lax.broadcasted_iota(jnp.int32, (size, size), 0)
     column_index = lax.broadcasted_iota(jnp.int32, (size, size), 1)
     identity = (row_index == column_index).astype(jnp.float32)
     real = jnp.concatenate([gram_real, identity], 1)
     imag = jnp.concatenate([gram_imag, jnp.zeros_like(identity)], 1)
-    wide_index = lax.broadcasted_iota(jnp.int32, (size, 2 * size), 0)
-    for j in range(size):
-        scale = 1.0 / real[j : j + 1, j : j + 1]
-        pivot_real = real[j : j + 1, :] * scale
-        pivot_imag = imag[j : j + 1, :] * scale
-        factor_real = real[:, j : j + 1]
-        factor_imag = imag[:, j : j + 1]
-        here = wide_index == j
-        next_real = real - (factor_real * pivot_real - factor_imag * pivot_imag)
-        next_imag = imag - (factor_real * pivot_imag + factor_imag * pivot_real)
-        real = jnp.where(here, pivot_real, next_real)
-        imag = jnp.where(here, pivot_imag, next_imag)
-    return real[:, size:], imag[:, size:]
+    tiles = [(real[t : t + 8], imag[t : t + 8]) for t in range(0, size, 8)]
+    sublane = lax.broadcasted_iota(jnp.int32, (8, width), 0)
+    for start in range(0, size, PIVOTS):
+        home, at = start // 8, start % 8
+        columns = [
+            [
+                tuple(jnp.broadcast_to(v[:, start + b : start + b + 1], (8, width)) for v in tile)
+                for b in range(PIVOTS)
+            ]
+            for tile in tiles
+        ]
+        rows = [tuple(v[at + a : at + a + 1] for v in tiles[home]) for a in range(PIVOTS)]
+        block = {
+            (a, b): tuple(
+                jnp.broadcast_to(v[:, start + b : start + b + 1], (1, width)) for v in rows[a]
+            )
+            for a in range(PIVOTS)
+            for b in range(PIVOTS)
+        }
+        for p in range(PIVOTS):
+            scale = 1.0 / block[p, p][0]
+            rows[p] = tuple(v * scale for v in rows[p])
+            for b in range(p + 1, PIVOTS):
+                block[p, b] = tuple(v * scale for v in block[p, b])
+            for a in range(PIVOTS):
+                if a == p:
+                    continue
+                rows[a] = minus_product(rows[a], block[a, p], rows[p])
+                for b in range(p + 1, PIVOTS):
+                    block[a, b] = minus_product(block[a, b], block[a, p], block[p, b])
+        for t in range(len(tiles)):
+            tile = tiles[t]
+            for b in range(PIVOTS):
+                tile = minus_product(tile, columns[t][b], rows[b])
+            if t == home:
+                for b in range(PIVOTS):
+                    here = sublane == at + b
+                    tile = tuple(jnp.where(here, rows[b][k], tile[k]) for k in range(2))
+            tiles[t] = tile
+        yield
+    for part in range(2):
+        result.append(jnp.concatenate([tile[part] for tile in tiles], 0)[:, size:])
+
+
+def interleave(*steps):
+    steps = list(steps)
+    while steps:
+        steps = [step for step in steps if next(step, steps) is not steps]
 
 
 def core_kernel(
@@ -326,36 +370,13 @@
     gram_imag = lax.dot_general(
         straight, turned, contract, precision=highest, preferred_element_type=jnp.float32
     )
-    inverse_real, inverse_imag = invert(gram_real, gram_imag)
-
-    bhat[...] = wide_dot(sketch[:, : 2 * ROWS], basis_high[...], basis_low[...])
-    mixer = jnp.concatenate([inverse_real, inverse_imag], 1)
-
-    def mix(b, carry):
-        real = bhat[rows(b * rank, rank), :half]
-        imag = bhat[rows(b * rank, rank), half:]
-        uhat[rows(b * rank, rank), :half] = jnp.dot(
-            mixer,
-            jnp.concatenate([real, imag], 0),
-            precision=highest,
-            preferred_element_type=jnp.float32,
-        )
-        uhat[rows(b * rank, rank), half:] = jnp.dot(
-            mixer,
-            jnp.concatenate([imag, -real], 0),
-            precision=highest,
-            preferred_element_type=jnp.float32,
-        )
-        return carry
-
-    sweep(blocks, mix, 0)
-
-    ghat[...] = jnp.zeros_like(ghat)
-
-    def own_pair(a, carry):
+    def partner(a):
         k1 = own - a
         valid = jnp.logical_and(k1 >= 0, k1 < span1).astype(jnp.float32)
-        k1 = jnp.clip(k1, 0, span1 - 1)
+        return jnp.clip(k1, 0, span1 - 1), valid
+
+    def own_columns(a):
+        k1, _ = partner(a)
         for piece in range(pieces):
             cache = {}
 
@@ -391,8 +412,17 @@
                         dhat[rows(start), pl.ds(piece * LANES, LANES)] = sums[k2][part]
                 return carry
 
-            sweep(tiles, column_tile, 0)
+            if small:
+                for tile in range(tiles):
+                    column_tile(tile, 0)
+                    yield
+            else:
+                sweep(tiles, column_tile, 0)
         dhat[...] = wide_dot(dhat[...], window_high[...], window_low[...])
+        yield
+
+    def own_planes(a):
+        _, valid = partner(a)
         for piece in range(pieces):
 
             def rebuild_tile(tile, sums):
@@ -429,6 +459,42 @@
                 place = pl.ds(piece * LANES, LANES)
                 where = pl.ds(part * second, second)
                 ghat[where, place] = ghat[where, place] + summed * valid
+
+    def own_basis():
+        bhat[...] = wide_dot(sketch[:, : 2 * ROWS], basis_high[...], basis_low[...])
+        yield
+        if small:
+            yield from own_columns(0)
+
+    inverse = []
+    interleave(invert(gram_real, gram_imag, inverse), own_basis())
+    mixer = jnp.concatenate(inverse, 1)
+
+    def mix(b, carry):
+        real = bhat[rows(b * rank, rank), :half]
+        imag = bhat[rows(b * rank, rank), half:]
+        uhat[rows(b * rank, rank), :half] = jnp.dot(
+            mixer,
+            jnp.concatenate([real, imag], 0),
+            precision=highest,
+            preferred_element_type=jnp.float32,
+        )
+        uhat[rows(b * rank, rank), half:] = jnp.dot(
+            mixer,
+            jnp.concatenate([imag, -real], 0),
+            precision=highest,
+            preferred_element_type=jnp.float32,
+        )
+        return carry
+
+    sweep(blocks, mix, 0)
+    ghat[...] = jnp.zeros_like(ghat)
+
+    def own_pair(a, carry):
+        if not (small and isinstance(a, int) and a == 0):
+            for _ in own_columns(a):
+                pass
+        own_planes(a)
         return carry
 
     sweep(keep1, own_pair, 0)

time: 32.2 us -> 30.8 us (0.957)
  Pallas kernels: 9.56 us -> 8.12 us
    pallas_call x1, Pallas kernels: 5.18 us -> 3.74 us  [per_device(): pl.pallas_call(functools.partial(core_kernel, (first, second, rank)), out...]
where the time goes in v2:
time: 30.8 us; the launch traced here: 30.5 us
  Pallas kernels  8.12 us (26%)
  starting transfers between devices  8.09 us (26%)
  blocking collectives  8.02 us (26%)
  waiting for transfers between devices  4.21 us (14%)
  local copies, waits for them, and re-layouts  1.85 us (6%)
    all_to_all x1, blocking collectives, per_device(): lax.all_to_all(rebuilt, 'wide', split_axis=0, concat_axis=0, tiled=True)  8.02 us
    all_to_all x1, starting transfers between devices, per_device(): lax.all_to_all(blocks, ('wide', 'narrow'), split_axis=0, concat_axis=0, t...  5.13 us
    all_to_all x1, waiting for transfers between devices, per_device(): lax.all_to_all(blocks, ('wide', 'narrow'), split_axis=0, concat_axis=0, t...  4.21 us
    pallas_call x1, Pallas kernels, per_device(): pl.pallas_call(functools.partial(core_kernel, (first, second, rank)), out...  3.74 us
    ppermute x1, starting transfers between devices, per_device(): omegas.append(lax.ppermute(omega, 'narrow', ring))  2.97 us
    pallas_call x1, Pallas kernels, per_device(): pl.pallas_call(spectrum_kernel, out_shape=jax.ShapeDtypeStruct((dests, li...  2.68 us
    unnamed x30, local copies, waits for them, and re-layouts  1.85 us
    pallas_call x1, Pallas kernels, per_device(): pl.pallas_call(synthesis_kernel, out_shape=jax.ShapeDtypeStruct((CELLS, S...  1.25 us
  transfers between devices with their start and end apart: 2, of which 1 were waited for; matrix products, arithmetic and copies ran while one was open for 0% of the time, Pallas kernels for 10%

profile of v2, /device:TPU:0, one launch (start us, length us, event | category | flops | bytes accessed | tf_op | source)
XLA Modules:
  0.0 30.5 jit_solution(3082371320637331647)
XLA Ops:
  0.0 3.0 %collective-permute-start = (f32[16,810]{1,0:T(8,128)}, f32[16,810]{1,0:T(8,128)S(1)}, u32[]{:S(2)}, u32[]{:S(2)}) collective-permute-start(f32[16,810]{1,0:T(8,128)} %refs_0_.1), channel_id=1, source_target_pairs={{0,1},{1,0},{2,3},{3,2},{4,5},{5,4},{6,7},{7,6},{8,9},{9,8},{10,11... | collective-permute-start | bytes 155528 | tf_op jit(solution)/shard_map/ppermute | solution.py:553
  3.0 0.0 copy-start.7
  3.0 0.0 copy-start.8
  3.0 0.0 copy-start.9
  3.0 2.7 %spectrum.1 = f32[16,4,128]{2,1,0:T(4,128)} custom-call(f32[256,1024]{1,0:T(8,128)} %bitcast.3, s32[1,256]{1,0:T(1,128)} %bitcast.4, bf16[64,1024]{1,0:T(8,128)(2,1)} %constant.30.clone.table_ref), custom_call_target="tpu_custom_call" | custom-call | tf_op jit(solution)/shard_map/spectrum/pallas_call | solution.py:556
  5.7 0.0 copy-start.3
  5.7 5.1 %all-to-all-start = ((f32[16,4,128]{2,1,0:T(4,128)}), f32[16,4,128]{2,1,0:T(4,128)S(1)}, u32[]{:S(2)}, u32[]{:S(2)}) async-start(f32[16,4,128]{2,1,0:T(4,128)} %spectrum.1), calls=%async_computation | async-start | bytes 65536 | tf_op jit(solution)/shard_map/all_to_all | solution.py:569
  10.9 0.0 copy-start
  10.9 0.0 copy-start.1
  10.9 0.0 copy-start.2
  10.9 0.0 collective-permute-done.refs_1_
  10.9 0.0 copy-done.10
  10.9 0.0 copy-start.11
  10.9 1.0 %copy-done.11 = bf16[128,512]{1,0:T(8,128)(2,1)S(1)} copy-done((bf16[128,512]{1,0:T(8,128)(2,1)S(1)}, bf16[128,512]{1,0:T(8,128)(2,1)}, u32[]{:S(2)}) %copy-start.11) | copy-done | bytes 131096
  11.9 0.8 %copy-done.13 = f32[16,810]{1,0:T(8,128)S(1)} copy-done((f32[16,810]{1,0:T(8,128)S(1)}, f32[16,810]{1,0:T(8,128)}, u32[]{:S(2)}) %copy-start.13) | copy-done | bytes 51864
  12.7 0.5 %omega.1.omega_ref = f32[320,512]{1,0:T(8,128)S(1)} custom-call(f32[16,810]{1,0:T(8,128)S(1)} %copy-done.13, f32[16,810]{1,0:T(8,128)S(1)} %collective-permute-done.refs_1_, bf16[128,512]{1,0:T(8,128)(2,1)S(1)} %copy-done.11, bf16[128,512]{1,0:T(8,128)(2,1)S(1)} %copy-done.10), custom_call_target="tpu_custom_call" | custom-call | flops 125829120 | bytes 655360 | tf_op jit(solution)/shard_map/omega/pallas_call | solution.py:574
  13.2 4.2 %all-to-all-done.x_ref = f32[16,4,128]{2,1,0:T(4,128)S(1)} async-done(((f32[16,4,128]{2,1,0:T(4,128)}), f32[16,4,128]{2,1,0:T(4,128)S(1)}, u32[]{:S(2)}, u32[]{:S(2)}) %all-to-all-start) | async-done | bytes 32800 | tf_op jit(solution)/shard_map/all_to_all | solution.py:569
  17.4 0.0 copy-done.4
  17.4 0.0 copy-done.5
  17.4 0.0 copy-done.6
  17.4 0.0 copy-done.7
  17.4 0.0 copy-done.8
  17.4 0.0 copy-done.9
  17.4 0.0 copy-done.3
  17.4 0.0 copy-done
  17.4 0.0 copy-done.1
  17.4 0.0 copy-done.2
  17.5 0.0 copy-done.14
  17.5 0.0 copy-start.12
  17.5 3.7 %core.1 = f32[8,4,128]{2,1,0:T(4,128)S(1)} custom-call(f32[16,4,128]{2,1,0:T(4,128)S(1)} %all-to-all-done.x_ref, f32[320,512]{1,0:T(8,128)S(1)} %omega.1.omega_ref, bf16[256,512]{1,0:T(8,128)(2,1)S(1)} %copy-done.5, bf16[256,512]{1,0:T(8,128)(2,1)S(1)} %copy-done.4, bf16[512,256]{1,0:T(8,128)(2,1)S(1)} %copy-done.3, bf16[512,256]{1,0:T(8,128)(2,1)S(1)} %copy-done.2, ...), custom_call_target="tpu_custom_call" | custom-call | tf_op jit(solution)/shard_map/core/pallas_call | solution.py:613
  21.2 8.0 %all_to_all.10.cells_ref = f32[8,4,128]{2,1,0:T(4,128)S(1)} all-to-all(f32[8,4,128]{2,1,0:T(4,128)S(1)} %core.1), channel_id=1, replica_groups=mesh['win'=2,'wide'=8,'narrow'=2] {'wide'}, dimensions={0} | all-to-all | bytes 32768 | tf_op jit(solution)/shard_map/all_to_all | solution.py:622
  29.2 1.2 %synthesis.1 = f32[256,1024]{1,0:T(8,128)} custom-call(f32[8,4,128]{2,1,0:T(4,128)S(1)} %all_to_all.10.cells_ref, bf16[48,1024]{1,0:T(8,128)(2,1)S(1)} %copy-done.12), custom_call_target="tpu_custom_call" | custom-call | tf_op jit(solution)/shard_map/synthesis/pallas_call | solution.py:625
  (7 shorter events, 0.0 us)
Async XLA Ops:
  0.0 10.9 %collective-permute-start = (f32[16,810]{1,0:T(8,128)}, f32[16,810]{1,0:T(8,128)S(1)}, u32[]{:S(2)}, u32[]{:S(2)}) collective-permute-start(f32[16,810]{1,0:T(8,128)} %refs_0_.1), channel_id=1, source_target_pairs={{0,1},{1,0},{2,3},{3,2},{4,5},{5,4},{6,7},{7,6},{8,9},{9,8},{10,11... | collective-permute-start | bytes 155528 | tf_op jit(solution)/shard_map/ppermute | solution.py:553
  3.0 7.9 %copy-start.10 = (bf16[128,512]{1,0:T(8,128)(2,1)S(1)}, bf16[128,512]{1,0:T(8,128)(2,1)}, u32[]{:S(2)}) copy-start(bf16[128,512]{1,0:T(8,128)(2,1)} %constant.32.clone.refs_3_) | copy-start | bytes 393220
  3.0 14.4 %copy-start.4 = (bf16[256,512]{1,0:T(8,128)(2,1)S(1)}, bf16[256,512]{1,0:T(8,128)(2,1)}, u32[]{:S(2)}) copy-start(bf16[256,512]{1,0:T(8,128)(2,1)} %constant.34.clone.analysis_low) | copy-start | bytes 786436
  3.0 14.4 %copy-start.5 = (bf16[256,512]{1,0:T(8,128)(2,1)S(1)}, bf16[256,512]{1,0:T(8,128)(2,1)}, u32[]{:S(2)}) copy-start(bf16[256,512]{1,0:T(8,128)(2,1)} %constant.33.clone.analysis_high) | copy-start | bytes 786436
  3.0 14.4 %copy-start.6 = (bf16[256,256]{1,0:T(8,128)(2,1)S(1)}, bf16[256,256]{1,0:T(8,128)(2,1)}, u32[]{:S(2)}) copy-start(bf16[256,256]{1,0:T(8,128)(2,1)} %constant.40.clone.window_low) | copy-start | bytes 393220
  3.0 14.4 %copy-start.7 = (bf16[256,256]{1,0:T(8,128)(2,1)S(1)}, bf16[256,256]{1,0:T(8,128)(2,1)}, u32[]{:S(2)}) copy-start(bf16[256,256]{1,0:T(8,128)(2,1)} %constant.39.clone.window_high) | copy-start | bytes 393220
  3.0 14.4 %copy-start.8 = (bf16[128,512]{1,0:T(8,128)(2,1)S(1)}, bf16[128,512]{1,0:T(8,128)(2,1)}, u32[]{:S(2)}) copy-start(bf16[128,512]{1,0:T(8,128)(2,1)} %constant.38.clone.basis_low) | copy-start | bytes 393220
  3.0 14.4 %copy-start.9 = (bf16[128,512]{1,0:T(8,128)(2,1)S(1)}, bf16[128,512]{1,0:T(8,128)(2,1)}, u32[]{:S(2)}) copy-start(bf16[128,512]{1,0:T(8,128)(2,1)} %constant.37.clone.basis_high) | copy-start | bytes 393220
  5.7 11.7 %copy-start.3 = (bf16[512,256]{1,0:T(8,128)(2,1)S(1)}, bf16[512,256]{1,0:T(8,128)(2,1)}, u32[]{:S(2)}) copy-start(bf16[512,256]{1,0:T(8,128)(2,1)} %constant.35.clone.sketch_high) | copy-start | bytes 786436
  5.7 11.7 %all-to-all-start = ((f32[16,4,128]{2,1,0:T(4,128)}), f32[16,4,128]{2,1,0:T(4,128)S(1)}, u32[]{:S(2)}, u32[]{:S(2)}) async-start(f32[16,4,128]{2,1,0:T(4,128)} %spectrum.1), calls=%async_computation | async-start | bytes 65536 | tf_op jit(solution)/shard_map/all_to_all | solution.py:569
  10.9 6.6 %copy-start = (bf16[256,512]{1,0:T(8,128)(2,1)S(1)}, bf16[256,512]{1,0:T(8,128)(2,1)}, u32[]{:S(2)}) copy-start(bf16[256,512]{1,0:T(8,128)(2,1)} %constant.42.clone.back_low) | copy-start | bytes 786436
  10.9 6.6 %copy-start.1 = (bf16[256,512]{1,0:T(8,128)(2,1)S(1)}, bf16[256,512]{1,0:T(8,128)(2,1)}, u32[]{:S(2)}) copy-start(bf16[256,512]{1,0:T(8,128)(2,1)} %constant.41.clone.back_high) | copy-start | bytes 786436
  10.9 6.6 %copy-start.2 = (bf16[512,256]{1,0:T(8,128)(2,1)S(1)}, bf16[512,256]{1,0:T(8,128)(2,1)}, u32[]{:S(2)}) copy-start(bf16[512,256]{1,0:T(8,128)(2,1)} %constant.36.clone.sketch_low) | copy-start | bytes 786436
  10.9 1.0 %copy-start.11 = (bf16[128,512]{1,0:T(8,128)(2,1)S(1)}, bf16[128,512]{1,0:T(8,128)(2,1)}, u32[]{:S(2)}) copy-start(bf16[128,512]{1,0:T(8,128)(2,1)} %constant.31.clone.refs_2_) | copy-start | bytes 393220
  11.9 0.8 %copy-start.13 = (f32[16,810]{1,0:T(8,128)S(1)}, f32[16,810]{1,0:T(8,128)}, u32[]{:S(2)}) copy-start(f32[16,810]{1,0:T(8,128)} %refs_0_.1) | copy-start | bytes 155524
  12.7 4.8 %copy-start.14 = (f32[16,256]{1,0:T(8,128)S(1)}, f32[16,256]{1,0:T(8,128)}, u32[]{:S(2)}) copy-start(f32[16,256]{1,0:T(8,128)} %constant.43.clone.weight_ref) | copy-start | bytes 49156
  17.5 11.8 %copy-start.12 = (bf16[48,1024]{1,0:T(8,128)(2,1)S(1)}, bf16[48,1024]{1,0:T(8,128)(2,1)}, u32[]{:S(2)}) copy-start(bf16[48,1024]{1,0:T(8,128)(2,1)} %constant.44.clone.table_ref) | copy-start | bytes 294916

commit v3 on v2

--- a/solution.py
+++ b/solution.py
@@ -17,7 +17,7 @@
 FIRST_BIN = 16
 LANES = 128
 MIB = 1 << 20
-CHUNKS = 4
+CHUNKS = 2
 PIVOTS = 4
 CELLS = G3 * G4
 KEEP3, KEEP4 = G3 // 2, G4 // 2
@@ -183,44 +183,63 @@
     )
 
 
-def invert(gram_real, gram_imag, result):
-    size = gram_real.shape[0]
+def pivot_pair(upper, lower, corner, other, cross, scale):
+    turned = (cross[0], -cross[1])
+    first = minus_product(tuple(other * v for v in upper), cross, lower)
+    second = minus_product(tuple(corner * v for v in lower), turned, upper)
+    return tuple(v * scale for v in first), tuple(v * scale for v in second)
+
+
+def invert(real, imag, result):
+    size = real.shape[0]
     width = 2 * size
-    row_index = lax.broadcasted_iota(jnp.int32, (size, size), 0)
-    column_index = lax.broadcasted_iota(jnp.int32, (size, size), 1)
-    identity = (row_index == column_index).astype(jnp.float32)
-    real = jnp.concatenate([gram_real, identity], 1)
-    imag = jnp.concatenate([gram_imag, jnp.zeros_like(identity)], 1)
     tiles = [(real[t : t + 8], imag[t : t + 8]) for t in range(0, size, 8)]
     sublane = lax.broadcasted_iota(jnp.int32, (8, width), 0)
     for start in range(0, size, PIVOTS):
         home, at = start // 8, start % 8
+        lane = size + start
+
+        def spread(value, b, height):
+            return jnp.broadcast_to(value[:, lane + b : lane + b + 1], (height, width))
+
+        rows = [tuple(v[at + a : at + a + 1] for v in tiles[home]) for a in range(PIVOTS)]
+        block = {}
+        for a in range(PIVOTS):
+            block[a, a] = (spread(rows[a][0], a, 1),)
+            for b in range(a + 1, PIVOTS):
+                block[a, b] = tuple(spread(v, b, 1) for v in rows[a])
+                block[b, a] = (block[a, b][0], -block[a, b][1])
         columns = [
-            [
-                tuple(jnp.broadcast_to(v[:, start + b : start + b + 1], (8, width)) for v in tile)
-                for b in range(PIVOTS)
-            ]
-            for tile in tiles
+            [tuple(spread(v, b, 8) for v in tile) for b in range(PIVOTS)] for tile in tiles
         ]
-        rows = [tuple(v[at + a : at + a + 1] for v in tiles[home]) for a in range(PIVOTS)]
-        block = {
-            (a, b): tuple(
-                jnp.broadcast_to(v[:, start + b : start + b + 1], (1, width)) for v in rows[a]
-            )
-            for a in range(PIVOTS)
-            for b in range(PIVOTS)
-        }
-        for p in range(PIVOTS):
-            scale = 1.0 / block[p, p][0]
-            rows[p] = tuple(v * scale for v in rows[p])
-            for b in range(p + 1, PIVOTS):
-                block[p, b] = tuple(v * scale for v in block[p, b])
-            for a in range(PIVOTS):
-                if a == p:
+        for p in range(0, PIVOTS, 2):
+            q = p + 1
+            corner, other, cross = block[p, p][0], block[q, q][0], block[p, q]
+            scale = 1.0 / (corner * other - (cross[0] * cross[0] + cross[1] * cross[1]))
+            pair = (corner, other, cross, scale)
+            rows[p], rows[q] = pivot_pair(rows[p], rows[q], *pair)
+            later = range(p + 2, PIVOTS)
+            done = {}
+            for c in later:
+                done[p, c], done[q, c] = pivot_pair(block[p, c], block[q, c], *pair)
+            for o in range(PIVOTS):
+                if o in (p, q):
                     continue
-                rows[a] = minus_product(rows[a], block[a, p], rows[p])
-                for b in range(p + 1, PIVOTS):
-                    block[a, b] = minus_product(block[a, b], block[a, p], block[p, b])
+                left, right = block[o, p], block[o, q]
+                rows[o] = minus_product(minus_product(rows[o], left, rows[p]), right, rows[q])
+                for c in later:
+                    if o == c:
+                        first, second = done[p, c], done[q, c]
+                        value = block[o, o][0]
+                        value = value - (left[0] * first[0] - left[1] * first[1])
+                        value = value - (right[0] * second[0] - right[1] * second[1])
+                        done[o, o] = (value,)
+                    elif o < c:
+                        value = minus_product(block[o, c], left, done[p, c])
+                        done[o, c] = minus_product(value, right, done[q, c])
+                        if o > q:
+                            done[c, o] = (done[o, c][0], -done[o, c][1])
+            block.update(done)
         for t in range(len(tiles)):
             tile = tiles[t]
             for b in range(PIVOTS):
@@ -232,7 +251,7 @@
             tiles[t] = tile
         yield
     for part in range(2):
-        result.append(jnp.concatenate([tile[part] for tile in tiles], 0)[:, size:])
+        result.append(jnp.concatenate([tile[part] for tile in tiles], 0)[:, :size])
 
 
 def interleave(*steps):
@@ -364,12 +383,24 @@
         [sketch[b * rank : (b + 1) * rank, 2 * ROWS :] for b in range(blocks)], 1
     )
     contract = (((1,), (1,)), ((), ()))
-    gram_real = lax.dot_general(
-        straight, straight, contract, precision=highest, preferred_element_type=jnp.float32
-    )
-    gram_imag = lax.dot_general(
-        straight, turned, contract, precision=highest, preferred_element_type=jnp.float32
-    )
+    space = jnp.zeros_like(straight)
+
+    def gram(right):
+        return lax.dot_general(
+            straight,
+            jnp.concatenate([space, right], 0),
+            contract,
+            precision=highest,
+            preferred_element_type=jnp.float32,
+        )
+
+    row_index = lax.broadcasted_iota(jnp.int32, (rank, 2 * rank), 0)
+    column_index = lax.broadcasted_iota(jnp.int32, (rank, 2 * rank), 1)
+    unit = 1.0 / jnp.max(jnp.abs(spectrum), keepdims=True)
+    gram_real = gram(straight) * unit * unit
+    gram_imag = gram(turned) * unit * unit
+    gram_real = jnp.where(row_index == column_index, 1.0, gram_real)
+
     def partner(a):
         k1 = own - a
         valid = jnp.logical_and(k1 >= 0, k1 < span1).astype(jnp.float32)
@@ -468,23 +499,15 @@
 
     inverse = []
     interleave(invert(gram_real, gram_imag, inverse), own_basis())
-    mixer = jnp.concatenate(inverse, 1)
+    mixer = jnp.concatenate(inverse, 0) * unit * unit
 
     def mix(b, carry):
-        real = bhat[rows(b * rank, rank), :half]
-        imag = bhat[rows(b * rank, rank), half:]
-        uhat[rows(b * rank, rank), :half] = jnp.dot(
-            mixer,
-            jnp.concatenate([real, imag], 0),
-            precision=highest,
-            preferred_element_type=jnp.float32,
+        where = rows(b * rank, rank)
+        both = jnp.dot(
+            mixer, bhat[where, :], precision=highest, preferred_element_type=jnp.float32
         )
-        uhat[rows(b * rank, rank), half:] = jnp.dot(
-            mixer,
-            jnp.concatenate([imag, -real], 0),
-            precision=highest,
-            preferred_element_type=jnp.float32,
-        )
+        uhat[where, :half] = both[:rank, :half] + both[rank:, half:]
+        uhat[where, half:] = both[:rank, half:] - both[rank:, :half]
         return carry
 
     sweep(blocks, mix, 0)

time: 30.8 us -> 30.4 us (0.987)
  Pallas kernels: 8.12 us -> 7.75 us
where the time goes in v3:
time: 30.4 us; the launch traced here: 30.1 us
  starting transfers between devices  8.09 us (27%)
  blocking collectives  8.02 us (26%)
  Pallas kernels  7.75 us (25%)
  waiting for transfers between devices  4.21 us (14%)
  local copies, waits for them, and re-layouts  1.85 us (6%)
    all_to_all x1, blocking collectives, per_device(): lax.all_to_all(rebuilt, 'wide', split_axis=0, concat_axis=0, tiled=True)  8.02 us
    all_to_all x1, starting transfers between devices, per_device(): lax.all_to_all(blocks, ('wide', 'narrow'), split_axis=0, concat_axis=0, t...  5.13 us
    all_to_all x1, waiting for transfers between devices, per_device(): lax.all_to_all(blocks, ('wide', 'narrow'), split_axis=0, concat_axis=0, t...  4.21 us
    pallas_call x1, Pallas kernels, per_device(): pl.pallas_call(functools.partial(core_kernel, (first, second, rank)), out...  3.6 us
    ppermute x1, starting transfers between devices, per_device(): omegas.append(lax.ppermute(omega, 'narrow', ring))  2.97 us
    pallas_call x1, Pallas kernels, per_device(): pl.pallas_call(spectrum_kernel, out_shape=jax.ShapeDtypeStruct((dests, li...  2.46 us
    unnamed x30, local copies, waits for them, and re-layouts  1.85 us
    pallas_call x1, Pallas kernels, per_device(): pl.pallas_call(synthesis_kernel, out_shape=jax.ShapeDtypeStruct((CELLS, S...  1.24 us
  transfers between devices with their start and end apart: 2, of which 1 were waited for; matrix products, arithmetic and copies ran while one was open for 0% of the time, Pallas kernels for 10%

profile of v3, /device:TPU:0, one launch (start us, length us, event | category | flops | bytes accessed | tf_op | source)
XLA Modules:
  0.0 30.1 jit_solution(2224616640309354329)
XLA Ops:
  0.0 3.0 %collective-permute-start = (f32[16,810]{1,0:T(8,128)}, f32[16,810]{1,0:T(8,128)S(1)}, u32[]{:S(2)}, u32[]{:S(2)}) collective-permute-start(f32[16,810]{1,0:T(8,128)} %refs_0_.1), channel_id=1, source_target_pairs={{0,1},{1,0},{2,3},{3,2},{4,5},{5,4},{6,7},{7,6},{8,9},{9,8},{10,11... | collective-permute-start | bytes 155528 | tf_op jit(solution)/shard_map/ppermute | solution.py:576
  3.0 0.0 copy-start.7
  3.0 0.0 copy-start.8
  3.0 0.0 copy-start.9
  3.0 2.5 %spectrum.1 = f32[16,4,128]{2,1,0:T(4,128)} custom-call(f32[256,1024]{1,0:T(8,128)} %bitcast.3, s32[1,256]{1,0:T(1,128)} %bitcast.4, bf16[64,1024]{1,0:T(8,128)(2,1)} %constant.30.clone.table_ref), custom_call_target="tpu_custom_call" | custom-call | tf_op jit(solution)/shard_map/spectrum/pallas_call | solution.py:579
  5.5 0.0 copy-start.3
  5.5 5.1 %all-to-all-start = ((f32[16,4,128]{2,1,0:T(4,128)}), f32[16,4,128]{2,1,0:T(4,128)S(1)}, u32[]{:S(2)}, u32[]{:S(2)}) async-start(f32[16,4,128]{2,1,0:T(4,128)} %spectrum.1), calls=%async_computation | async-start | bytes 65536 | tf_op jit(solution)/shard_map/all_to_all | solution.py:592
  10.6 0.0 copy-start
  10.6 0.0 copy-start.1
  10.7 0.0 copy-start.2
  10.7 0.0 collective-permute-done.refs_1_
  10.7 0.0 copy-done.10
  10.7 0.0 copy-start.11
  10.7 1.0 %copy-done.11 = bf16[128,512]{1,0:T(8,128)(2,1)S(1)} copy-done((bf16[128,512]{1,0:T(8,128)(2,1)S(1)}, bf16[128,512]{1,0:T(8,128)(2,1)}, u32[]{:S(2)}) %copy-start.11) | copy-done | bytes 131096
  11.7 0.8 %copy-done.13 = f32[16,810]{1,0:T(8,128)S(1)} copy-done((f32[16,810]{1,0:T(8,128)S(1)}, f32[16,810]{1,0:T(8,128)}, u32[]{:S(2)}) %copy-start.13) | copy-done | bytes 51864
  12.5 0.5 %omega.1.omega_ref = f32[320,512]{1,0:T(8,128)S(1)} custom-call(f32[16,810]{1,0:T(8,128)S(1)} %copy-done.13, f32[16,810]{1,0:T(8,128)S(1)} %collective-permute-done.refs_1_, bf16[128,512]{1,0:T(8,128)(2,1)S(1)} %copy-done.11, bf16[128,512]{1,0:T(8,128)(2,1)S(1)} %copy-done.10), custom_call_target="tpu_custom_call" | custom-call | flops 125829120 | bytes 655360 | tf_op jit(solution)/shard_map/omega/pallas_call | solution.py:597
  12.9 4.2 %all-to-all-done.x_ref = f32[16,4,128]{2,1,0:T(4,128)S(1)} async-done(((f32[16,4,128]{2,1,0:T(4,128)}), f32[16,4,128]{2,1,0:T(4,128)S(1)}, u32[]{:S(2)}, u32[]{:S(2)}) %all-to-all-start) | async-done | bytes 32800 | tf_op jit(solution)/shard_map/all_to_all | solution.py:592
  17.2 0.0 copy-done.4
  17.2 0.0 copy-done.5
  17.2 0.0 copy-done.6
  17.2 0.0 copy-done.7
  17.2 0.0 copy-done.8
  17.2 0.0 copy-done.9
  17.2 0.0 copy-done.3
  17.2 0.0 copy-done
  17.2 0.0 copy-done.1
  17.2 0.0 copy-done.2
  17.2 0.0 copy-done.14
  17.2 0.0 copy-start.12
  17.3 3.6 %core.1 = f32[8,4,128]{2,1,0:T(4,128)S(1)} custom-call(f32[16,4,128]{2,1,0:T(4,128)S(1)} %all-to-all-done.x_ref, f32[320,512]{1,0:T(8,128)S(1)} %omega.1.omega_ref, bf16[256,512]{1,0:T(8,128)(2,1)S(1)} %copy-done.5, bf16[256,512]{1,0:T(8,128)(2,1)S(1)} %copy-done.4, bf16[512,256]{1,0:T(8,128)(2,1)S(1)} %copy-done.3, bf16[512,256]{1,0:T(8,128)(2,1)S(1)} %copy-done.2, ...), custom_call_target="tpu_custom_call" | custom-call | tf_op jit(solution)/shard_map/core/pallas_call | solution.py:636
  20.9 8.0 %all_to_all.10.cells_ref = f32[8,4,128]{2,1,0:T(4,128)S(1)} all-to-all(f32[8,4,128]{2,1,0:T(4,128)S(1)} %core.1), channel_id=1, replica_groups=mesh['win'=2,'wide'=8,'narrow'=2] {'wide'}, dimensions={0} | all-to-all | bytes 32768 | tf_op jit(solution)/shard_map/all_to_all | solution.py:645
  28.9 1.2 %synthesis.1 = f32[256,1024]{1,0:T(8,128)} custom-call(f32[8,4,128]{2,1,0:T(4,128)S(1)} %all_to_all.10.cells_ref, bf16[48,1024]{1,0:T(8,128)(2,1)S(1)} %copy-done.12), custom_call_target="tpu_custom_call" | custom-call | tf_op jit(solution)/shard_map/synthesis/pallas_call | solution.py:648
  (7 shorter events, 0.0 us)
Async XLA Ops:
  0.0 10.7 %collective-permute-start = (f32[16,810]{1,0:T(8,128)}, f32[16,810]{1,0:T(8,128)S(1)}, u32[]{:S(2)}, u32[]{:S(2)}) collective-permute-start(f32[16,810]{1,0:T(8,128)} %refs_0_.1), channel_id=1, source_target_pairs={{0,1},{1,0},{2,3},{3,2},{4,5},{5,4},{6,7},{7,6},{8,9},{9,8},{10,11... | collective-permute-start | bytes 155528 | tf_op jit(solution)/shard_map/ppermute | solution.py:576
  3.0 7.7 %copy-start.10 = (bf16[128,512]{1,0:T(8,128)(2,1)S(1)}, bf16[128,512]{1,0:T(8,128)(2,1)}, u32[]{:S(2)}) copy-start(bf16[128,512]{1,0:T(8,128)(2,1)} %constant.32.clone.refs_3_) | copy-start | bytes 393220
  3.0 14.2 %copy-start.4 = (bf16[256,512]{1,0:T(8,128)(2,1)S(1)}, bf16[256,512]{1,0:T(8,128)(2,1)}, u32[]{:S(2)}) copy-start(bf16[256,512]{1,0:T(8,128)(2,1)} %constant.34.clone.analysis_low) | copy-start | bytes 786436
  3.0 14.2 %copy-start.5 = (bf16[256,512]{1,0:T(8,128)(2,1)S(1)}, bf16[256,512]{1,0:T(8,128)(2,1)}, u32[]{:S(2)}) copy-start(bf16[256,512]{1,0:T(8,128)(2,1)} %constant.33.clone.analysis_high) | copy-start | bytes 786436
  3.0 14.2 %copy-start.6 = (bf16[256,256]{1,0:T(8,128)(2,1)S(1)}, bf16[256,256]{1,0:T(8,128)(2,1)}, u32[]{:S(2)}) copy-start(bf16[256,256]{1,0:T(8,128)(2,1)} %constant.40.clone.window_low) | copy-start | bytes 393220
  3.0 14.2 %copy-start.7 = (bf16[256,256]{1,0:T(8,128)(2,1)S(1)}, bf16[256,256]{1,0:T(8,128)(2,1)}, u32[]{:S(2)}) copy-start(bf16[256,256]{1,0:T(8,128)(2,1)} %constant.39.clone.window_high) | copy-start | bytes 393220
  3.0 14.2 %copy-start.8 = (bf16[128,512]{1,0:T(8,128)(2,1)S(1)}, bf16[128,512]{1,0:T(8,128)(2,1)}, u32[]{:S(2)}) copy-start(bf16[128,512]{1,0:T(8,128)(2,1)} %constant.38.clone.basis_low) | copy-start | bytes 393220
  3.0 14.2 %copy-start.9 = (bf16[128,512]{1,0:T(8,128)(2,1)S(1)}, bf16[128,512]{1,0:T(8,128)(2,1)}, u32[]{:S(2)}) copy-start(bf16[128,512]{1,0:T(8,128)(2,1)} %constant.37.clone.basis_high) | copy-start | bytes 393220
  5.5 11.7 %copy-start.3 = (bf16[512,256]{1,0:T(8,128)(2,1)S(1)}, bf16[512,256]{1,0:T(8,128)(2,1)}, u32[]{:S(2)}) copy-start(bf16[512,256]{1,0:T(8,128)(2,1)} %constant.35.clone.sketch_high) | copy-start | bytes 786436
  5.5 11.7 %all-to-all-start = ((f32[16,4,128]{2,1,0:T(4,128)}), f32[16,4,128]{2,1,0:T(4,128)S(1)}, u32[]{:S(2)}, u32[]{:S(2)}) async-start(f32[16,4,128]{2,1,0:T(4,128)} %spectrum.1), calls=%async_computation | async-start | bytes 65536 | tf_op jit(solution)/shard_map/all_to_all | solution.py:592
  10.6 6.6 %copy-start = (bf16[256,512]{1,0:T(8,128)(2,1)S(1)}, bf16[256,512]{1,0:T(8,128)(2,1)}, u32[]{:S(2)}) copy-start(bf16[256,512]{1,0:T(8,128)(2,1)} %constant.42.clone.back_low) | copy-start | bytes 786436
  10.6 6.6 %copy-start.1 = (bf16[256,512]{1,0:T(8,128)(2,1)S(1)}, bf16[256,512]{1,0:T(8,128)(2,1)}, u32[]{:S(2)}) copy-start(bf16[256,512]{1,0:T(8,128)(2,1)} %constant.41.clone.back_high) | copy-start | bytes 786436
  10.7 6.6 %copy-start.2 = (bf16[512,256]{1,0:T(8,128)(2,1)S(1)}, bf16[512,256]{1,0:T(8,128)(2,1)}, u32[]{:S(2)}) copy-start(bf16[512,256]{1,0:T(8,128)(2,1)} %constant.36.clone.sketch_low) | copy-start | bytes 786436
  10.7 1.0 %copy-start.11 = (bf16[128,512]{1,0:T(8,128)(2,1)S(1)}, bf16[128,512]{1,0:T(8,128)(2,1)}, u32[]{:S(2)}) copy-start(bf16[128,512]{1,0:T(8,128)(2,1)} %constant.31.clone.refs_2_) | copy-start | bytes 393220
  11.7 0.8 %copy-start.13 = (f32[16,810]{1,0:T(8,128)S(1)}, f32[16,810]{1,0:T(8,128)}, u32[]{:S(2)}) copy-start(f32[16,810]{1,0:T(8,128)} %refs_0_.1) | copy-start | bytes 155524
  12.5 4.8 %copy-start.14 = (f32[16,256]{1,0:T(8,128)S(1)}, f32[16,256]{1,0:T(8,128)}, u32[]{:S(2)}) copy-start(f32[16,256]{1,0:T(8,128)} %constant.43.clone.weight_ref) | copy-start | bytes 49156
  17.2 11.6 %copy-start.12 = (bf16[48,1024]{1,0:T(8,128)(2,1)S(1)}, bf16[48,1024]{1,0:T(8,128)(2,1)}, u32[]{:S(2)}) copy-start(bf16[48,1024]{1,0:T(8,128)(2,1)} %constant.44.clone.table_ref) | copy-start | bytes 294916

commit v4 on v3

--- a/solution.py
+++ b/solution.py
@@ -276,12 +276,14 @@
     back_low,
     weight_ref,
     out_ref,
+    handed_ref,
     xhat,
     shat,
     bhat,
     uhat,
     dhat,
     ghat,
+    sends,
 ):
     first, second, rank = dims
     keep1, keep2 = first // 2, second // 2
@@ -528,14 +530,26 @@
     weight = weight_ref[pl.ds(pl.multiple_of(own * second, 8), second), :]
     real = real * weight
     imag = imag * weight
-    for piece in range(pieces):
-        out_ref[:, piece, :] = real[:, piece * LANES : (piece + 1) * LANES]
-        out_ref[:, pieces + piece, :] = imag[:, piece * LANES : (piece + 1) * LANES]
-
-
-def synthesis_kernel(cells_ref, table_ref, out_ref, out, sems):
+    here = lax.axis_index("wide")
+    for w in range(second):
+        offset = jnp.bitwise_xor(here, w)
+        slot = (offset % 2) * (second // 2) + offset // 2
+        for piece in range(pieces):
+            place = slice(piece * LANES, (piece + 1) * LANES)
+            sends[slot, pl.ds(piece, 1), :] = real[w : w + 1, place]
+            sends[slot, pl.ds(pieces + piece, 1), :] = imag[w : w + 1, place]
+    out_ref[...] = sends[: second // 2]
+    handed_ref[...] = sends[second // 2 :]
+
+
+def synthesis_kernel(*refs):
+    *block_refs, table_ref, out_ref, out, cells, sems = refs
+    here = lax.axis_index("wide")
+    for i in range(len(block_refs)):
+        for j in range(2):
+            cells[jnp.bitwise_xor(here, 2 * i + j)] = block_refs[i][j]
     parts = [
-        jnp.concatenate([cells_ref[:, part * PIECES + piece, :] for piece in range(PIECES)], 1)
+        jnp.concatenate([cells[:, part * PIECES + piece, :] for piece in range(PIECES)], 1)
         for part in range(2)
     ]
     high, low = split(jnp.concatenate(parts, 0))
@@ -632,31 +646,40 @@
         (area, 2 * CELLS),
         (2 * span2 * rank, CELLS),
         (2 * second, CELLS),
+        (second, lines, LANES),
     ]
-    rebuilt = pl.pallas_call(
+    chips = second // 2
+    kept, handed = pl.pallas_call(
         functools.partial(core_kernel, (first, second, rank)),
-        out_shape=jax.ShapeDtypeStruct((second, lines, LANES), jnp.float32),
+        out_shape=[jax.ShapeDtypeStruct((chips, lines, LANES), jnp.float32)] * 2,
         in_specs=[VMEM] * (2 + len(tables)),
-        out_specs=VMEM,
+        out_specs=[VMEM] * 2,
         scratch_shapes=[pltpu.VMEM(shape, jnp.float32) for shape in scratch],
         compiler_params=pltpu.CompilerParams(vmem_limit_bytes=24 * MIB),
         name="core",
     )(grid, omega_hat, *tables)
-    returned = lax.all_to_all(rebuilt, "wide", split_axis=0, concat_axis=0, tiled=True)
+
+    def across(value, offset):
+        return lax.ppermute(value, "wide", [(i, i ^ offset) for i in range(second)])
+
+    handed = across(handed, 1)
+    joined = jnp.stack([kept, handed], 1)
+    returned = [joined[0]] + [across(joined[i], 2 * i) for i in range(1, chips)]
 
     high, low = halves(synthesis_table(freq_total))
     filtered = pl.pallas_call(
         synthesis_kernel,
         out_shape=jax.ShapeDtypeStruct((CELLS, S), jnp.float32),
-        in_specs=[VMEM] * 2,
+        in_specs=[VMEM] * (chips + 1),
         out_specs=HBM,
         scratch_shapes=[
             pltpu.VMEM((PIECES, LANES, S), jnp.float32),
+            pltpu.VMEM((second, lines, LANES), jnp.float32),
             pltpu.SemaphoreType.DMA((PIECES,)),
         ],
         compiler_params=pltpu.CompilerParams(vmem_limit_bytes=8 * MIB),
         name="synthesis",
-    )(returned, np.concatenate([high, high, low], 0))
+    )(*returned, np.concatenate([high, high, low], 0))
     return filtered.reshape(traces.shape)
 
 

time: 30.4 us -> 29.6 us (0.974)
  blocking collectives: 8.02 us -> 0 us
  starting transfers between devices: 8.09 us -> 12.7 us
  waiting for transfers between devices: 4.21 us -> 6.86 us
    all_to_all x1 -> x0, blocking collectives: 8.02 us -> none  [per_device(): lax.all_to_all(rebuilt, 'wide', split_axis=0, concat_axis=0, tiled=True)]
    ppermute x0 -> x4, starting transfers between devices: none -> 4.57 us  [across(): return lax.ppermute(value, 'wide', [(i, i ^ offset) for i in range(second)])]
    ppermute x0 -> x4, waiting for transfers between devices: none -> 2.64 us  [across(): return lax.ppermute(value, 'wide', [(i, i ^ offset) for i in range(second)])]
  transfers between devices with their start and end apart: 2 -> 6, of which waited for: 1 -> 4; matrix products, arithmetic and copies ran while one was open for 0% -> 0% of each run, Pallas kernels for 10% -> 10%
where the time goes in v4:
time: 29.6 us; the launch traced here: 29.4 us
  starting transfers between devices  12.7 us (43%)
  Pallas kernels  7.79 us (26%)
  waiting for transfers between devices  6.86 us (23%)
  local copies, waits for them, and re-layouts  1.85 us (6%)
    all_to_all x1, starting transfers between devices, per_device(): lax.all_to_all(blocks, ('wide', 'narrow'), split_axis=0, concat_axis=0, t...  5.13 us
    ppermute x4, starting transfers between devices, across(): return lax.ppermute(value, 'wide', [(i, i ^ offset) for i in range(second)])  4.57 us
    all_to_all x1, waiting for transfers between devices, per_device(): lax.all_to_all(blocks, ('wide', 'narrow'), split_axis=0, concat_axis=0, t...  4.21 us
    pallas_call x1, Pallas kernels, per_device(): pl.pallas_call(functools.partial(core_kernel, (first, second, rank)), out...  3.63 us
    ppermute x1, starting transfers between devices, per_device(): omegas.append(lax.ppermute(omega, 'narrow', ring))  2.97 us
    ppermute x4, waiting for transfers between devices, across(): return lax.ppermute(value, 'wide', [(i, i ^ offset) for i in range(second)])  2.64 us
    pallas_call x1, Pallas kernels, per_device(): pl.pallas_call(spectrum_kernel, out_shape=jax.ShapeDtypeStruct((dests, li...  2.46 us
    unnamed x30, local copies, waits for them, and re-layouts  1.85 us
  transfers between devices with their start and end apart: 6, of which 4 were waited for; matrix products, arithmetic and copies ran while one was open for 0% of the time, Pallas kernels for 10%

profile of v4, /device:TPU:0, one launch (start us, length us, event | category | flops | bytes accessed | tf_op | source)
XLA Modules:
  0.0 29.4 jit_solution(13591878694702898093)
XLA Ops:
  0.0 3.0 %collective-permute-start = (f32[16,810]{1,0:T(8,128)}, f32[16,810]{1,0:T(8,128)S(1)}, u32[]{:S(2)}, u32[]{:S(2)}) collective-permute-start(f32[16,810]{1,0:T(8,128)} %refs_0_.1), channel_id=1, source_target_pairs={{0,1},{1,0},{2,3},{3,2},{4,5},{5,4},{6,7},{7,6},{8,9},{9,8},{10,11... | collective-permute-start | bytes 155528 | tf_op jit(solution)/shard_map/ppermute | solution.py:590
  3.0 0.0 copy-start.7
  3.0 0.0 copy-start.8
  3.0 0.0 copy-start.9
  3.0 2.5 %spectrum.1 = f32[16,4,128]{2,1,0:T(4,128)} custom-call(f32[256,1024]{1,0:T(8,128)} %bitcast.14, s32[1,256]{1,0:T(1,128)} %bitcast.16, bf16[64,1024]{1,0:T(8,128)(2,1)} %constant.30.clone.table_ref), custom_call_target="tpu_custom_call" | custom-call | tf_op jit(solution)/shard_map/spectrum/pallas_call | solution.py:593
  5.5 0.0 copy-start.3
  5.5 5.1 %all-to-all-start = ((f32[16,4,128]{2,1,0:T(4,128)}), f32[16,4,128]{2,1,0:T(4,128)S(1)}, u32[]{:S(2)}, u32[]{:S(2)}) async-start(f32[16,4,128]{2,1,0:T(4,128)} %spectrum.1), calls=%async_computation | async-start | bytes 65536 | tf_op jit(solution)/shard_map/all_to_all | solution.py:606
  10.6 0.0 copy-start
  10.6 0.0 copy-start.1
  10.7 0.0 copy-start.2
  10.7 0.0 collective-permute-done.refs_1_
  10.7 0.0 copy-done.10
  10.7 0.0 copy-start.11
  10.7 1.0 %copy-done.11 = bf16[128,512]{1,0:T(8,128)(2,1)S(1)} copy-done((bf16[128,512]{1,0:T(8,128)(2,1)S(1)}, bf16[128,512]{1,0:T(8,128)(2,1)}, u32[]{:S(2)}) %copy-start.11) | copy-done | bytes 131096
  11.7 0.8 %copy-done.13 = f32[16,810]{1,0:T(8,128)S(1)} copy-done((f32[16,810]{1,0:T(8,128)S(1)}, f32[16,810]{1,0:T(8,128)}, u32[]{:S(2)}) %copy-start.13) | copy-done | bytes 51864
  12.5 0.5 %omega.1.omega_ref = f32[320,512]{1,0:T(8,128)S(1)} custom-call(f32[16,810]{1,0:T(8,128)S(1)} %copy-done.13, f32[16,810]{1,0:T(8,128)S(1)} %collective-permute-done.refs_1_, bf16[128,512]{1,0:T(8,128)(2,1)S(1)} %copy-done.11, bf16[128,512]{1,0:T(8,128)(2,1)S(1)} %copy-done.10), custom_call_target="tpu_custom_call" | custom-call | flops 125829120 | bytes 655360 | tf_op jit(solution)/shard_map/omega/pallas_call | solution.py:611
  12.9 4.2 %all-to-all-done.x_ref = f32[16,4,128]{2,1,0:T(4,128)S(1)} async-done(((f32[16,4,128]{2,1,0:T(4,128)}), f32[16,4,128]{2,1,0:T(4,128)S(1)}, u32[]{:S(2)}, u32[]{:S(2)}) %all-to-all-start) | async-done | bytes 32800 | tf_op jit(solution)/shard_map/all_to_all | solution.py:606
  17.2 0.0 copy-done.4
  17.2 0.0 copy-done.5
  17.2 0.0 copy-done.6
  17.2 0.0 copy-done.7
  17.2 0.0 copy-start.12
  17.3 3.6 %core.1 = (f32[4,4,128]{2,1,0:T(4,128)S(1)}, f32[4,4,128]{2,1,0:T(4,128)S(1)}) custom-call(f32[16,4,128]{2,1,0:T(4,128)S(1)} %all-to-all-done.x_ref, f32[320,512]{1,0:T(8,128)S(1)} %omega.1.omega_ref, bf16[256,512]{1,0:T(8,128)(2,1)S(1)} %copy-done.5, bf16[256,512]{1,0:T(8,128)(2,1)S(1)} %copy-done.4, bf16[512,256]{1,0:T(8,128)(2,1)S(1)} %copy-done.3, ...), custom_call_target="tpu_custom_call" | custom-call | tf_op jit(solution)/shard_map/core/pallas_call | solution.py:652
  20.9 0.2 collective-permute-start.1
  21.1 1.1 %collective-permute-done.1 = f32[4,4,128]{2,1,0:T(4,128)S(1)} collective-permute-done((f32[4,4,128]{2,1,0:T(4,128)S(1)}, f32[4,4,128]{2,1,0:T(4,128)S(1)}, u32[]{:S(2)}, u32[]{:S(2)}) %collective-permute-start.1) | collective-permute-done | bytes 8224 | tf_op jit(solution)/shard_map/ppermute | solution.py:663
  22.1 0.7 %collective-permute-start.4 = (f32[2,4,128]{2,1,0:T(4,128)S(1)}, f32[2,4,128]{2,1,0:T(4,128)S(1)}, u32[]{:S(2)}, u32[]{:S(2)}) collective-permute-start(f32[2,4,128]{2,1,0:T(4,128)S(1)} %get-tuple-element.9), channel_id=1, source_target_pairs={{0,12},{2,14},{4,8},{6,10},{8,4},{10,6},{12,0},{14,2},{1,13},{3,15... | collective-permute-start | bytes 12296 | tf_op jit(solution)/shard_map/ppermute | solution.py:663
  22.9 0.5 %collective-permute-start.2 = (f32[2,4,128]{2,1,0:T(4,128)S(1)}, f32[2,4,128]{2,1,0:T(4,128)S(1)}, u32[]{:S(2)}, u32[]{:S(2)}) collective-permute-start(f32[2,4,128]{2,1,0:T(4,128)S(1)} %get-tuple-element.11), channel_id=1, source_target_pairs={{0,4},{2,6},{4,0},{6,2},{8,12},{10,14},{12,8},{14,10},{1,5},{3,7},... | collective-permute-start | bytes 12296 | tf_op jit(solution)/shard_map/ppermute | solution.py:663
  23.3 3.2 %collective-permute-start.3 = (f32[2,4,128]{2,1,0:T(4,128)S(1)}, f32[2,4,128]{2,1,0:T(4,128)S(1)}, u32[]{:S(2)}, u32[]{:S(2)}) collective-permute-start(f32[2,4,128]{2,1,0:T(4,128)S(1)} %get-tuple-element.12), channel_id=1, source_target_pairs={{0,8},{2,10},{4,12},{6,14},{8,0},{10,2},{12,4},{14,6},{1,9},{3,11}... | collective-permute-start | bytes 12296 | tf_op jit(solution)/shard_map/ppermute | solution.py:663
  26.5 1.0 %collective-permute-done.4.refs_3_ = f32[2,4,128]{2,1,0:T(4,128)S(1)} collective-permute-done((f32[2,4,128]{2,1,0:T(4,128)S(1)}, f32[2,4,128]{2,1,0:T(4,128)S(1)}, u32[]{:S(2)}, u32[]{:S(2)}) %collective-permute-start.4) | collective-permute-done | bytes 4128 | tf_op jit(solution)/shard_map/ppermute | solution.py:663
  27.5 0.0 collective-permute-done.2.refs_1_
  27.5 0.6 %collective-permute-done.3.refs_2_ = f32[2,4,128]{2,1,0:T(4,128)S(1)} collective-permute-done((f32[2,4,128]{2,1,0:T(4,128)S(1)}, f32[2,4,128]{2,1,0:T(4,128)S(1)}, u32[]{:S(2)}, u32[]{:S(2)}) %collective-permute-start.3) | collective-permute-done | bytes 4128 | tf_op jit(solution)/shard_map/ppermute | solution.py:663
  28.1 1.3 %synthesis.1 = f32[256,1024]{1,0:T(8,128)} custom-call(f32[2,4,128]{2,1,0:T(4,128)S(1)} %get-tuple-element.10.refs_0_, f32[2,4,128]{2,1,0:T(4,128)S(1)} %collective-permute-done.2.refs_1_, f32[2,4,128]{2,1,0:T(4,128)S(1)} %collective-permute-done.3.refs_2_, f32[2,4,128]{2,1,0:T(4,128)S(1)} %collective-permute-done.4.refs_3_, bf16[48,1024]{1,0:T(8,128)(2,1)S(1)} %copy-done.12), custom_call_target="tpu_custom_call" | custom-call | tf_op jit(solution)/shard_map/synthesis/pallas_call | solution.py:670
  (15 shorter events, 0.0 us)
Async XLA Ops:
  0.0 10.7 %collective-permute-start = (f32[16,810]{1,0:T(8,128)}, f32[16,810]{1,0:T(8,128)S(1)}, u32[]{:S(2)}, u32[]{:S(2)}) collective-permute-start(f32[16,810]{1,0:T(8,128)} %refs_0_.1), channel_id=1, source_target_pairs={{0,1},{1,0},{2,3},{3,2},{4,5},{5,4},{6,7},{7,6},{8,9},{9,8},{10,11... | collective-permute-start | bytes 155528 | tf_op jit(solution)/shard_map/ppermute | solution.py:590
  3.0 7.7 %copy-start.10 = (bf16[128,512]{1,0:T(8,128)(2,1)S(1)}, bf16[128,512]{1,0:T(8,128)(2,1)}, u32[]{:S(2)}) copy-start(bf16[128,512]{1,0:T(8,128)(2,1)} %constant.32.clone.refs_3_) | copy-start | bytes 393220
  3.0 14.2 %copy-start.4 = (bf16[256,512]{1,0:T(8,128)(2,1)S(1)}, bf16[256,512]{1,0:T(8,128)(2,1)}, u32[]{:S(2)}) copy-start(bf16[256,512]{1,0:T(8,128)(2,1)} %constant.34.clone.analysis_low) | copy-start | bytes 786436
  3.0 14.2 %copy-start.5 = (bf16[256,512]{1,0:T(8,128)(2,1)S(1)}, bf16[256,512]{1,0:T(8,128)(2,1)}, u32[]{:S(2)}) copy-start(bf16[256,512]{1,0:T(8,128)(2,1)} %constant.33.clone.analysis_high) | copy-start | bytes 786436
  3.0 14.2 %copy-start.6 = (bf16[256,256]{1,0:T(8,128)(2,1)S(1)}, bf16[256,256]{1,0:T(8,128)(2,1)}, u32[]{:S(2)}) copy-start(bf16[256,256]{1,0:T(8,128)(2,1)} %constant.40.clone.window_low) | copy-start | bytes 393220
  3.0 14.2 %copy-start.7 = (bf16[256,256]{1,0:T(8,128)(2,1)S(1)}, bf16[256,256]{1,0:T(8,128)(2,1)}, u32[]{:S(2)}) copy-start(bf16[256,256]{1,0:T(8,128)(2,1)} %constant.39.clone.window_high) | copy-start | bytes 393220
  3.0 14.2 %copy-start.8 = (bf16[128,512]{1,0:T(8,128)(2,1)S(1)}, bf16[128,512]{1,0:T(8,128)(2,1)}, u32[]{:S(2)}) copy-start(bf16[128,512]{1,0:T(8,128)(2,1)} %constant.38.clone.basis_low) | copy-start | bytes 393220
  3.0 14.2 %copy-start.9 = (bf16[128,512]{1,0:T(8,128)(2,1)S(1)}, bf16[128,512]{1,0:T(8,128)(2,1)}, u32[]{:S(2)}) copy-start(bf16[128,512]{1,0:T(8,128)(2,1)} %constant.37.clone.basis_high) | copy-start | bytes 393220
  5.5 11.7 %copy-start.3 = (bf16[512,256]{1,0:T(8,128)(2,1)S(1)}, bf16[512,256]{1,0:T(8,128)(2,1)}, u32[]{:S(2)}) copy-start(bf16[512,256]{1,0:T(8,128)(2,1)} %constant.35.clone.sketch_high) | copy-start | bytes 786436
  5.5 11.7 %all-to-all-start = ((f32[16,4,128]{2,1,0:T(4,128)}), f32[16,4,128]{2,1,0:T(4,128)S(1)}, u32[]{:S(2)}, u32[]{:S(2)}) async-start(f32[16,4,128]{2,1,0:T(4,128)} %spectrum.1), calls=%async_computation | async-start | bytes 65536 | tf_op jit(solution)/shard_map/all_to_all | solution.py:606
  10.6 6.6 %copy-start = (bf16[256,512]{1,0:T(8,128)(2,1)S(1)}, bf16[256,512]{1,0:T(8,128)(2,1)}, u32[]{:S(2)}) copy-start(bf16[256,512]{1,0:T(8,128)(2,1)} %constant.42.clone.back_low) | copy-start | bytes 786436
  10.6 6.6 %copy-start.1 = (bf16[256,512]{1,0:T(8,128)(2,1)S(1)}, bf16[256,512]{1,0:T(8,128)(2,1)}, u32[]{:S(2)}) copy-start(bf16[256,512]{1,0:T(8,128)(2,1)} %constant.41.clone.back_high) | copy-start | bytes 786436
  10.7 6.6 %copy-start.2 = (bf16[512,256]{1,0:T(8,128)(2,1)S(1)}, bf16[512,256]{1,0:T(8,128)(2,1)}, u32[]{:S(2)}) copy-start(bf16[512,256]{1,0:T(8,128)(2,1)} %constant.36.clone.sketch_low) | copy-start | bytes 786436
  10.7 1.0 %copy-start.11 = (bf16[128,512]{1,0:T(8,128)(2,1)S(1)}, bf16[128,512]{1,0:T(8,128)(2,1)}, u32[]{:S(2)}) copy-start(bf16[128,512]{1,0:T(8,128)(2,1)} %constant.31.clone.refs_2_) | copy-start | bytes 393220
  11.7 0.8 %copy-start.13 = (f32[16,810]{1,0:T(8,128)S(1)}, f32[16,810]{1,0:T(8,128)}, u32[]{:S(2)}) copy-start(f32[16,810]{1,0:T(8,128)} %refs_0_.1) | copy-start | bytes 155524
  12.5 4.8 %copy-start.14 = (f32[16,256]{1,0:T(8,128)S(1)}, f32[16,256]{1,0:T(8,128)}, u32[]{:S(2)}) copy-start(f32[16,256]{1,0:T(8,128)} %constant.43.clone.weight_ref) | copy-start | bytes 49156
  17.2 10.9 %copy-start.12 = (bf16[48,1024]{1,0:T(8,128)(2,1)S(1)}, bf16[48,1024]{1,0:T(8,128)(2,1)}, u32[]{:S(2)}) copy-start(bf16[48,1024]{1,0:T(8,128)(2,1)} %constant.44.clone.refs_4_) | copy-start | bytes 294916
  20.9 1.2 %collective-permute-start.1 = (f32[4,4,128]{2,1,0:T(4,128)S(1)}, f32[4,4,128]{2,1,0:T(4,128)S(1)}, u32[]{:S(2)}, u32[]{:S(2)}) collective-permute-start(f32[4,4,128]{2,1,0:T(4,128)S(1)} %get-tuple-element.8), channel_id=1, source_target_pairs={{0,2},{2,0},{4,6},{6,4},{8,10},{10,8},{12,14},{14,12},{1,3},{3,1},... | collective-permute-start | bytes 24584 | tf_op jit(solution)/shard_map/ppermute | solution.py:663
  22.1 5.4 %collective-permute-start.4 = (f32[2,4,128]{2,1,0:T(4,128)S(1)}, f32[2,4,128]{2,1,0:T(4,128)S(1)}, u32[]{:S(2)}, u32[]{:S(2)}) collective-permute-start(f32[2,4,128]{2,1,0:T(4,128)S(1)} %get-tuple-element.9), channel_id=1, source_target_pairs={{0,12},{2,14},{4,8},{6,10},{8,4},{10,6},{12,0},{14,2},{1,13},{3,15... | collective-permute-start | bytes 12296 | tf_op jit(solution)/shard_map/ppermute | solution.py:663
  22.9 4.7 %collective-permute-start.2 = (f32[2,4,128]{2,1,0:T(4,128)S(1)}, f32[2,4,128]{2,1,0:T(4,128)S(1)}, u32[]{:S(2)}, u32[]{:S(2)}) collective-permute-start(f32[2,4,128]{2,1,0:T(4,128)S(1)} %get-tuple-element.11), channel_id=1, source_target_pairs={{0,4},{2,6},{4,0},{6,2},{8,12},{10,14},{12,8},{14,10},{1,5},{3,7},... | collective-permute-start | bytes 12296 | tf_op jit(solution)/shard_map/ppermute | solution.py:663
  23.3 4.8 %collective-permute-start.3 = (f32[2,4,128]{2,1,0:T(4,128)S(1)}, f32[2,4,128]{2,1,0:T(4,128)S(1)}, u32[]{:S(2)}, u32[]{:S(2)}) collective-permute-start(f32[2,4,128]{2,1,0:T(4,128)S(1)} %get-tuple-element.12), channel_id=1, source_target_pairs={{0,8},{2,10},{4,12},{6,14},{8,0},{10,2},{12,4},{14,6},{1,9},{3,11}... | collective-permute-start | bytes 12296 | tf_op jit(solution)/shard_map/ppermute | solution.py:663

commit v5 on v4

--- a/solution.py
+++ b/solution.py
@@ -60,8 +60,8 @@
     ).astype(np.float64)
 
 
-def spectrum_table(freq_total, copies):
-    angles = np.repeat(phases(freq_total), copies, 0)
+def spectrum_table(freq_total, owners):
+    angles = phases(freq_total)[owners]
     return np.concatenate([np.cos(angles), -np.sin(angles)], 0) / math.sqrt(S)
 
 
@@ -262,6 +262,7 @@
 
 def core_kernel(
     dims,
+    order,
     x_ref,
     omega_ref,
     analysis_high,
@@ -326,9 +327,10 @@
     for part in range(2):
         for piece in range(pieces):
             values = hats[part][:, piece * LANES : (piece + 1) * LANES]
-            xhat[:, part * pieces + piece] = jnp.broadcast_to(
-                values[:, None, :], (planes, 8, LANES)
-            )
+            for p in range(planes):
+                xhat[order[p], part * pieces + piece] = jnp.broadcast_to(
+                    values[p : p + 1], (8, LANES)
+                )
 
     def load_x(g1, g2, piece):
         row = g2 * first + g1
@@ -589,7 +591,8 @@
         ring = [(i, (i + step) % narrow_count) for i in range(narrow_count)]
         omegas.append(lax.ppermute(omega, "narrow", ring))
 
-    high, low = halves(spectrum_table(freq_total, narrow_count))
+    order = [(3 * dests // 4 - 1 - i) % dests for i in range(dests)]
+    high, low = halves(spectrum_table(freq_total, [i // narrow_count for i in order]))
     blocks = pl.pallas_call(
         spectrum_kernel,
         out_shape=jax.ShapeDtypeStruct((dests, lines, LANES), jnp.float32),
@@ -603,7 +606,14 @@
         ],
         name="spectrum",
     )(traces.reshape(CELLS, S), mask.reshape(1, CELLS), np.concatenate([high, low], 0))
-    grid = lax.all_to_all(blocks, ("wide", "narrow"), split_axis=0, concat_axis=0, tiled=True)
+    grid = lax.all_to_all(
+        blocks,
+        ("wide", "narrow"),
+        split_axis=0,
+        concat_axis=0,
+        axis_index_groups=[order],
+        tiled=True,
+    )
 
     if omega.shape[0] % 8:
         omegas = [jnp.concatenate(omegas, 0)]
@@ -650,7 +660,7 @@
     ]
     chips = second // 2
     kept, handed = pl.pallas_call(
-        functools.partial(core_kernel, (first, second, rank)),
+        functools.partial(core_kernel, (first, second, rank), order),
         out_shape=[jax.ShapeDtypeStruct((chips, lines, LANES), jnp.float32)] * 2,
         in_specs=[VMEM] * (2 + len(tables)),
         out_specs=[VMEM] * 2,

time: 29.6 us -> 28.5 us (0.963)
  waiting for transfers between devices: 6.86 us -> 4.69 us
  starting transfers between devices: 12.7 us -> 13.6 us
    all_to_all x1, waiting for transfers between devices: 4.21 us -> 1.14 us  [per_device(): lax.all_to_all(blocks, ('wide', 'narrow'), split_axis=0, concat_axis=0, a...]
    all_to_all x1, starting transfers between devices: 5.13 us -> 6.22 us  [per_device(): lax.all_to_all(blocks, ('wide', 'narrow'), split_axis=0, concat_axis=0, a...]
    ppermute x4, waiting for transfers between devices: 2.64 us -> 3.55 us  [across(): return lax.ppermute(value, 'wide', [(i, i ^ offset) for i in range(second)])]
  transfers between devices with their start and end apart: 6 -> 6, of which waited for: 4 -> 5; matrix products, arithmetic and copies ran while one was open for 0% -> 0% of each run, Pallas kernels for 10% -> 10%
where the time goes in v5:
time: 28.5 us; the launch traced here: 28.2 us
  starting transfers between devices  13.6 us (48%)
  Pallas kernels  7.8 us (27%)
  waiting for transfers between devices  4.69 us (16%)
  local copies, waits for them, and re-layouts  1.85 us (6%)
    all_to_all x1, starting transfers between devices, per_device(): lax.all_to_all(blocks, ('wide', 'narrow'), split_axis=0, concat_axis=0, a...  6.22 us
    ppermute x4, starting transfers between devices, across(): return lax.ppermute(value, 'wide', [(i, i ^ offset) for i in range(second)])  4.46 us
    pallas_call x1, Pallas kernels, per_device(): pl.pallas_call(functools.partial(core_kernel, (first, second, rank), orde...  3.62 us
    ppermute x4, waiting for transfers between devices, across(): return lax.ppermute(value, 'wide', [(i, i ^ offset) for i in range(second)])  3.55 us
    ppermute x1, starting transfers between devices, per_device(): omegas.append(lax.ppermute(omega, 'narrow', ring))  2.97 us
    pallas_call x1, Pallas kernels, per_device(): pl.pallas_call(spectrum_kernel, out_shape=jax.ShapeDtypeStruct((dests, li...  2.46 us
    unnamed x30, local copies, waits for them, and re-layouts  1.85 us
    pallas_call x1, Pallas kernels, per_device(): pl.pallas_call(synthesis_kernel, out_shape=jax.ShapeDtypeStruct((CELLS, S...  1.27 us
  transfers between devices with their start and end apart: 6, of which 5 were waited for; matrix products, arithmetic and copies ran while one was open for 0% of the time, Pallas kernels for 10%

profile of v5, /device:TPU:0, one launch (start us, length us, event | category | flops | bytes accessed | tf_op | source)
XLA Modules:
  0.0 28.2 jit_solution(2391207648507519558)
XLA Ops:
  0.0 3.0 %collective-permute-start = (f32[16,810]{1,0:T(8,128)}, f32[16,810]{1,0:T(8,128)S(1)}, u32[]{:S(2)}, u32[]{:S(2)}) collective-permute-start(f32[16,810]{1,0:T(8,128)} %refs_0_.1), channel_id=1, source_target_pairs={{0,1},{1,0},{2,3},{3,2},{4,5},{5,4},{6,7},{7,6},{8,9},{9,8},{10,11... | collective-permute-start | bytes 155528 | tf_op jit(solution)/shard_map/ppermute | solution.py:592
  3.0 0.0 copy-start.7
  3.0 0.0 copy-start.8
  3.0 0.0 copy-start.9
  3.0 2.5 %spectrum.1 = f32[16,4,128]{2,1,0:T(4,128)} custom-call(f32[256,1024]{1,0:T(8,128)} %bitcast.14, s32[1,256]{1,0:T(1,128)} %bitcast.16, bf16[64,1024]{1,0:T(8,128)(2,1)} %constant.30.clone.table_ref), custom_call_target="tpu_custom_call" | custom-call | tf_op jit(solution)/shard_map/spectrum/pallas_call | solution.py:596
  5.5 0.0 copy-start.3
  5.5 6.2 %all-to-all-start = ((f32[16,4,128]{2,1,0:T(4,128)}), f32[16,4,128]{2,1,0:T(4,128)S(1)}, u32[]{:S(2)}, u32[]{:S(2)}) async-start(f32[16,4,128]{2,1,0:T(4,128)} %spectrum.1), calls=%async_computation | async-start | bytes 65536 | tf_op jit(solution)/shard_map/all_to_all | solution.py:609
  11.7 0.0 copy-start.1
  11.7 0.0 copy-start.2
  11.7 0.0 collective-permute-done.refs_1_
  11.8 0.0 copy-done.10
  11.8 0.0 copy-start.11
  11.8 1.0 %copy-done.11 = bf16[128,512]{1,0:T(8,128)(2,1)S(1)} copy-done((bf16[128,512]{1,0:T(8,128)(2,1)S(1)}, bf16[128,512]{1,0:T(8,128)(2,1)}, u32[]{:S(2)}) %copy-start.11) | copy-done | bytes 131096
  12.7 0.8 %copy-done.13 = f32[16,810]{1,0:T(8,128)S(1)} copy-done((f32[16,810]{1,0:T(8,128)S(1)}, f32[16,810]{1,0:T(8,128)}, u32[]{:S(2)}) %copy-start.13) | copy-done | bytes 51864
  13.6 0.5 %omega.1.omega_ref = f32[320,512]{1,0:T(8,128)S(1)} custom-call(f32[16,810]{1,0:T(8,128)S(1)} %copy-done.13, f32[16,810]{1,0:T(8,128)S(1)} %collective-permute-done.refs_1_, bf16[128,512]{1,0:T(8,128)(2,1)S(1)} %copy-done.11, bf16[128,512]{1,0:T(8,128)(2,1)S(1)} %copy-done.10), custom_call_target="tpu_custom_call" | custom-call | flops 125829120 | bytes 655360 | tf_op jit(solution)/shard_map/omega/pallas_call | solution.py:621
  14.0 1.1 %all-to-all-done.x_ref = f32[16,4,128]{2,1,0:T(4,128)S(1)} async-done(((f32[16,4,128]{2,1,0:T(4,128)}), f32[16,4,128]{2,1,0:T(4,128)S(1)}, u32[]{:S(2)}, u32[]{:S(2)}) %all-to-all-start) | async-done | bytes 32800 | tf_op jit(solution)/shard_map/all_to_all | solution.py:609
  15.2 0.0 copy-done.4
  15.2 0.0 copy-done.5
  15.2 0.0 copy-done.6
  15.2 0.0 copy-done.7
  15.2 0.0 copy-done.8
  15.3 0.0 copy-start.12
  15.3 3.6 %core.1 = (f32[4,4,128]{2,1,0:T(4,128)S(1)}, f32[4,4,128]{2,1,0:T(4,128)S(1)}) custom-call(f32[16,4,128]{2,1,0:T(4,128)S(1)} %all-to-all-done.x_ref, f32[320,512]{1,0:T(8,128)S(1)} %omega.1.omega_ref, bf16[256,512]{1,0:T(8,128)(2,1)S(1)} %copy-done.5, bf16[256,512]{1,0:T(8,128)(2,1)S(1)} %copy-done.4, bf16[512,256]{1,0:T(8,128)(2,1)S(1)} %copy-done.3, ...), custom_call_target="tpu_custom_call" | custom-call | tf_op jit(solution)/shard_map/core/pallas_call | solution.py:662
  18.9 0.1 collective-permute-start.1
  19.0 1.2 %collective-permute-done.1 = f32[4,4,128]{2,1,0:T(4,128)S(1)} collective-permute-done((f32[4,4,128]{2,1,0:T(4,128)S(1)}, f32[4,4,128]{2,1,0:T(4,128)S(1)}, u32[]{:S(2)}, u32[]{:S(2)}) %collective-permute-start.1) | collective-permute-done | bytes 8224 | tf_op jit(solution)/shard_map/ppermute | solution.py:673
  20.1 2.3 %collective-permute-start.4 = (f32[2,4,128]{2,1,0:T(4,128)S(1)}, f32[2,4,128]{2,1,0:T(4,128)S(1)}, u32[]{:S(2)}, u32[]{:S(2)}) collective-permute-start(f32[2,4,128]{2,1,0:T(4,128)S(1)} %get-tuple-element.9), channel_id=1, source_target_pairs={{0,12},{2,14},{4,8},{6,10},{8,4},{10,6},{12,0},{14,2},{1,13},{3,15... | collective-permute-start | bytes 12296 | tf_op jit(solution)/shard_map/ppermute | solution.py:673
  22.4 0.0 collective-permute-start.2
  22.4 2.1 %collective-permute-start.3 = (f32[2,4,128]{2,1,0:T(4,128)S(1)}, f32[2,4,128]{2,1,0:T(4,128)S(1)}, u32[]{:S(2)}, u32[]{:S(2)}) collective-permute-start(f32[2,4,128]{2,1,0:T(4,128)S(1)} %get-tuple-element.12), channel_id=1, source_target_pairs={{0,8},{2,10},{4,12},{6,14},{8,0},{10,2},{12,4},{14,6},{1,9},{3,11}... | collective-permute-start | bytes 12296 | tf_op jit(solution)/shard_map/ppermute | solution.py:673
  24.5 1.0 %collective-permute-done.4.refs_3_ = f32[2,4,128]{2,1,0:T(4,128)S(1)} collective-permute-done((f32[2,4,128]{2,1,0:T(4,128)S(1)}, f32[2,4,128]{2,1,0:T(4,128)S(1)}, u32[]{:S(2)}, u32[]{:S(2)}) %collective-permute-start.4) | collective-permute-done | bytes 4128 | tf_op jit(solution)/shard_map/ppermute | solution.py:673
  25.5 0.5 %collective-permute-done.2.refs_1_ = f32[2,4,128]{2,1,0:T(4,128)S(1)} collective-permute-done((f32[2,4,128]{2,1,0:T(4,128)S(1)}, f32[2,4,128]{2,1,0:T(4,128)S(1)}, u32[]{:S(2)}, u32[]{:S(2)}) %collective-permute-start.2) | collective-permute-done | bytes 4128 | tf_op jit(solution)/shard_map/ppermute | solution.py:673
  26.0 0.9 %collective-permute-done.3.refs_2_ = f32[2,4,128]{2,1,0:T(4,128)S(1)} collective-permute-done((f32[2,4,128]{2,1,0:T(4,128)S(1)}, f32[2,4,128]{2,1,0:T(4,128)S(1)}, u32[]{:S(2)}, u32[]{:S(2)}) %collective-permute-start.3) | collective-permute-done | bytes 4128 | tf_op jit(solution)/shard_map/ppermute | solution.py:673
  26.9 1.3 %synthesis.1 = f32[256,1024]{1,0:T(8,128)} custom-call(f32[2,4,128]{2,1,0:T(4,128)S(1)} %get-tuple-element.10.refs_0_, f32[2,4,128]{2,1,0:T(4,128)S(1)} %collective-permute-done.2.refs_1_, f32[2,4,128]{2,1,0:T(4,128)S(1)} %collective-permute-done.3.refs_2_, f32[2,4,128]{2,1,0:T(4,128)S(1)} %collective-permute-done.4.refs_3_, bf16[48,1024]{1,0:T(8,128)(2,1)S(1)} %copy-done.12), custom_call_target="tpu_custom_call" | custom-call | tf_op jit(solution)/shard_map/synthesis/pallas_call | solution.py:680
  (15 shorter events, 0.0 us)
Async XLA Ops:
  0.0 11.8 %collective-permute-start = (f32[16,810]{1,0:T(8,128)}, f32[16,810]{1,0:T(8,128)S(1)}, u32[]{:S(2)}, u32[]{:S(2)}) collective-permute-start(f32[16,810]{1,0:T(8,128)} %refs_0_.1), channel_id=1, source_target_pairs={{0,1},{1,0},{2,3},{3,2},{4,5},{5,4},{6,7},{7,6},{8,9},{9,8},{10,11... | collective-permute-start | bytes 155528 | tf_op jit(solution)/shard_map/ppermute | solution.py:592
  3.0 8.8 %copy-start.10 = (bf16[128,512]{1,0:T(8,128)(2,1)S(1)}, bf16[128,512]{1,0:T(8,128)(2,1)}, u32[]{:S(2)}) copy-start(bf16[128,512]{1,0:T(8,128)(2,1)} %constant.32.clone.refs_3_) | copy-start | bytes 393220
  3.0 12.2 %copy-start.4 = (bf16[256,512]{1,0:T(8,128)(2,1)S(1)}, bf16[256,512]{1,0:T(8,128)(2,1)}, u32[]{:S(2)}) copy-start(bf16[256,512]{1,0:T(8,128)(2,1)} %constant.34.clone.analysis_low) | copy-start | bytes 786436
  3.0 12.2 %copy-start.5 = (bf16[256,512]{1,0:T(8,128)(2,1)S(1)}, bf16[256,512]{1,0:T(8,128)(2,1)}, u32[]{:S(2)}) copy-start(bf16[256,512]{1,0:T(8,128)(2,1)} %constant.33.clone.analysis_high) | copy-start | bytes 786436
  3.0 12.2 %copy-start.6 = (bf16[256,256]{1,0:T(8,128)(2,1)S(1)}, bf16[256,256]{1,0:T(8,128)(2,1)}, u32[]{:S(2)}) copy-start(bf16[256,256]{1,0:T(8,128)(2,1)} %constant.40.clone.window_low) | copy-start | bytes 393220
  3.0 12.2 %copy-start.7 = (bf16[256,256]{1,0:T(8,128)(2,1)S(1)}, bf16[256,256]{1,0:T(8,128)(2,1)}, u32[]{:S(2)}) copy-start(bf16[256,256]{1,0:T(8,128)(2,1)} %constant.39.clone.window_high) | copy-start | bytes 393220
  3.0 12.2 %copy-start.8 = (bf16[128,512]{1,0:T(8,128)(2,1)S(1)}, bf16[128,512]{1,0:T(8,128)(2,1)}, u32[]{:S(2)}) copy-start(bf16[128,512]{1,0:T(8,128)(2,1)} %constant.38.clone.basis_low) | copy-start | bytes 393220
  3.0 12.2 %copy-start.9 = (bf16[128,512]{1,0:T(8,128)(2,1)S(1)}, bf16[128,512]{1,0:T(8,128)(2,1)}, u32[]{:S(2)}) copy-start(bf16[128,512]{1,0:T(8,128)(2,1)} %constant.37.clone.basis_high) | copy-start | bytes 393220
  5.5 9.7 %copy-start.3 = (bf16[512,256]{1,0:T(8,128)(2,1)S(1)}, bf16[512,256]{1,0:T(8,128)(2,1)}, u32[]{:S(2)}) copy-start(bf16[512,256]{1,0:T(8,128)(2,1)} %constant.35.clone.sketch_high) | copy-start | bytes 786436
  5.5 9.7 %all-to-all-start = ((f32[16,4,128]{2,1,0:T(4,128)}), f32[16,4,128]{2,1,0:T(4,128)S(1)}, u32[]{:S(2)}, u32[]{:S(2)}) async-start(f32[16,4,128]{2,1,0:T(4,128)} %spectrum.1), calls=%async_computation | async-start | bytes 65536 | tf_op jit(solution)/shard_map/all_to_all | solution.py:609
  11.7 3.5 %copy-start = (bf16[256,512]{1,0:T(8,128)(2,1)S(1)}, bf16[256,512]{1,0:T(8,128)(2,1)}, u32[]{:S(2)}) copy-start(bf16[256,512]{1,0:T(8,128)(2,1)} %constant.42.clone.back_low) | copy-start | bytes 786436
  11.7 3.5 %copy-start.1 = (bf16[256,512]{1,0:T(8,128)(2,1)S(1)}, bf16[256,512]{1,0:T(8,128)(2,1)}, u32[]{:S(2)}) copy-start(bf16[256,512]{1,0:T(8,128)(2,1)} %constant.41.clone.back_high) | copy-start | bytes 786436
  11.7 3.5 %copy-start.2 = (bf16[512,256]{1,0:T(8,128)(2,1)S(1)}, bf16[512,256]{1,0:T(8,128)(2,1)}, u32[]{:S(2)}) copy-start(bf16[512,256]{1,0:T(8,128)(2,1)} %constant.36.clone.sketch_low) | copy-start | bytes 786436
  11.8 1.0 %copy-start.11 = (bf16[128,512]{1,0:T(8,128)(2,1)S(1)}, bf16[128,512]{1,0:T(8,128)(2,1)}, u32[]{:S(2)}) copy-start(bf16[128,512]{1,0:T(8,128)(2,1)} %constant.31.clone.refs_2_) | copy-start | bytes 393220
  12.7 0.8 %copy-start.13 = (f32[16,810]{1,0:T(8,128)S(1)}, f32[16,810]{1,0:T(8,128)}, u32[]{:S(2)}) copy-start(f32[16,810]{1,0:T(8,128)} %refs_0_.1) | copy-start | bytes 155524
  13.6 1.7 %copy-start.14 = (f32[16,256]{1,0:T(8,128)S(1)}, f32[16,256]{1,0:T(8,128)}, u32[]{:S(2)}) copy-start(f32[16,256]{1,0:T(8,128)} %constant.43.clone.weight_ref) | copy-start | bytes 49156
  15.3 11.7 %copy-start.12 = (bf16[48,1024]{1,0:T(8,128)(2,1)S(1)}, bf16[48,1024]{1,0:T(8,128)(2,1)}, u32[]{:S(2)}) copy-start(bf16[48,1024]{1,0:T(8,128)(2,1)} %constant.44.clone.refs_4_) | copy-start | bytes 294916
  18.9 1.2 %collective-permute-start.1 = (f32[4,4,128]{2,1,0:T(4,128)S(1)}, f32[4,4,128]{2,1,0:T(4,128)S(1)}, u32[]{:S(2)}, u32[]{:S(2)}) collective-permute-start(f32[4,4,128]{2,1,0:T(4,128)S(1)} %get-tuple-element.8), channel_id=1, source_target_pairs={{0,2},{2,0},{4,6},{6,4},{8,10},{10,8},{12,14},{14,12},{1,3},{3,1},... | collective-permute-start | bytes 24584 | tf_op jit(solution)/shard_map/ppermute | solution.py:673
  20.1 5.4 %collective-permute-start.4 = (f32[2,4,128]{2,1,0:T(4,128)S(1)}, f32[2,4,128]{2,1,0:T(4,128)S(1)}, u32[]{:S(2)}, u32[]{:S(2)}) collective-permute-start(f32[2,4,128]{2,1,0:T(4,128)S(1)} %get-tuple-element.9), channel_id=1, source_target_pairs={{0,12},{2,14},{4,8},{6,10},{8,4},{10,6},{12,0},{14,2},{1,13},{3,15... | collective-permute-start | bytes 12296 | tf_op jit(solution)/shard_map/ppermute | solution.py:673
  22.4 3.6 %collective-permute-start.2 = (f32[2,4,128]{2,1,0:T(4,128)S(1)}, f32[2,4,128]{2,1,0:T(4,128)S(1)}, u32[]{:S(2)}, u32[]{:S(2)}) collective-permute-start(f32[2,4,128]{2,1,0:T(4,128)S(1)} %get-tuple-element.11), channel_id=1, source_target_pairs={{0,4},{2,6},{4,0},{6,2},{8,12},{10,14},{12,8},{14,10},{1,5},{3,7},... | collective-permute-start | bytes 12296 | tf_op jit(solution)/shard_map/ppermute | solution.py:673
  22.4 4.5 %collective-permute-start.3 = (f32[2,4,128]{2,1,0:T(4,128)S(1)}, f32[2,4,128]{2,1,0:T(4,128)S(1)}, u32[]{:S(2)}, u32[]{:S(2)}) collective-permute-start(f32[2,4,128]{2,1,0:T(4,128)S(1)} %get-tuple-element.12), channel_id=1, source_target_pairs={{0,8},{2,10},{4,12},{6,14},{8,0},{10,2},{12,4},{14,6},{1,9},{3,11}... | collective-permute-start | bytes 12296 | tf_op jit(solution)/shard_map/ppermute | solution.py:673

commit v6 on v3

--- a/solution.py
+++ b/solution.py
@@ -60,13 +60,13 @@
     ).astype(np.float64)
 
 
-def spectrum_table(freq_total, copies):
-    angles = np.repeat(phases(freq_total), copies, 0)
+def spectrum_table(freq_total, owners):
+    angles = phases(freq_total)[owners]
     return np.concatenate([np.cos(angles), -np.sin(angles)], 0) / math.sqrt(S)
 
 
-def synthesis_table(freq_total):
-    angles = phases(freq_total)
+def synthesis_table(freq_total, order):
+    angles = phases(freq_total)[order]
     return np.concatenate([np.cos(angles), -np.sin(angles)], 0) * math.sqrt(2.0 / freq_total)
 
 
@@ -262,6 +262,8 @@
 
 def core_kernel(
     dims,
+    order,
+    back_order,
     x_ref,
     omega_ref,
     analysis_high,
@@ -324,9 +326,10 @@
     for part in range(2):
         for piece in range(pieces):
             values = hats[part][:, piece * LANES : (piece + 1) * LANES]
-            xhat[:, part * pieces + piece] = jnp.broadcast_to(
-                values[:, None, :], (planes, 8, LANES)
-            )
+            for p in range(planes):
+                xhat[order[p], part * pieces + piece] = jnp.broadcast_to(
+                    values[p : p + 1], (8, LANES)
+                )
 
     def load_x(g1, g2, piece):
         row = g2 * first + g1
@@ -528,9 +531,12 @@
     weight = weight_ref[pl.ds(pl.multiple_of(own * second, 8), second), :]
     real = real * weight
     imag = imag * weight
-    for piece in range(pieces):
-        out_ref[:, piece, :] = real[:, piece * LANES : (piece + 1) * LANES]
-        out_ref[:, pieces + piece, :] = imag[:, piece * LANES : (piece + 1) * LANES]
+    for j in range(second):
+        row = slice(back_order[j], back_order[j] + 1)
+        for piece in range(pieces):
+            place = slice(piece * LANES, (piece + 1) * LANES)
+            out_ref[j, pl.ds(piece, 1), :] = real[row, place]
+            out_ref[j, pl.ds(pieces + piece, 1), :] = imag[row, place]
 
 
 def synthesis_kernel(cells_ref, table_ref, out_ref, out, sems):
@@ -558,6 +564,10 @@
         copy.wait()
 
 
+def group_order(count):
+    return [(3 * count // 4 - 1 - i) % count for i in range(count)]
+
+
 def per_device(traces, mask, omega):
     narrow_count = lax.axis_size("narrow")
     wide_count = lax.axis_size("wide")
@@ -575,7 +585,8 @@
         ring = [(i, (i + step) % narrow_count) for i in range(narrow_count)]
         omegas.append(lax.ppermute(omega, "narrow", ring))
 
-    high, low = halves(spectrum_table(freq_total, narrow_count))
+    order = group_order(dests)
+    high, low = halves(spectrum_table(freq_total, [i // narrow_count for i in order]))
     blocks = pl.pallas_call(
         spectrum_kernel,
         out_shape=jax.ShapeDtypeStruct((dests, lines, LANES), jnp.float32),
@@ -589,7 +600,14 @@
         ],
         name="spectrum",
     )(traces.reshape(CELLS, S), mask.reshape(1, CELLS), np.concatenate([high, low], 0))
-    grid = lax.all_to_all(blocks, ("wide", "narrow"), split_axis=0, concat_axis=0, tiled=True)
+    grid = lax.all_to_all(
+        blocks,
+        ("wide", "narrow"),
+        split_axis=0,
+        concat_axis=0,
+        axis_index_groups=[order],
+        tiled=True,
+    )
 
     if omega.shape[0] % 8:
         omegas = [jnp.concatenate(omegas, 0)]
@@ -633,8 +651,9 @@
         (2 * span2 * rank, CELLS),
         (2 * second, CELLS),
     ]
+    back_order = group_order(second)
     rebuilt = pl.pallas_call(
-        functools.partial(core_kernel, (first, second, rank)),
+        functools.partial(core_kernel, (first, second, rank), order, back_order),
         out_shape=jax.ShapeDtypeStruct((second, lines, LANES), jnp.float32),
         in_specs=[VMEM] * (2 + len(tables)),
         out_specs=VMEM,
@@ -642,9 +661,16 @@
         compiler_params=pltpu.CompilerParams(vmem_limit_bytes=24 * MIB),
         name="core",
     )(grid, omega_hat, *tables)
-    returned = lax.all_to_all(rebuilt, "wide", split_axis=0, concat_axis=0, tiled=True)
-
-    high, low = halves(synthesis_table(freq_total))
+    returned = lax.all_to_all(
+        rebuilt,
+        "wide",
+        split_axis=0,
+        concat_axis=0,
+        axis_index_groups=[back_order],
+        tiled=True,
+    )
+
+    high, low = halves(synthesis_table(freq_total, back_order))
     filtered = pl.pallas_call(
         synthesis_kernel,
         out_shape=jax.ShapeDtypeStruct((CELLS, S), jnp.float32),

time: 30.4 us -> 27.4 us (0.901)
  waiting for transfers between devices: 4.21 us -> 1.14 us
  starting transfers between devices: 8.09 us -> 9.19 us
  blocking collectives: 8.02 us -> 7.01 us
    all_to_all x1, waiting for transfers between devices: 4.21 us -> 1.14 us  [per_device(): lax.all_to_all(blocks, ('wide', 'narrow'), split_axis=0, concat_axis=0, a...]
    all_to_all x1, starting transfers between devices: 5.13 us -> 6.22 us  [per_device(): lax.all_to_all(blocks, ('wide', 'narrow'), split_axis=0, concat_axis=0, a...]
    all_to_all x1, blocking collectives: 8.02 us -> 7.01 us  [per_device(): lax.all_to_all(rebuilt, 'wide', split_axis=0, concat_axis=0, axis_index_g...]
  transfers between devices with their start and end apart: 2 -> 2, of which waited for: 1 -> 1; matrix products, arithmetic and copies ran while one was open for 0% -> 0% of each run, Pallas kernels for 10% -> 11%
where the time goes in v6:
time: 27.4 us; the launch traced here: 27.1 us
  starting transfers between devices  9.19 us (34%)
  Pallas kernels  7.72 us (28%)
  blocking collectives  7.01 us (26%)
  local copies, waits for them, and re-layouts  1.85 us (7%)
  waiting for transfers between devices  1.14 us (4%)
    all_to_all x1, blocking collectives, per_device(): lax.all_to_all(rebuilt, 'wide', split_axis=0, concat_axis=0, axis_index_g...  7.01 us
    all_to_all x1, starting transfers between devices, per_device(): lax.all_to_all(blocks, ('wide', 'narrow'), split_axis=0, concat_axis=0, a...  6.22 us
    pallas_call x1, Pallas kernels, per_device(): pl.pallas_call(functools.partial(core_kernel, (first, second, rank), orde...  3.57 us
    ppermute x1, starting transfers between devices, per_device(): omegas.append(lax.ppermute(omega, 'narrow', ring))  2.97 us
    pallas_call x1, Pallas kernels, per_device(): pl.pallas_call(spectrum_kernel, out_shape=jax.ShapeDtypeStruct((dests, li...  2.46 us
    unnamed x30, local copies, waits for them, and re-layouts  1.85 us
    pallas_call x1, Pallas kernels, per_device(): pl.pallas_call(synthesis_kernel, out_shape=jax.ShapeDtypeStruct((CELLS, S...  1.24 us
    all_to_all x1, waiting for transfers between devices, per_device(): lax.all_to_all(blocks, ('wide', 'narrow'), split_axis=0, concat_axis=0, a...  1.14 us
  transfers between devices with their start and end apart: 2, of which 1 were waited for; matrix products, arithmetic and copies ran while one was open for 0% of the time, Pallas kernels for 11%

profile of v6, /device:TPU:0, one launch (start us, length us, event | category | flops | bytes accessed | tf_op | source)
XLA Modules:
  0.0 27.1 jit_solution(11823739056611999572)
XLA Ops:
  0.0 3.0 %collective-permute-start = (f32[16,810]{1,0:T(8,128)}, f32[16,810]{1,0:T(8,128)S(1)}, u32[]{:S(2)}, u32[]{:S(2)}) collective-permute-start(f32[16,810]{1,0:T(8,128)} %refs_0_.1), channel_id=1, source_target_pairs={{0,1},{1,0},{2,3},{3,2},{4,5},{5,4},{6,7},{7,6},{8,9},{9,8},{10,11... | collective-permute-start | bytes 155528 | tf_op jit(solution)/shard_map/ppermute | solution.py:586
  3.0 0.0 copy-start.7
  3.0 0.0 copy-start.8
  3.0 0.0 copy-start.9
  3.0 2.5 %spectrum.1 = f32[16,4,128]{2,1,0:T(4,128)} custom-call(f32[256,1024]{1,0:T(8,128)} %bitcast.3, s32[1,256]{1,0:T(1,128)} %bitcast.4, bf16[64,1024]{1,0:T(8,128)(2,1)} %constant.30.clone.table_ref), custom_call_target="tpu_custom_call" | custom-call | tf_op jit(solution)/shard_map/spectrum/pallas_call | solution.py:590
  5.5 0.0 copy-start.3
  5.5 6.2 %all-to-all-start = ((f32[16,4,128]{2,1,0:T(4,128)}), f32[16,4,128]{2,1,0:T(4,128)S(1)}, u32[]{:S(2)}, u32[]{:S(2)}) async-start(f32[16,4,128]{2,1,0:T(4,128)} %spectrum.1), calls=%async_computation | async-start | bytes 65536 | tf_op jit(solution)/shard_map/all_to_all | solution.py:603
  11.7 0.0 copy-start.1
  11.7 0.0 copy-start.2
  11.7 0.0 collective-permute-done.refs_1_
  11.8 0.0 copy-done.10
  11.8 0.0 copy-start.11
  11.8 1.0 %copy-done.11 = bf16[128,512]{1,0:T(8,128)(2,1)S(1)} copy-done((bf16[128,512]{1,0:T(8,128)(2,1)S(1)}, bf16[128,512]{1,0:T(8,128)(2,1)}, u32[]{:S(2)}) %copy-start.11) | copy-done | bytes 131096
  12.7 0.8 %copy-done.13 = f32[16,810]{1,0:T(8,128)S(1)} copy-done((f32[16,810]{1,0:T(8,128)S(1)}, f32[16,810]{1,0:T(8,128)}, u32[]{:S(2)}) %copy-start.13) | copy-done | bytes 51864
  13.6 0.5 %omega.1.omega_ref = f32[320,512]{1,0:T(8,128)S(1)} custom-call(f32[16,810]{1,0:T(8,128)S(1)} %copy-done.13, f32[16,810]{1,0:T(8,128)S(1)} %collective-permute-done.refs_1_, bf16[128,512]{1,0:T(8,128)(2,1)S(1)} %copy-done.11, bf16[128,512]{1,0:T(8,128)(2,1)S(1)} %copy-done.10), custom_call_target="tpu_custom_call" | custom-call | flops 125829120 | bytes 655360 | tf_op jit(solution)/shard_map/omega/pallas_call | solution.py:615
  14.0 1.1 %all-to-all-done.x_ref = f32[16,4,128]{2,1,0:T(4,128)S(1)} async-done(((f32[16,4,128]{2,1,0:T(4,128)}), f32[16,4,128]{2,1,0:T(4,128)S(1)}, u32[]{:S(2)}, u32[]{:S(2)}) %all-to-all-start) | async-done | bytes 32800 | tf_op jit(solution)/shard_map/all_to_all | solution.py:603
  15.2 0.0 copy-done.4
  15.2 0.0 copy-done.5
  15.2 0.0 copy-done.6
  15.2 0.0 copy-done.7
  15.2 0.0 copy-done.8
  15.2 0.0 copy-done.9
  15.2 0.0 copy-done.3
  15.2 0.0 copy-done
  15.2 0.0 copy-done.1
  15.2 0.0 copy-done.2
  15.2 0.0 copy-done.14
  15.3 0.0 copy-start.12
  15.3 3.6 %core.1 = f32[8,4,128]{2,1,0:T(4,128)S(1)} custom-call(f32[16,4,128]{2,1,0:T(4,128)S(1)} %all-to-all-done.x_ref, f32[320,512]{1,0:T(8,128)S(1)} %omega.1.omega_ref, bf16[256,512]{1,0:T(8,128)(2,1)S(1)} %copy-done.5, bf16[256,512]{1,0:T(8,128)(2,1)S(1)} %copy-done.4, bf16[512,256]{1,0:T(8,128)(2,1)S(1)} %copy-done.3, bf16[512,256]{1,0:T(8,128)(2,1)S(1)} %copy-done.2, ...), custom_call_target="tpu_custom_call" | custom-call | tf_op jit(solution)/shard_map/core/pallas_call | solution.py:655
  18.8 7.0 %all_to_all.10.cells_ref = f32[8,4,128]{2,1,0:T(4,128)S(1)} all-to-all(f32[8,4,128]{2,1,0:T(4,128)S(1)} %core.1), channel_id=1, replica_groups={{10,8,6,4,2,0,14,12},{11,9,7,5,3,1,15,13},{26,24,22,20,18,16,30,28},{27..., dimensions={0} | all-to-all | bytes 32768 | tf_op jit(solution)/shard_map/all_to_all | solution.py:664
  25.8 0.0 copy-done.12
  25.8 1.2 %synthesis.1 = f32[256,1024]{1,0:T(8,128)} custom-call(f32[8,4,128]{2,1,0:T(4,128)S(1)} %all_to_all.10.cells_ref, bf16[48,1024]{1,0:T(8,128)(2,1)S(1)} %copy-done.12), custom_call_target="tpu_custom_call" | custom-call | tf_op jit(solution)/shard_map/synthesis/pallas_call | solution.py:674
  (7 shorter events, 0.0 us)
Async XLA Ops:
  0.0 11.8 %collective-permute-start = (f32[16,810]{1,0:T(8,128)}, f32[16,810]{1,0:T(8,128)S(1)}, u32[]{:S(2)}, u32[]{:S(2)}) collective-permute-start(f32[16,810]{1,0:T(8,128)} %refs_0_.1), channel_id=1, source_target_pairs={{0,1},{1,0},{2,3},{3,2},{4,5},{5,4},{6,7},{7,6},{8,9},{9,8},{10,11... | collective-permute-start | bytes 155528 | tf_op jit(solution)/shard_map/ppermute | solution.py:586
  3.0 8.8 %copy-start.10 = (bf16[128,512]{1,0:T(8,128)(2,1)S(1)}, bf16[128,512]{1,0:T(8,128)(2,1)}, u32[]{:S(2)}) copy-start(bf16[128,512]{1,0:T(8,128)(2,1)} %constant.32.clone.refs_3_) | copy-start | bytes 393220
  3.0 12.2 %copy-start.4 = (bf16[256,512]{1,0:T(8,128)(2,1)S(1)}, bf16[256,512]{1,0:T(8,128)(2,1)}, u32[]{:S(2)}) copy-start(bf16[256,512]{1,0:T(8,128)(2,1)} %constant.34.clone.analysis_low) | copy-start | bytes 786436
  3.0 12.2 %copy-start.5 = (bf16[256,512]{1,0:T(8,128)(2,1)S(1)}, bf16[256,512]{1,0:T(8,128)(2,1)}, u32[]{:S(2)}) copy-start(bf16[256,512]{1,0:T(8,128)(2,1)} %constant.33.clone.analysis_high) | copy-start | bytes 786436
  3.0 12.2 %copy-start.6 = (bf16[256,256]{1,0:T(8,128)(2,1)S(1)}, bf16[256,256]{1,0:T(8,128)(2,1)}, u32[]{:S(2)}) copy-start(bf16[256,256]{1,0:T(8,128)(2,1)} %constant.40.clone.window_low) | copy-start | bytes 393220
  3.0 12.2 %copy-start.7 = (bf16[256,256]{1,0:T(8,128)(2,1)S(1)}, bf16[256,256]{1,0:T(8,128)(2,1)}, u32[]{:S(2)}) copy-start(bf16[256,256]{1,0:T(8,128)(2,1)} %constant.39.clone.window_high) | copy-start | bytes 393220
  3.0 12.2 %copy-start.8 = (bf16[128,512]{1,0:T(8,128)(2,1)S(1)}, bf16[128,512]{1,0:T(8,128)(2,1)}, u32[]{:S(2)}) copy-start(bf16[128,512]{1,0:T(8,128)(2,1)} %constant.38.clone.basis_low) | copy-start | bytes 393220
  3.0 12.2 %copy-start.9 = (bf16[128,512]{1,0:T(8,128)(2,1)S(1)}, bf16[128,512]{1,0:T(8,128)(2,1)}, u32[]{:S(2)}) copy-start(bf16[128,512]{1,0:T(8,128)(2,1)} %constant.37.clone.basis_high) | copy-start | bytes 393220
  5.5 9.7 %copy-start.3 = (bf16[512,256]{1,0:T(8,128)(2,1)S(1)}, bf16[512,256]{1,0:T(8,128)(2,1)}, u32[]{:S(2)}) copy-start(bf16[512,256]{1,0:T(8,128)(2,1)} %constant.35.clone.sketch_high) | copy-start | bytes 786436
  5.5 9.7 %all-to-all-start = ((f32[16,4,128]{2,1,0:T(4,128)}), f32[16,4,128]{2,1,0:T(4,128)S(1)}, u32[]{:S(2)}, u32[]{:S(2)}) async-start(f32[16,4,128]{2,1,0:T(4,128)} %spectrum.1), calls=%async_computation | async-start | bytes 65536 | tf_op jit(solution)/shard_map/all_to_all | solution.py:603
  11.7 3.5 %copy-start = (bf16[256,512]{1,0:T(8,128)(2,1)S(1)}, bf16[256,512]{1,0:T(8,128)(2,1)}, u32[]{:S(2)}) copy-start(bf16[256,512]{1,0:T(8,128)(2,1)} %constant.42.clone.back_low) | copy-start | bytes 786436
  11.7 3.5 %copy-start.1 = (bf16[256,512]{1,0:T(8,128)(2,1)S(1)}, bf16[256,512]{1,0:T(8,128)(2,1)}, u32[]{:S(2)}) copy-start(bf16[256,512]{1,0:T(8,128)(2,1)} %constant.41.clone.back_high) | copy-start | bytes 786436
  11.7 3.5 %copy-start.2 = (bf16[512,256]{1,0:T(8,128)(2,1)S(1)}, bf16[512,256]{1,0:T(8,128)(2,1)}, u32[]{:S(2)}) copy-start(bf16[512,256]{1,0:T(8,128)(2,1)} %constant.36.clone.sketch_low) | copy-start | bytes 786436
  11.8 1.0 %copy-start.11 = (bf16[128,512]{1,0:T(8,128)(2,1)S(1)}, bf16[128,512]{1,0:T(8,128)(2,1)}, u32[]{:S(2)}) copy-start(bf16[128,512]{1,0:T(8,128)(2,1)} %constant.31.clone.refs_2_) | copy-start | bytes 393220
  12.7 0.8 %copy-start.13 = (f32[16,810]{1,0:T(8,128)S(1)}, f32[16,810]{1,0:T(8,128)}, u32[]{:S(2)}) copy-start(f32[16,810]{1,0:T(8,128)} %refs_0_.1) | copy-start | bytes 155524
  13.6 1.7 %copy-start.14 = (f32[16,256]{1,0:T(8,128)S(1)}, f32[16,256]{1,0:T(8,128)}, u32[]{:S(2)}) copy-start(f32[16,256]{1,0:T(8,128)} %constant.43.clone.weight_ref) | copy-start | bytes 49156
  15.3 10.6 %copy-start.12 = (bf16[48,1024]{1,0:T(8,128)(2,1)S(1)}, bf16[48,1024]{1,0:T(8,128)(2,1)}, u32[]{:S(2)}) copy-start(bf16[48,1024]{1,0:T(8,128)(2,1)} %constant.44.clone.table_ref) | copy-start | bytes 294916

commit v7 on v6

--- a/solution.py
+++ b/solution.py
@@ -173,7 +173,11 @@
     blocks = [
         jnp.concatenate([omega[:, k * COLS : (k + 1) * COLS], pad], 1) for k in range(columns)
     ]
-    out_ref[...] = wide_dot(jnp.concatenate(blocks, 0), high_ref[...], low_ref[...])
+    hats = wide_dot(jnp.concatenate(blocks, 0), high_ref[...], low_ref[...])
+    real, imag = hats[:, :CELLS], hats[:, CELLS:]
+    out_ref[:, :CELLS] = real
+    out_ref[:, CELLS : 2 * CELLS] = real - imag
+    out_ref[:, 2 * CELLS :] = real + imag
 
 
 def minus_product(value, left, right):
@@ -323,7 +327,8 @@
         both[:planes, :half] + both[planes:, half:],
         both[planes:, :half] - both[:planes, half:],
     )
-    for part in range(2):
+    hats = (*hats, hats[0] + hats[1])
+    for part in range(3):
         for piece in range(pieces):
             values = hats[part][:, piece * LANES : (piece + 1) * LANES]
             for p in range(planes):
@@ -331,18 +336,18 @@
                     values[p : p + 1], (8, LANES)
                 )
 
-    def load_x(g1, g2, piece):
+    def load_x(g1, g2, piece, parts=2):
         row = g2 * first + g1
-        return xhat[row, piece], xhat[row, pieces + piece]
+        return tuple(xhat[row, part * pieces + piece] for part in range(parts))
 
     for piece in range(pieces):
         cache = {}
 
         def cached_x(g1, g2):
             if not small:
-                return load_x(g1, g2, piece)
+                return load_x(g1, g2, piece, 3)
             if (g1, g2) not in cache:
-                cache[g1, g2] = load_x(g1, g2, piece)
+                cache[g1, g2] = load_x(g1, g2, piece, 3)
             return cache[g1, g2]
 
         def sketch_tile(tile, carry):
@@ -352,25 +357,26 @@
                 def columns(k1, sums):
                     def column(k2, sums):
                         start = (k1 * span2 + k2) * rank + tile * 8
-                        w_real = omega_ref[rows(start), lanes(0, piece)]
-                        w_imag = omega_ref[rows(start), lanes(1, piece)]
+                        weights = [omega_ref[rows(start), lanes(k, piece)] for k in range(3)]
                         sums = list(sums)
                         for l2 in range(keep2):
-                            x_real, x_imag = cached_x(l1 + k1, l2 + k2)
-                            real, imag = sums[l2]
+                            x_real, x_imag, x_sum = cached_x(l1 + k1, l2 + k2)
+                            common, less_real, less_imag = sums[l2]
                             sums[l2] = (
-                                real + (x_real * w_real + x_imag * w_imag),
-                                imag + (x_imag * w_real - x_real * w_imag),
+                                common + x_sum * weights[0],
+                                less_real + x_imag * weights[1],
+                                less_imag + x_real * weights[2],
                             )
                         return tuple(sums)
 
                     return sweep(span2, column, sums)
 
-                sums = sweep(span1, columns, ((zero, zero),) * keep2)
+                sums = sweep(span1, columns, ((zero, zero, zero),) * keep2)
                 for l2 in range(keep2):
                     start = (l1 * keep2 + l2) * rank + tile * 8
-                    shat[rows(start), lanes(0, piece)] = sums[l2][0]
-                    shat[rows(start), lanes(1, piece)] = sums[l2][1]
+                    common, less_real, less_imag = sums[l2]
+                    shat[rows(start), lanes(0, piece)] = common - less_real
+                    shat[rows(start), lanes(1, piece)] = common - less_imag
                 return carry
 
             return sweep(keep1, first_keep, carry)
@@ -614,7 +620,7 @@
     columns = span1 * span2
     omega_hat = pl.pallas_call(
         functools.partial(omega_kernel, columns),
-        out_shape=jax.ShapeDtypeStruct((columns * rank, 2 * CELLS), jnp.float32),
+        out_shape=jax.ShapeDtypeStruct((columns * rank, 3 * CELLS), jnp.float32),
         in_specs=[VMEM] * (len(omegas) + 2),
         out_specs=VMEM,
         cost_estimate=pl.CostEstimate(
@@ -644,7 +650,7 @@
     )
     area = keep1 * keep2 * rank
     scratch = [
-        (first * second, lines, 8, LANES),
+        (first * second, 3 * PIECES, 8, LANES),
         (area, 2 * CELLS),
         (area, 2 * CELLS),
         (area, 2 * CELLS),

time: 27.4 us -> 27.1 us (0.989)
  local copies, waits for them, and re-layouts: 1.85 us -> 0.09 us
  waiting for transfers between devices: 1.14 us -> 2.87 us
  Pallas kernels: 7.72 us -> 7.43 us
    unnamed x30, local copies, waits for them, and re-layouts: 1.85 us -> 0.09 us
    all_to_all x1, waiting for transfers between devices: 1.14 us -> 2.87 us  [per_device(): lax.all_to_all(blocks, ('wide', 'narrow'), split_axis=0, concat_axis=0, a...]
    pallas_call x1, Pallas kernels: 3.57 us -> 3.27 us  [per_device(): pl.pallas_call(functools.partial(core_kernel, (first, second, rank), orde...]
where the time goes in v7:
time: 27.1 us; the launch traced here: 26.8 us
  starting transfers between devices  9.19 us (34%)
  Pallas kernels  7.43 us (27%)
  blocking collectives  7.01 us (26%)
  waiting for transfers between devices  2.87 us (11%)
    all_to_all x1, blocking collectives, per_device(): lax.all_to_all(rebuilt, 'wide', split_axis=0, concat_axis=0, axis_index_g...  7.01 us
    all_to_all x1, starting transfers between devices, per_device(): lax.all_to_all(blocks, ('wide', 'narrow'), split_axis=0, concat_axis=0, a...  6.22 us
    pallas_call x1, Pallas kernels, per_device(): pl.pallas_call(functools.partial(core_kernel, (first, second, rank), orde...  3.27 us
    ppermute x1, starting transfers between devices, per_device(): omegas.append(lax.ppermute(omega, 'narrow', ring))  2.97 us
    all_to_all x1, waiting for transfers between devices, per_device(): lax.all_to_all(blocks, ('wide', 'narrow'), split_axis=0, concat_axis=0, a...  2.87 us
    pallas_call x1, Pallas kernels, per_device(): pl.pallas_call(spectrum_kernel, out_shape=jax.ShapeDtypeStruct((dests, li...  2.45 us
    pallas_call x1, Pallas kernels, per_device(): pl.pallas_call(synthesis_kernel, out_shape=jax.ShapeDtypeStruct((CELLS, S...  1.25 us
  transfers between devices with their start and end apart: 2, of which 1 were waited for; matrix products, arithmetic and copies ran while one was open for 0% of the time, Pallas kernels for 11%

profile of v7, /device:TPU:0, one launch (start us, length us, event | category | flops | bytes accessed | tf_op | source)
XLA Modules:
  0.0 26.8 jit_solution(14449386986626586437)
XLA Ops:
  0.0 3.0 %collective-permute-start = (f32[16,810]{1,0:T(8,128)}, f32[16,810]{1,0:T(8,128)S(1)}, u32[]{:S(2)}, u32[]{:S(2)}) collective-permute-start(f32[16,810]{1,0:T(8,128)} %refs_0_.1), channel_id=1, source_target_pairs={{0,1},{1,0},{2,3},{3,2},{4,5},{5,4},{6,7},{7,6},{8,9},{9,8},{10,11... | collective-permute-start | bytes 155528 | tf_op jit(solution)/shard_map/ppermute | solution.py:592
  3.0 0.0 copy-start.7
  3.0 0.0 copy-start.8
  3.0 0.0 copy-start.9
  3.0 2.4 %spectrum.1 = f32[16,4,128]{2,1,0:T(4,128)} custom-call(f32[256,1024]{1,0:T(8,128)} %bitcast.3, s32[1,256]{1,0:T(1,128)} %bitcast.4, bf16[64,1024]{1,0:T(8,128)(2,1)} %constant.30.clone.table_ref), custom_call_target="tpu_custom_call" | custom-call | tf_op jit(solution)/shard_map/spectrum/pallas_call | solution.py:596
  5.5 0.0 copy-start.13
  5.5 6.2 %all-to-all-start = ((f32[16,4,128]{2,1,0:T(4,128)}), f32[16,4,128]{2,1,0:T(4,128)S(1)}, u32[]{:S(2)}, u32[]{:S(2)}) async-start(f32[16,4,128]{2,1,0:T(4,128)} %spectrum.1), calls=%async_computation | async-start | bytes 65536 | tf_op jit(solution)/shard_map/all_to_all | solution.py:609
  11.7 0.0 copy-start.1
  11.7 0.0 copy-start.2
  11.7 0.0 copy-start.3
  11.8 0.0 copy-start.4
  11.8 0.0 copy-start.14
  11.8 0.0 collective-permute-done.refs_1_
  11.8 0.0 copy-done.10
  11.8 0.0 copy-done.11
  11.8 0.0 copy-done.13
  11.8 0.5 %omega.1.omega_ref = f32[320,768]{1,0:T(8,128)S(1)} custom-call(f32[16,810]{1,0:T(8,128)S(1)} %copy-done.13, f32[16,810]{1,0:T(8,128)S(1)} %collective-permute-done.refs_1_, bf16[128,512]{1,0:T(8,128)(2,1)S(1)} %copy-done.10, bf16[128,512]{1,0:T(8,128)(2,1)S(1)} %copy-done.11), custom_call_target="tpu_custom_call" | custom-call | flops 125829120 | bytes 655360 | tf_op jit(solution)/shard_map/omega/pallas_call | solution.py:621
  12.3 2.9 %all-to-all-done.x_ref = f32[16,4,128]{2,1,0:T(4,128)S(1)} async-done(((f32[16,4,128]{2,1,0:T(4,128)}), f32[16,4,128]{2,1,0:T(4,128)S(1)}, u32[]{:S(2)}, u32[]{:S(2)}) %all-to-all-start) | async-done | bytes 32800 | tf_op jit(solution)/shard_map/all_to_all | solution.py:609
  15.2 0.0 copy-done.5
  15.2 0.0 copy-done.6
  15.2 0.0 copy-done.7
  15.2 0.0 copy-done.8
  15.2 0.0 copy-done.9
  15.2 0.0 copy-done
  15.2 0.0 copy-done.1
  15.2 0.0 copy-done.2
  15.2 0.0 copy-done.3
  15.2 0.0 copy-done.4
  15.2 0.0 copy-start.12
  15.3 3.3 %core.1 = f32[8,4,128]{2,1,0:T(4,128)S(1)} custom-call(f32[16,4,128]{2,1,0:T(4,128)S(1)} %all-to-all-done.x_ref, f32[320,768]{1,0:T(8,128)S(1)} %omega.1.omega_ref, bf16[256,512]{1,0:T(8,128)(2,1)S(1)} %copy-done, bf16[256,512]{1,0:T(8,128)(2,1)S(1)} %copy-done.1, bf16[512,256]{1,0:T(8,128)(2,1)S(1)} %copy-done.2, bf16[512,256]{1,0:T(8,128)(2,1)S(1)} %copy-done.3, ...), custom_call_target="tpu_custom_call" | custom-call | tf_op jit(solution)/shard_map/core/pallas_call | solution.py:661
  18.5 7.0 %all_to_all.10.cells_ref = f32[8,4,128]{2,1,0:T(4,128)S(1)} all-to-all(f32[8,4,128]{2,1,0:T(4,128)S(1)} %core.1), channel_id=1, replica_groups={{10,8,6,4,2,0,14,12},{11,9,7,5,3,1,15,13},{26,24,22,20,18,16,30,28},{27..., dimensions={0} | all-to-all | bytes 32768 | tf_op jit(solution)/shard_map/all_to_all | solution.py:670
  25.5 1.3 %synthesis.1 = f32[256,1024]{1,0:T(8,128)} custom-call(f32[8,4,128]{2,1,0:T(4,128)S(1)} %all_to_all.10.cells_ref, bf16[48,1024]{1,0:T(8,128)(2,1)S(1)} %copy-done.12), custom_call_target="tpu_custom_call" | custom-call | tf_op jit(solution)/shard_map/synthesis/pallas_call | solution.py:680
  (7 shorter events, 0.0 us)
Async XLA Ops:
  0.0 11.8 %collective-permute-start = (f32[16,810]{1,0:T(8,128)}, f32[16,810]{1,0:T(8,128)S(1)}, u32[]{:S(2)}, u32[]{:S(2)}) collective-permute-start(f32[16,810]{1,0:T(8,128)} %refs_0_.1), channel_id=1, source_target_pairs={{0,1},{1,0},{2,3},{3,2},{4,5},{5,4},{6,7},{7,6},{8,9},{9,8},{10,11... | collective-permute-start | bytes 155528 | tf_op jit(solution)/shard_map/ppermute | solution.py:592
  3.0 8.8 %copy-start.10 = (bf16[128,512]{1,0:T(8,128)(2,1)S(1)}, bf16[128,512]{1,0:T(8,128)(2,1)}, u32[]{:S(2)}) copy-start(bf16[128,512]{1,0:T(8,128)(2,1)} %constant.31.clone.refs_2_) | copy-start | bytes 393220
  3.0 8.8 %copy-start.11 = (bf16[128,512]{1,0:T(8,128)(2,1)S(1)}, bf16[128,512]{1,0:T(8,128)(2,1)}, u32[]{:S(2)}) copy-start(bf16[128,512]{1,0:T(8,128)(2,1)} %constant.32.clone.refs_3_) | copy-start | bytes 393220
  3.0 12.2 %copy-start.5 = (bf16[256,512]{1,0:T(8,128)(2,1)S(1)}, bf16[256,512]{1,0:T(8,128)(2,1)}, u32[]{:S(2)}) copy-start(bf16[256,512]{1,0:T(8,128)(2,1)} %constant.42.clone.back_low) | copy-start | bytes 786436
  3.0 12.2 %copy-start.6 = (bf16[128,512]{1,0:T(8,128)(2,1)S(1)}, bf16[128,512]{1,0:T(8,128)(2,1)}, u32[]{:S(2)}) copy-start(bf16[128,512]{1,0:T(8,128)(2,1)} %constant.37.clone.basis_high) | copy-start | bytes 393220
  3.0 12.2 %copy-start.7 = (bf16[128,512]{1,0:T(8,128)(2,1)S(1)}, bf16[128,512]{1,0:T(8,128)(2,1)}, u32[]{:S(2)}) copy-start(bf16[128,512]{1,0:T(8,128)(2,1)} %constant.38.clone.basis_low) | copy-start | bytes 393220
  3.0 12.2 %copy-start.8 = (bf16[256,256]{1,0:T(8,128)(2,1)S(1)}, bf16[256,256]{1,0:T(8,128)(2,1)}, u32[]{:S(2)}) copy-start(bf16[256,256]{1,0:T(8,128)(2,1)} %constant.39.clone.window_high) | copy-start | bytes 393220
  3.0 12.2 %copy-start.9 = (bf16[256,256]{1,0:T(8,128)(2,1)S(1)}, bf16[256,256]{1,0:T(8,128)(2,1)}, u32[]{:S(2)}) copy-start(bf16[256,256]{1,0:T(8,128)(2,1)} %constant.40.clone.window_low) | copy-start | bytes 393220
  5.5 6.3 %copy-start.13 = (f32[16,810]{1,0:T(8,128)S(1)}, f32[16,810]{1,0:T(8,128)}, u32[]{:S(2)}) copy-start(f32[16,810]{1,0:T(8,128)} %refs_0_.1) | copy-start | bytes 155524
  5.5 9.7 %all-to-all-start = ((f32[16,4,128]{2,1,0:T(4,128)}), f32[16,4,128]{2,1,0:T(4,128)S(1)}, u32[]{:S(2)}, u32[]{:S(2)}) async-start(f32[16,4,128]{2,1,0:T(4,128)} %spectrum.1), calls=%async_computation | async-start | bytes 65536 | tf_op jit(solution)/shard_map/all_to_all | solution.py:609
  11.7 3.5 %copy-start = (bf16[256,512]{1,0:T(8,128)(2,1)S(1)}, bf16[256,512]{1,0:T(8,128)(2,1)}, u32[]{:S(2)}) copy-start(bf16[256,512]{1,0:T(8,128)(2,1)} %constant.33.clone.analysis_high) | copy-start | bytes 786436
  11.7 3.5 %copy-start.1 = (bf16[256,512]{1,0:T(8,128)(2,1)S(1)}, bf16[256,512]{1,0:T(8,128)(2,1)}, u32[]{:S(2)}) copy-start(bf16[256,512]{1,0:T(8,128)(2,1)} %constant.34.clone.analysis_low) | copy-start | bytes 786436
  11.7 3.5 %copy-start.2 = (bf16[512,256]{1,0:T(8,128)(2,1)S(1)}, bf16[512,256]{1,0:T(8,128)(2,1)}, u32[]{:S(2)}) copy-start(bf16[512,256]{1,0:T(8,128)(2,1)} %constant.35.clone.sketch_high) | copy-start | bytes 786436
  11.7 3.5 %copy-start.3 = (bf16[512,256]{1,0:T(8,128)(2,1)S(1)}, bf16[512,256]{1,0:T(8,128)(2,1)}, u32[]{:S(2)}) copy-start(bf16[512,256]{1,0:T(8,128)(2,1)} %constant.36.clone.sketch_low) | copy-start | bytes 786436
  11.8 3.5 %copy-start.4 = (bf16[256,512]{1,0:T(8,128)(2,1)S(1)}, bf16[256,512]{1,0:T(8,128)(2,1)}, u32[]{:S(2)}) copy-start(bf16[256,512]{1,0:T(8,128)(2,1)} %constant.41.clone.back_high) | copy-start | bytes 786436
  11.8 3.5 %copy-start.14 = (f32[16,256]{1,0:T(8,128)S(1)}, f32[16,256]{1,0:T(8,128)}, u32[]{:S(2)}) copy-start(f32[16,256]{1,0:T(8,128)} %constant.43.clone.weight_ref) | copy-start | bytes 49156
  15.2 10.3 %copy-start.12 = (bf16[48,1024]{1,0:T(8,128)(2,1)S(1)}, bf16[48,1024]{1,0:T(8,128)(2,1)}, u32[]{:S(2)}) copy-start(bf16[48,1024]{1,0:T(8,128)(2,1)} %constant.44.clone.table_ref) | copy-start | bytes 294916

commit v8 on v7

--- a/solution.py
+++ b/solution.py
@@ -586,11 +586,6 @@
     dests = wide_count * narrow_count
     lines = 2 * PIECES
 
-    omegas = [omega]
-    for step in range(1, narrow_count):
-        ring = [(i, (i + step) % narrow_count) for i in range(narrow_count)]
-        omegas.append(lax.ppermute(omega, "narrow", ring))
-
     order = group_order(dests)
     high, low = halves(spectrum_table(freq_total, [i // narrow_count for i in order]))
     blocks = pl.pallas_call(
@@ -606,6 +601,12 @@
         ],
         name="spectrum",
     )(traces.reshape(CELLS, S), mask.reshape(1, CELLS), np.concatenate([high, low], 0))
+    blocks, omega = lax.optimization_barrier((blocks, omega))
+    omegas = [omega]
+    for step in range(1, narrow_count):
+        ring = [(i, (i + step) % narrow_count) for i in range(narrow_count)]
+        omegas.append(lax.ppermute(omega, "narrow", ring))
+
     grid = lax.all_to_all(
         blocks,
         ("wide", "narrow"),

time: 27.1 us -> 26.9 us (level)
  transfers between devices with their start and end apart: 2 -> 2, of which waited for: 1 -> 1; matrix products, arithmetic and copies ran while one was open for 0% -> 0% of each run, Pallas kernels for 11% -> 2%
where the time goes in v8:
time: 26.9 us; the launch traced here: 26.7 us
  starting transfers between devices  9.14 us (34%)
  Pallas kernels  7.41 us (28%)
  blocking collectives  7.01 us (26%)
  waiting for transfers between devices  2.88 us (11%)
    all_to_all x1, blocking collectives, per_device(): lax.all_to_all(rebuilt, 'wide', split_axis=0, concat_axis=0, axis_index_g...  7.01 us
    all_to_all x1, starting transfers between devices, per_device(): lax.all_to_all(blocks, ('wide', 'narrow'), split_axis=0, concat_axis=0, a...  6.08 us
    pallas_call x1, Pallas kernels, per_device(): pl.pallas_call(functools.partial(core_kernel, (first, second, rank), orde...  3.26 us
    ppermute x1, starting transfers between devices, per_device(): omegas.append(lax.ppermute(omega, 'narrow', ring))  3.06 us
    all_to_all x1, waiting for transfers between devices, per_device(): lax.all_to_all(blocks, ('wide', 'narrow'), split_axis=0, concat_axis=0, a...  2.87 us
    pallas_call x1, Pallas kernels, per_device(): pl.pallas_call(spectrum_kernel, out_shape=jax.ShapeDtypeStruct((dests, li...  2.45 us
    pallas_call x1, Pallas kernels, per_device(): pl.pallas_call(synthesis_kernel, out_shape=jax.ShapeDtypeStruct((CELLS, S...  1.24 us
  transfers between devices with their start and end apart: 2, of which 1 were waited for; matrix products, arithmetic and copies ran while one was open for 0% of the time, Pallas kernels for 2%

profile of v8, /device:TPU:0, one launch (start us, length us, event | category | flops | bytes accessed | tf_op | source)
XLA Modules:
  0.0 26.7 jit_solution(18077304463794796808)
XLA Ops:
  0.0 0.0 copy-start.7
  0.0 0.0 copy-start.8
  0.0 0.0 copy-start.9
  0.1 2.5 %spectrum.1 = f32[16,4,128]{2,1,0:T(4,128)} custom-call(f32[256,1024]{1,0:T(8,128)} %bitcast.3, s32[1,256]{1,0:T(1,128)} %bitcast.4, bf16[64,1024]{1,0:T(8,128)(2,1)} %constant.30.clone.table_ref), custom_call_target="tpu_custom_call" | custom-call | tf_op jit(solution)/shard_map/spectrum/pallas_call | solution.py:591
  2.5 0.0 copy-done.13
  2.5 3.1 %collective-permute-start = (f32[16,810]{1,0:T(8,128)S(1)}, f32[16,810]{1,0:T(8,128)S(1)}, u32[]{:S(2)}, u32[]{:S(2)}) collective-permute-start(f32[16,810]{1,0:T(8,128)S(1)} %copy-done.13), channel_id=1, source_target_pairs={{0,1},{1,0},{2,3},{3,2},{4,5},{5,4},{6,7},{7,6},{8,9},{9,8},{10,11... | collective-permute-start | bytes 155528 | tf_op jit(solution)/shard_map/ppermute | solution.py:608
  5.6 6.1 %all-to-all-start = ((f32[16,4,128]{2,1,0:T(4,128)}), f32[16,4,128]{2,1,0:T(4,128)S(1)}, u32[]{:S(2)}, u32[]{:S(2)}) async-start(f32[16,4,128]{2,1,0:T(4,128)} %spectrum.1), calls=%async_computation | async-start | bytes 65536 | tf_op jit(solution)/shard_map/all_to_all | solution.py:610
  11.7 0.0 copy-start.1
  11.7 0.0 copy-start.2
  11.7 0.0 copy-start.3
  11.7 0.0 copy-start.4
  11.7 0.0 copy-start.14
  11.7 0.0 collective-permute-done.refs_1_
  11.7 0.0 copy-done.10
  11.8 0.0 copy-done.11
  11.8 0.5 %omega.1.omega_ref = f32[320,768]{1,0:T(8,128)S(1)} custom-call(f32[16,810]{1,0:T(8,128)S(1)} %copy-done.13, f32[16,810]{1,0:T(8,128)S(1)} %collective-permute-done.refs_1_, bf16[128,512]{1,0:T(8,128)(2,1)S(1)} %copy-done.11, bf16[128,512]{1,0:T(8,128)(2,1)S(1)} %copy-done.10), custom_call_target="tpu_custom_call" | custom-call | flops 125829120 | bytes 655360 | tf_op jit(solution)/shard_map/omega/pallas_call | solution.py:622
  12.2 2.9 %all-to-all-done.x_ref = f32[16,4,128]{2,1,0:T(4,128)S(1)} async-done(((f32[16,4,128]{2,1,0:T(4,128)}), f32[16,4,128]{2,1,0:T(4,128)S(1)}, u32[]{:S(2)}, u32[]{:S(2)}) %all-to-all-start) | async-done | bytes 32800 | tf_op jit(solution)/shard_map/all_to_all | solution.py:610
  15.1 0.0 copy-done.5
  15.1 0.0 copy-done.6
  15.1 0.0 copy-done.7
  15.1 0.0 copy-done.8
  15.1 0.0 copy-done.9
  15.1 0.0 copy-done
  15.1 0.0 copy-done.1
  15.2 0.0 copy-done.2
  15.2 0.0 copy-done.3
  15.2 0.0 copy-done.4
  15.2 0.0 copy-done.14
  15.2 0.0 copy-start.12
  15.2 3.3 %core.1 = f32[8,4,128]{2,1,0:T(4,128)S(1)} custom-call(f32[16,4,128]{2,1,0:T(4,128)S(1)} %all-to-all-done.x_ref, f32[320,768]{1,0:T(8,128)S(1)} %omega.1.omega_ref, bf16[256,512]{1,0:T(8,128)(2,1)S(1)} %copy-done.5, bf16[256,512]{1,0:T(8,128)(2,1)S(1)} %copy-done.4, bf16[512,256]{1,0:T(8,128)(2,1)S(1)} %copy-done.3, bf16[512,256]{1,0:T(8,128)(2,1)S(1)} %copy-done.2, ...), custom_call_target="tpu_custom_call" | custom-call | tf_op jit(solution)/shard_map/core/pallas_call | solution.py:662
  18.5 7.0 %all_to_all.10.cells_ref = f32[8,4,128]{2,1,0:T(4,128)S(1)} all-to-all(f32[8,4,128]{2,1,0:T(4,128)S(1)} %core.1), channel_id=1, replica_groups={{10,8,6,4,2,0,14,12},{11,9,7,5,3,1,15,13},{26,24,22,20,18,16,30,28},{27..., dimensions={0} | all-to-all | bytes 32768 | tf_op jit(solution)/shard_map/all_to_all | solution.py:671
  25.5 1.2 %synthesis.1 = f32[256,1024]{1,0:T(8,128)} custom-call(f32[8,4,128]{2,1,0:T(4,128)S(1)} %all_to_all.10.cells_ref, bf16[48,1024]{1,0:T(8,128)(2,1)S(1)} %copy-done.12), custom_call_target="tpu_custom_call" | custom-call | tf_op jit(solution)/shard_map/synthesis/pallas_call | solution.py:681
  (7 shorter events, 0.0 us)
Async XLA Ops:
  0.0 2.5 %copy-start.13 = (f32[16,810]{1,0:T(8,128)S(1)}, f32[16,810]{1,0:T(8,128)}, u32[]{:S(2)}) copy-start(f32[16,810]{1,0:T(8,128)} %refs_0_) | copy-start | bytes 155524
  0.0 11.7 %copy-start.10 = (bf16[128,512]{1,0:T(8,128)(2,1)S(1)}, bf16[128,512]{1,0:T(8,128)(2,1)}, u32[]{:S(2)}) copy-start(bf16[128,512]{1,0:T(8,128)(2,1)} %constant.32.clone.refs_3_) | copy-start | bytes 393220
  0.0 11.8 %copy-start.11 = (bf16[128,512]{1,0:T(8,128)(2,1)S(1)}, bf16[128,512]{1,0:T(8,128)(2,1)}, u32[]{:S(2)}) copy-start(bf16[128,512]{1,0:T(8,128)(2,1)} %constant.31.clone.refs_2_) | copy-start | bytes 393220
  0.0 15.1 %copy-start.5 = (bf16[256,512]{1,0:T(8,128)(2,1)S(1)}, bf16[256,512]{1,0:T(8,128)(2,1)}, u32[]{:S(2)}) copy-start(bf16[256,512]{1,0:T(8,128)(2,1)} %constant.33.clone.analysis_high) | copy-start | bytes 786436
  0.0 15.1 %copy-start.6 = (bf16[256,256]{1,0:T(8,128)(2,1)S(1)}, bf16[256,256]{1,0:T(8,128)(2,1)}, u32[]{:S(2)}) copy-start(bf16[256,256]{1,0:T(8,128)(2,1)} %constant.40.clone.window_low) | copy-start | bytes 393220
  0.0 15.1 %copy-start.7 = (bf16[256,256]{1,0:T(8,128)(2,1)S(1)}, bf16[256,256]{1,0:T(8,128)(2,1)}, u32[]{:S(2)}) copy-start(bf16[256,256]{1,0:T(8,128)(2,1)} %constant.39.clone.window_high) | copy-start | bytes 393220
  0.0 15.1 %copy-start.8 = (bf16[128,512]{1,0:T(8,128)(2,1)S(1)}, bf16[128,512]{1,0:T(8,128)(2,1)}, u32[]{:S(2)}) copy-start(bf16[128,512]{1,0:T(8,128)(2,1)} %constant.38.clone.basis_low) | copy-start | bytes 393220
  0.0 15.1 %copy-start.9 = (bf16[128,512]{1,0:T(8,128)(2,1)S(1)}, bf16[128,512]{1,0:T(8,128)(2,1)}, u32[]{:S(2)}) copy-start(bf16[128,512]{1,0:T(8,128)(2,1)} %constant.37.clone.basis_high) | copy-start | bytes 393220
  2.5 9.2 %collective-permute-start = (f32[16,810]{1,0:T(8,128)S(1)}, f32[16,810]{1,0:T(8,128)S(1)}, u32[]{:S(2)}, u32[]{:S(2)}) collective-permute-start(f32[16,810]{1,0:T(8,128)S(1)} %copy-done.13), channel_id=1, source_target_pairs={{0,1},{1,0},{2,3},{3,2},{4,5},{5,4},{6,7},{7,6},{8,9},{9,8},{10,11... | collective-permute-start | bytes 155528 | tf_op jit(solution)/shard_map/ppermute | solution.py:608
  5.6 9.5 %all-to-all-start = ((f32[16,4,128]{2,1,0:T(4,128)}), f32[16,4,128]{2,1,0:T(4,128)S(1)}, u32[]{:S(2)}, u32[]{:S(2)}) async-start(f32[16,4,128]{2,1,0:T(4,128)} %spectrum.1), calls=%async_computation | async-start | bytes 65536 | tf_op jit(solution)/shard_map/all_to_all | solution.py:610
  11.7 3.5 %copy-start = (bf16[256,512]{1,0:T(8,128)(2,1)S(1)}, bf16[256,512]{1,0:T(8,128)(2,1)}, u32[]{:S(2)}) copy-start(bf16[256,512]{1,0:T(8,128)(2,1)} %constant.42.clone.back_low) | copy-start | bytes 786436
  11.7 3.5 %copy-start.1 = (bf16[256,512]{1,0:T(8,128)(2,1)S(1)}, bf16[256,512]{1,0:T(8,128)(2,1)}, u32[]{:S(2)}) copy-start(bf16[256,512]{1,0:T(8,128)(2,1)} %constant.41.clone.back_high) | copy-start | bytes 786436
  11.7 3.5 %copy-start.2 = (bf16[512,256]{1,0:T(8,128)(2,1)S(1)}, bf16[512,256]{1,0:T(8,128)(2,1)}, u32[]{:S(2)}) copy-start(bf16[512,256]{1,0:T(8,128)(2,1)} %constant.36.clone.sketch_low) | copy-start | bytes 786436
  11.7 3.5 %copy-start.3 = (bf16[512,256]{1,0:T(8,128)(2,1)S(1)}, bf16[512,256]{1,0:T(8,128)(2,1)}, u32[]{:S(2)}) copy-start(bf16[512,256]{1,0:T(8,128)(2,1)} %constant.35.clone.sketch_high) | copy-start | bytes 786436
  11.7 3.5 %copy-start.4 = (bf16[256,512]{1,0:T(8,128)(2,1)S(1)}, bf16[256,512]{1,0:T(8,128)(2,1)}, u32[]{:S(2)}) copy-start(bf16[256,512]{1,0:T(8,128)(2,1)} %constant.34.clone.analysis_low) | copy-start | bytes 786436
  11.7 3.5 %copy-start.14 = (f32[16,256]{1,0:T(8,128)S(1)}, f32[16,256]{1,0:T(8,128)}, u32[]{:S(2)}) copy-start(f32[16,256]{1,0:T(8,128)} %constant.43.clone.weight_ref) | copy-start | bytes 49156
  15.2 10.3 %copy-start.12 = (bf16[48,1024]{1,0:T(8,128)(2,1)S(1)}, bf16[48,1024]{1,0:T(8,128)(2,1)}, u32[]{:S(2)}) copy-start(bf16[48,1024]{1,0:T(8,128)(2,1)} %constant.44.clone.table_ref) | copy-start | bytes 294916

commit v9 on v8

--- a/solution.py
+++ b/solution.py
@@ -422,9 +422,9 @@
 
             def cached_x(l1, g2):
                 if not small:
-                    return load_x(l1 + k1, g2, piece)
+                    return load_x(l1 + k1, g2, piece, 3)
                 if (l1, g2) not in cache:
-                    cache[l1, g2] = load_x(l1 + k1, g2, piece)
+                    cache[l1, g2] = load_x(l1 + k1, g2, piece, 3)
                 return cache[l1, g2]
 
             def column_tile(tile, carry):
@@ -436,20 +436,24 @@
                         start = (l1 * keep2 + l2) * rank + tile * 8
                         s_real = bhat[rows(start), lanes(0, piece)]
                         s_imag = bhat[rows(start), lanes(1, piece)]
+                        s_less, s_more = s_real - s_imag, s_real + s_imag
                         for k2 in range(span2):
-                            x_real, x_imag = cached_x(l1, l2 + k2)
-                            real, imag = sums[k2]
+                            x_real, x_imag, x_sum = cached_x(l1, l2 + k2)
+                            common, less_real, less_imag = sums[k2]
                             sums[k2] = (
-                                real + (s_real * x_real + s_imag * x_imag),
-                                imag + (s_real * x_imag - s_imag * x_real),
+                                common + x_sum * s_real,
+                                less_real + x_imag * s_less,
+                                less_imag + x_real * s_more,
                             )
                     return tuple(sums)
 
-                sums = sweep(keep1, first_keep, ((zero, zero),) * span2)
+                sums = sweep(keep1, first_keep, ((zero, zero, zero),) * span2)
                 for k2 in range(span2):
                     for part in range(2):
                         start = (part * span2 + k2) * rank + tile * 8
-                        dhat[rows(start), pl.ds(piece * LANES, LANES)] = sums[k2][part]
+                        dhat[rows(start), pl.ds(piece * LANES, LANES)] = (
+                            sums[k2][0] - sums[k2][1 + part]
+                        )
                 return carry
 
             if small:

time: 26.9 us -> 26.9 us (level)
  no operation moved by 1% of the time
where the time goes in v9:
time: 26.9 us; the launch traced here: 26.7 us
  starting transfers between devices  9.14 us (34%)
  Pallas kernels  7.41 us (28%)
  blocking collectives  7.01 us (26%)
  waiting for transfers between devices  2.88 us (11%)
    all_to_all x1, blocking collectives, per_device(): lax.all_to_all(rebuilt, 'wide', split_axis=0, concat_axis=0, axis_index_g...  7.01 us
    all_to_all x1, starting transfers between devices, per_device(): lax.all_to_all(blocks, ('wide', 'narrow'), split_axis=0, concat_axis=0, a...  6.08 us
    pallas_call x1, Pallas kernels, per_device(): pl.pallas_call(functools.partial(core_kernel, (first, second, rank), orde...  3.26 us
    ppermute x1, starting transfers between devices, per_device(): omegas.append(lax.ppermute(omega, 'narrow', ring))  3.06 us
    all_to_all x1, waiting for transfers between devices, per_device(): lax.all_to_all(blocks, ('wide', 'narrow'), split_axis=0, concat_axis=0, a...  2.87 us
    pallas_call x1, Pallas kernels, per_device(): pl.pallas_call(spectrum_kernel, out_shape=jax.ShapeDtypeStruct((dests, li...  2.45 us
    pallas_call x1, Pallas kernels, per_device(): pl.pallas_call(synthesis_kernel, out_shape=jax.ShapeDtypeStruct((CELLS, S...  1.24 us
  transfers between devices with their start and end apart: 2, of which 1 were waited for; matrix products, arithmetic and copies ran while one was open for 0% of the time, Pallas kernels for 2%

profile of v9, /device:TPU:0, one launch (start us, length us, event | category | flops | bytes accessed | tf_op | source)
XLA Modules:
  0.0 26.7 jit_solution(10271865264990002895)
XLA Ops:
  0.0 0.0 copy-start.7
  0.0 0.0 copy-start.8
  0.0 0.0 copy-start.9
  0.1 2.5 %spectrum.1 = f32[16,4,128]{2,1,0:T(4,128)} custom-call(f32[256,1024]{1,0:T(8,128)} %bitcast.3, s32[1,256]{1,0:T(1,128)} %bitcast.4, bf16[64,1024]{1,0:T(8,128)(2,1)} %constant.30.clone.table_ref), custom_call_target="tpu_custom_call" | custom-call | tf_op jit(solution)/shard_map/spectrum/pallas_call | solution.py:595
  2.5 0.0 copy-done.13
  2.5 3.1 %collective-permute-start = (f32[16,810]{1,0:T(8,128)S(1)}, f32[16,810]{1,0:T(8,128)S(1)}, u32[]{:S(2)}, u32[]{:S(2)}) collective-permute-start(f32[16,810]{1,0:T(8,128)S(1)} %copy-done.13), channel_id=1, source_target_pairs={{0,1},{1,0},{2,3},{3,2},{4,5},{5,4},{6,7},{7,6},{8,9},{9,8},{10,11... | collective-permute-start | bytes 155528 | tf_op jit(solution)/shard_map/ppermute | solution.py:612
  5.6 6.1 %all-to-all-start = ((f32[16,4,128]{2,1,0:T(4,128)}), f32[16,4,128]{2,1,0:T(4,128)S(1)}, u32[]{:S(2)}, u32[]{:S(2)}) async-start(f32[16,4,128]{2,1,0:T(4,128)} %spectrum.1), calls=%async_computation | async-start | bytes 65536 | tf_op jit(solution)/shard_map/all_to_all | solution.py:614
  11.7 0.0 copy-start.1
  11.7 0.0 copy-start.2
  11.7 0.0 copy-start.3
  11.7 0.0 copy-start.4
  11.7 0.0 copy-start.14
  11.7 0.0 collective-permute-done.refs_1_
  11.7 0.0 copy-done.10
  11.8 0.0 copy-done.11
  11.8 0.5 %omega.1.omega_ref = f32[320,768]{1,0:T(8,128)S(1)} custom-call(f32[16,810]{1,0:T(8,128)S(1)} %copy-done.13, f32[16,810]{1,0:T(8,128)S(1)} %collective-permute-done.refs_1_, bf16[128,512]{1,0:T(8,128)(2,1)S(1)} %copy-done.11, bf16[128,512]{1,0:T(8,128)(2,1)S(1)} %copy-done.10), custom_call_target="tpu_custom_call" | custom-call | flops 125829120 | bytes 655360 | tf_op jit(solution)/shard_map/omega/pallas_call | solution.py:626
  12.2 2.9 %all-to-all-done.x_ref = f32[16,4,128]{2,1,0:T(4,128)S(1)} async-done(((f32[16,4,128]{2,1,0:T(4,128)}), f32[16,4,128]{2,1,0:T(4,128)S(1)}, u32[]{:S(2)}, u32[]{:S(2)}) %all-to-all-start) | async-done | bytes 32800 | tf_op jit(solution)/shard_map/all_to_all | solution.py:614
  15.1 0.0 copy-done.5
  15.1 0.0 copy-done.6
  15.1 0.0 copy-done.7
  15.1 0.0 copy-done.8
  15.1 0.0 copy-done.9
  15.1 0.0 copy-done
  15.1 0.0 copy-done.1
  15.2 0.0 copy-done.2
  15.2 0.0 copy-done.3
  15.2 0.0 copy-done.4
  15.2 0.0 copy-done.14
  15.2 0.0 copy-start.12
  15.2 3.3 %core.1 = f32[8,4,128]{2,1,0:T(4,128)S(1)} custom-call(f32[16,4,128]{2,1,0:T(4,128)S(1)} %all-to-all-done.x_ref, f32[320,768]{1,0:T(8,128)S(1)} %omega.1.omega_ref, bf16[256,512]{1,0:T(8,128)(2,1)S(1)} %copy-done.5, bf16[256,512]{1,0:T(8,128)(2,1)S(1)} %copy-done.4, bf16[512,256]{1,0:T(8,128)(2,1)S(1)} %copy-done.3, bf16[512,256]{1,0:T(8,128)(2,1)S(1)} %copy-done.2, ...), custom_call_target="tpu_custom_call" | custom-call | tf_op jit(solution)/shard_map/core/pallas_call | solution.py:666
  18.5 7.0 %all_to_all.10.cells_ref = f32[8,4,128]{2,1,0:T(4,128)S(1)} all-to-all(f32[8,4,128]{2,1,0:T(4,128)S(1)} %core.1), channel_id=1, replica_groups={{10,8,6,4,2,0,14,12},{11,9,7,5,3,1,15,13},{26,24,22,20,18,16,30,28},{27..., dimensions={0} | all-to-all | bytes 32768 | tf_op jit(solution)/shard_map/all_to_all | solution.py:675
  25.5 1.2 %synthesis.1 = f32[256,1024]{1,0:T(8,128)} custom-call(f32[8,4,128]{2,1,0:T(4,128)S(1)} %all_to_all.10.cells_ref, bf16[48,1024]{1,0:T(8,128)(2,1)S(1)} %copy-done.12), custom_call_target="tpu_custom_call" | custom-call | tf_op jit(solution)/shard_map/synthesis/pallas_call | solution.py:685
  (7 shorter events, 0.0 us)
Async XLA Ops:
  0.0 2.5 %copy-start.13 = (f32[16,810]{1,0:T(8,128)S(1)}, f32[16,810]{1,0:T(8,128)}, u32[]{:S(2)}) copy-start(f32[16,810]{1,0:T(8,128)} %refs_0_) | copy-start | bytes 155524
  0.0 11.7 %copy-start.10 = (bf16[128,512]{1,0:T(8,128)(2,1)S(1)}, bf16[128,512]{1,0:T(8,128)(2,1)}, u32[]{:S(2)}) copy-start(bf16[128,512]{1,0:T(8,128)(2,1)} %constant.32.clone.refs_3_) | copy-start | bytes 393220
  0.0 11.8 %copy-start.11 = (bf16[128,512]{1,0:T(8,128)(2,1)S(1)}, bf16[128,512]{1,0:T(8,128)(2,1)}, u32[]{:S(2)}) copy-start(bf16[128,512]{1,0:T(8,128)(2,1)} %constant.31.clone.refs_2_) | copy-start | bytes 393220
  0.0 15.1 %copy-start.5 = (bf16[256,512]{1,0:T(8,128)(2,1)S(1)}, bf16[256,512]{1,0:T(8,128)(2,1)}, u32[]{:S(2)}) copy-start(bf16[256,512]{1,0:T(8,128)(2,1)} %constant.33.clone.analysis_high) | copy-start | bytes 786436
  0.0 15.1 %copy-start.6 = (bf16[256,256]{1,0:T(8,128)(2,1)S(1)}, bf16[256,256]{1,0:T(8,128)(2,1)}, u32[]{:S(2)}) copy-start(bf16[256,256]{1,0:T(8,128)(2,1)} %constant.40.clone.window_low) | copy-start | bytes 393220
  0.0 15.1 %copy-start.7 = (bf16[256,256]{1,0:T(8,128)(2,1)S(1)}, bf16[256,256]{1,0:T(8,128)(2,1)}, u32[]{:S(2)}) copy-start(bf16[256,256]{1,0:T(8,128)(2,1)} %constant.39.clone.window_high) | copy-start | bytes 393220
  0.0 15.1 %copy-start.8 = (bf16[128,512]{1,0:T(8,128)(2,1)S(1)}, bf16[128,512]{1,0:T(8,128)(2,1)}, u32[]{:S(2)}) copy-start(bf16[128,512]{1,0:T(8,128)(2,1)} %constant.38.clone.basis_low) | copy-start | bytes 393220
  0.0 15.1 %copy-start.9 = (bf16[128,512]{1,0:T(8,128)(2,1)S(1)}, bf16[128,512]{1,0:T(8,128)(2,1)}, u32[]{:S(2)}) copy-start(bf16[128,512]{1,0:T(8,128)(2,1)} %constant.37.clone.basis_high) | copy-start | bytes 393220
  2.5 9.2 %collective-permute-start = (f32[16,810]{1,0:T(8,128)S(1)}, f32[16,810]{1,0:T(8,128)S(1)}, u32[]{:S(2)}, u32[]{:S(2)}) collective-permute-start(f32[16,810]{1,0:T(8,128)S(1)} %copy-done.13), channel_id=1, source_target_pairs={{0,1},{1,0},{2,3},{3,2},{4,5},{5,4},{6,7},{7,6},{8,9},{9,8},{10,11... | collective-permute-start | bytes 155528 | tf_op jit(solution)/shard_map/ppermute | solution.py:612
  5.6 9.5 %all-to-all-start = ((f32[16,4,128]{2,1,0:T(4,128)}), f32[16,4,128]{2,1,0:T(4,128)S(1)}, u32[]{:S(2)}, u32[]{:S(2)}) async-start(f32[16,4,128]{2,1,0:T(4,128)} %spectrum.1), calls=%async_computation | async-start | bytes 65536 | tf_op jit(solution)/shard_map/all_to_all | solution.py:614
  11.7 3.5 %copy-start = (bf16[256,512]{1,0:T(8,128)(2,1)S(1)}, bf16[256,512]{1,0:T(8,128)(2,1)}, u32[]{:S(2)}) copy-start(bf16[256,512]{1,0:T(8,128)(2,1)} %constant.42.clone.back_low) | copy-start | bytes 786436
  11.7 3.5 %copy-start.1 = (bf16[256,512]{1,0:T(8,128)(2,1)S(1)}, bf16[256,512]{1,0:T(8,128)(2,1)}, u32[]{:S(2)}) copy-start(bf16[256,512]{1,0:T(8,128)(2,1)} %constant.41.clone.back_high) | copy-start | bytes 786436
  11.7 3.5 %copy-start.2 = (bf16[512,256]{1,0:T(8,128)(2,1)S(1)}, bf16[512,256]{1,0:T(8,128)(2,1)}, u32[]{:S(2)}) copy-start(bf16[512,256]{1,0:T(8,128)(2,1)} %constant.36.clone.sketch_low) | copy-start | bytes 786436
  11.7 3.5 %copy-start.3 = (bf16[512,256]{1,0:T(8,128)(2,1)S(1)}, bf16[512,256]{1,0:T(8,128)(2,1)}, u32[]{:S(2)}) copy-start(bf16[512,256]{1,0:T(8,128)(2,1)} %constant.35.clone.sketch_high) | copy-start | bytes 786436
  11.7 3.5 %copy-start.4 = (bf16[256,512]{1,0:T(8,128)(2,1)S(1)}, bf16[256,512]{1,0:T(8,128)(2,1)}, u32[]{:S(2)}) copy-start(bf16[256,512]{1,0:T(8,128)(2,1)} %constant.34.clone.analysis_low) | copy-start | bytes 786436
  11.7 3.5 %copy-start.14 = (f32[16,256]{1,0:T(8,128)S(1)}, f32[16,256]{1,0:T(8,128)}, u32[]{:S(2)}) copy-start(f32[16,256]{1,0:T(8,128)} %constant.43.clone.weight_ref) | copy-start | bytes 49156
  15.2 10.3 %copy-start.12 = (bf16[48,1024]{1,0:T(8,128)(2,1)S(1)}, bf16[48,1024]{1,0:T(8,128)(2,1)}, u32[]{:S(2)}) copy-start(bf16[48,1024]{1,0:T(8,128)(2,1)} %constant.44.clone.table_ref) | copy-start | bytes 294916

commit v10 on v9

--- a/solution.py
+++ b/solution.py
@@ -474,28 +474,28 @@
                 us = []
                 for l2 in range(keep2):
                     start = (a * keep2 + l2) * rank + tile * 8
-                    us.append(
-                        (
-                            uhat[rows(start), lanes(0, piece)],
-                            uhat[rows(start), lanes(1, piece)],
-                        )
-                    )
+                    u_real = uhat[rows(start), lanes(0, piece)]
+                    u_imag = uhat[rows(start), lanes(1, piece)]
+                    us.append((u_real, u_real + u_imag, u_imag - u_real))
                 for k2 in range(span2):
                     d_real = dhat[rows(k2 * rank + tile * 8), pl.ds(piece * LANES, LANES)]
                     d_imag = dhat[
                         rows((span2 + k2) * rank + tile * 8), pl.ds(piece * LANES, LANES)
                     ]
+                    d_sum = d_real + d_imag
                     for l2 in range(keep2):
-                        u_real, u_imag = us[l2]
-                        real, imag = sums[l2 + k2]
+                        u_real, u_more, u_less = us[l2]
+                        common, less_real, more_imag = sums[l2 + k2]
                         sums[l2 + k2] = (
-                            real + (u_real * d_real - u_imag * d_imag),
-                            imag + (u_real * d_imag + u_imag * d_real),
+                            common + u_real * d_sum,
+                            less_real + u_more * d_imag,
+                            more_imag + u_less * d_real,
                         )
                 return tuple(sums)
 
             zero = jnp.zeros((8, LANES), jnp.float32)
-            sums = sweep(tiles, rebuild_tile, ((zero, zero),) * second)
+            sums = sweep(tiles, rebuild_tile, ((zero, zero, zero),) * second)
+            sums = [(common - less, common + more) for common, less, more in sums]
             for part in range(2):
                 summed = jnp.concatenate(
                     [jnp.sum(sums[g2][part], 0, keepdims=True) for g2 in range(second)], 0

time: 26.9 us -> 27 us (level)
  no operation moved by 1% of the time
where the time goes in v10:
time: 27 us; the launch traced here: 26.7 us
  starting transfers between devices  9.14 us (34%)
  Pallas kernels  7.42 us (27%)
  blocking collectives  7.01 us (26%)
  waiting for transfers between devices  2.88 us (11%)
    all_to_all x1, blocking collectives, per_device(): lax.all_to_all(rebuilt, 'wide', split_axis=0, concat_axis=0, axis_index_g...  7.01 us
    all_to_all x1, starting transfers between devices, per_device(): lax.all_to_all(blocks, ('wide', 'narrow'), split_axis=0, concat_axis=0, a...  6.08 us
    pallas_call x1, Pallas kernels, per_device(): pl.pallas_call(functools.partial(core_kernel, (first, second, rank), orde...  3.26 us
    ppermute x1, starting transfers between devices, per_device(): omegas.append(lax.ppermute(omega, 'narrow', ring))  3.06 us
    all_to_all x1, waiting for transfers between devices, per_device(): lax.all_to_all(blocks, ('wide', 'narrow'), split_axis=0, concat_axis=0, a...  2.87 us
    pallas_call x1, Pallas kernels, per_device(): pl.pallas_call(spectrum_kernel, out_shape=jax.ShapeDtypeStruct((dests, li...  2.45 us
    pallas_call x1, Pallas kernels, per_device(): pl.pallas_call(synthesis_kernel, out_shape=jax.ShapeDtypeStruct((CELLS, S...  1.24 us
  transfers between devices with their start and end apart: 2, of which 1 were waited for; matrix products, arithmetic and copies ran while one was open for 0% of the time, Pallas kernels for 2%

profile of v10, /device:TPU:0, one launch (start us, length us, event | category | flops | bytes accessed | tf_op | source)
XLA Modules:
  0.0 26.7 jit_solution(13706400090291192123)
XLA Ops:
  0.0 0.0 copy-start.7
  0.0 0.0 copy-start.8
  0.0 0.0 copy-start.9
  0.1 2.5 %spectrum.1 = f32[16,4,128]{2,1,0:T(4,128)} custom-call(f32[256,1024]{1,0:T(8,128)} %bitcast.3, s32[1,256]{1,0:T(1,128)} %bitcast.4, bf16[64,1024]{1,0:T(8,128)(2,1)} %constant.30.clone.table_ref), custom_call_target="tpu_custom_call" | custom-call | tf_op jit(solution)/shard_map/spectrum/pallas_call | solution.py:595
  2.5 0.0 copy-done.13
  2.5 3.1 %collective-permute-start = (f32[16,810]{1,0:T(8,128)S(1)}, f32[16,810]{1,0:T(8,128)S(1)}, u32[]{:S(2)}, u32[]{:S(2)}) collective-permute-start(f32[16,810]{1,0:T(8,128)S(1)} %copy-done.13), channel_id=1, source_target_pairs={{0,1},{1,0},{2,3},{3,2},{4,5},{5,4},{6,7},{7,6},{8,9},{9,8},{10,11... | collective-permute-start | bytes 155528 | tf_op jit(solution)/shard_map/ppermute | solution.py:612
  5.6 6.1 %all-to-all-start = ((f32[16,4,128]{2,1,0:T(4,128)}), f32[16,4,128]{2,1,0:T(4,128)S(1)}, u32[]{:S(2)}, u32[]{:S(2)}) async-start(f32[16,4,128]{2,1,0:T(4,128)} %spectrum.1), calls=%async_computation | async-start | bytes 65536 | tf_op jit(solution)/shard_map/all_to_all | solution.py:614
  11.7 0.0 copy-start.1
  11.7 0.0 copy-start.2
  11.7 0.0 copy-start.3
  11.7 0.0 copy-start.4
  11.7 0.0 copy-start.14
  11.7 0.0 collective-permute-done.refs_1_
  11.7 0.0 copy-done.10
  11.8 0.0 copy-done.11
  11.8 0.5 %omega.1.omega_ref = f32[320,768]{1,0:T(8,128)S(1)} custom-call(f32[16,810]{1,0:T(8,128)S(1)} %copy-done.13, f32[16,810]{1,0:T(8,128)S(1)} %collective-permute-done.refs_1_, bf16[128,512]{1,0:T(8,128)(2,1)S(1)} %copy-done.11, bf16[128,512]{1,0:T(8,128)(2,1)S(1)} %copy-done.10), custom_call_target="tpu_custom_call" | custom-call | flops 125829120 | bytes 655360 | tf_op jit(solution)/shard_map/omega/pallas_call | solution.py:626
  12.2 2.9 %all-to-all-done.x_ref = f32[16,4,128]{2,1,0:T(4,128)S(1)} async-done(((f32[16,4,128]{2,1,0:T(4,128)}), f32[16,4,128]{2,1,0:T(4,128)S(1)}, u32[]{:S(2)}, u32[]{:S(2)}) %all-to-all-start) | async-done | bytes 32800 | tf_op jit(solution)/shard_map/all_to_all | solution.py:614
  15.1 0.0 copy-done.5
  15.1 0.0 copy-done.6
  15.1 0.0 copy-done.7
  15.1 0.0 copy-done.8
  15.1 0.0 copy-done.9
  15.1 0.0 copy-done
  15.1 0.0 copy-done.1
  15.2 0.0 copy-done.2
  15.2 0.0 copy-done.3
  15.2 0.0 copy-done.4
  15.2 0.0 copy-done.14
  15.2 0.0 copy-start.12
  15.2 3.3 %core.1 = f32[8,4,128]{2,1,0:T(4,128)S(1)} custom-call(f32[16,4,128]{2,1,0:T(4,128)S(1)} %all-to-all-done.x_ref, f32[320,768]{1,0:T(8,128)S(1)} %omega.1.omega_ref, bf16[256,512]{1,0:T(8,128)(2,1)S(1)} %copy-done.5, bf16[256,512]{1,0:T(8,128)(2,1)S(1)} %copy-done.4, bf16[512,256]{1,0:T(8,128)(2,1)S(1)} %copy-done.3, bf16[512,256]{1,0:T(8,128)(2,1)S(1)} %copy-done.2, ...), custom_call_target="tpu_custom_call" | custom-call | tf_op jit(solution)/shard_map/core/pallas_call | solution.py:666
  18.5 7.0 %all_to_all.10.cells_ref = f32[8,4,128]{2,1,0:T(4,128)S(1)} all-to-all(f32[8,4,128]{2,1,0:T(4,128)S(1)} %core.1), channel_id=1, replica_groups={{10,8,6,4,2,0,14,12},{11,9,7,5,3,1,15,13},{26,24,22,20,18,16,30,28},{27..., dimensions={0} | all-to-all | bytes 32768 | tf_op jit(solution)/shard_map/all_to_all | solution.py:675
  25.5 1.2 %synthesis.1 = f32[256,1024]{1,0:T(8,128)} custom-call(f32[8,4,128]{2,1,0:T(4,128)S(1)} %all_to_all.10.cells_ref, bf16[48,1024]{1,0:T(8,128)(2,1)S(1)} %copy-done.12), custom_call_target="tpu_custom_call" | custom-call | tf_op jit(solution)/shard_map/synthesis/pallas_call | solution.py:685
  (7 shorter events, 0.0 us)
Async XLA Ops:
  0.0 2.5 %copy-start.13 = (f32[16,810]{1,0:T(8,128)S(1)}, f32[16,810]{1,0:T(8,128)}, u32[]{:S(2)}) copy-start(f32[16,810]{1,0:T(8,128)} %refs_0_) | copy-start | bytes 155524
  0.0 11.7 %copy-start.10 = (bf16[128,512]{1,0:T(8,128)(2,1)S(1)}, bf16[128,512]{1,0:T(8,128)(2,1)}, u32[]{:S(2)}) copy-start(bf16[128,512]{1,0:T(8,128)(2,1)} %constant.32.clone.refs_3_) | copy-start | bytes 393220
  0.0 11.8 %copy-start.11 = (bf16[128,512]{1,0:T(8,128)(2,1)S(1)}, bf16[128,512]{1,0:T(8,128)(2,1)}, u32[]{:S(2)}) copy-start(bf16[128,512]{1,0:T(8,128)(2,1)} %constant.31.clone.refs_2_) | copy-start | bytes 393220
  0.0 15.1 %copy-start.5 = (bf16[256,512]{1,0:T(8,128)(2,1)S(1)}, bf16[256,512]{1,0:T(8,128)(2,1)}, u32[]{:S(2)}) copy-start(bf16[256,512]{1,0:T(8,128)(2,1)} %constant.33.clone.analysis_high) | copy-start | bytes 786436
  0.0 15.1 %copy-start.6 = (bf16[256,256]{1,0:T(8,128)(2,1)S(1)}, bf16[256,256]{1,0:T(8,128)(2,1)}, u32[]{:S(2)}) copy-start(bf16[256,256]{1,0:T(8,128)(2,1)} %constant.40.clone.window_low) | copy-start | bytes 393220
  0.0 15.1 %copy-start.7 = (bf16[256,256]{1,0:T(8,128)(2,1)S(1)}, bf16[256,256]{1,0:T(8,128)(2,1)}, u32[]{:S(2)}) copy-start(bf16[256,256]{1,0:T(8,128)(2,1)} %constant.39.clone.window_high) | copy-start | bytes 393220
  0.0 15.1 %copy-start.8 = (bf16[128,512]{1,0:T(8,128)(2,1)S(1)}, bf16[128,512]{1,0:T(8,128)(2,1)}, u32[]{:S(2)}) copy-start(bf16[128,512]{1,0:T(8,128)(2,1)} %constant.38.clone.basis_low) | copy-start | bytes 393220
  0.0 15.1 %copy-start.9 = (bf16[128,512]{1,0:T(8,128)(2,1)S(1)}, bf16[128,512]{1,0:T(8,128)(2,1)}, u32[]{:S(2)}) copy-start(bf16[128,512]{1,0:T(8,128)(2,1)} %constant.37.clone.basis_high) | copy-start | bytes 393220
  2.5 9.2 %collective-permute-start = (f32[16,810]{1,0:T(8,128)S(1)}, f32[16,810]{1,0:T(8,128)S(1)}, u32[]{:S(2)}, u32[]{:S(2)}) collective-permute-start(f32[16,810]{1,0:T(8,128)S(1)} %copy-done.13), channel_id=1, source_target_pairs={{0,1},{1,0},{2,3},{3,2},{4,5},{5,4},{6,7},{7,6},{8,9},{9,8},{10,11... | collective-permute-start | bytes 155528 | tf_op jit(solution)/shard_map/ppermute | solution.py:612
  5.6 9.5 %all-to-all-start = ((f32[16,4,128]{2,1,0:T(4,128)}), f32[16,4,128]{2,1,0:T(4,128)S(1)}, u32[]{:S(2)}, u32[]{:S(2)}) async-start(f32[16,4,128]{2,1,0:T(4,128)} %spectrum.1), calls=%async_computation | async-start | bytes 65536 | tf_op jit(solution)/shard_map/all_to_all | solution.py:614
  11.7 3.5 %copy-start = (bf16[256,512]{1,0:T(8,128)(2,1)S(1)}, bf16[256,512]{1,0:T(8,128)(2,1)}, u32[]{:S(2)}) copy-start(bf16[256,512]{1,0:T(8,128)(2,1)} %constant.42.clone.back_low) | copy-start | bytes 786436
  11.7 3.5 %copy-start.1 = (bf16[256,512]{1,0:T(8,128)(2,1)S(1)}, bf16[256,512]{1,0:T(8,128)(2,1)}, u32[]{:S(2)}) copy-start(bf16[256,512]{1,0:T(8,128)(2,1)} %constant.41.clone.back_high) | copy-start | bytes 786436
  11.7 3.5 %copy-start.2 = (bf16[512,256]{1,0:T(8,128)(2,1)S(1)}, bf16[512,256]{1,0:T(8,128)(2,1)}, u32[]{:S(2)}) copy-start(bf16[512,256]{1,0:T(8,128)(2,1)} %constant.36.clone.sketch_low) | copy-start | bytes 786436
  11.7 3.5 %copy-start.3 = (bf16[512,256]{1,0:T(8,128)(2,1)S(1)}, bf16[512,256]{1,0:T(8,128)(2,1)}, u32[]{:S(2)}) copy-start(bf16[512,256]{1,0:T(8,128)(2,1)} %constant.35.clone.sketch_high) | copy-start | bytes 786436
  11.7 3.5 %copy-start.4 = (bf16[256,512]{1,0:T(8,128)(2,1)S(1)}, bf16[256,512]{1,0:T(8,128)(2,1)}, u32[]{:S(2)}) copy-start(bf16[256,512]{1,0:T(8,128)(2,1)} %constant.34.clone.analysis_low) | copy-start | bytes 786436
  11.7 3.5 %copy-start.14 = (f32[16,256]{1,0:T(8,128)S(1)}, f32[16,256]{1,0:T(8,128)}, u32[]{:S(2)}) copy-start(f32[16,256]{1,0:T(8,128)} %constant.43.clone.weight_ref) | copy-start | bytes 49156
  15.2 10.3 %copy-start.12 = (bf16[48,1024]{1,0:T(8,128)(2,1)S(1)}, bf16[48,1024]{1,0:T(8,128)(2,1)}, u32[]{:S(2)}) copy-start(bf16[48,1024]{1,0:T(8,128)(2,1)} %constant.44.clone.table_ref) | copy-start | bytes 294916
